TPU v7x, 128 devices: a whole 4x4x4 slice. The times are simulated.
128 devices in a mesh: dp: 2 (over x_lo), fsdp: 8 (over y, core), tp: 8 (over z, x_hi).
Axes of the slice: x: 4 (x_hi: 2, x_lo: 2; x = x_hi * 2 + x_lo), y: 4, z: 4, core: 2. Of those that a mesh axis runs over, the one named last changes fastest.
Arguments:
- ref_hidden: bfloat16 [2048, 4096], P(('dp', 'fsdp', 'tp')), may hold values from -18 to 18
- proxy_hidden: bfloat16 [2048, 1024], P(('dp', 'fsdp')), may hold values from -91 to 91
- targets: int32 [2048], P(('dp', 'fsdp')), may hold values from 0 to 65535
- languages: int32 [2048], P(('dp', 'fsdp')), may hold values from 0 to 63
- ref_gain: float32 [4096], replicated, may hold values from 0.25 to 1.75
- ref_head: bfloat16 [65536, 4096], P(('fsdp', 'tp')), may hold values from -16 to 16
- proxy_gain_in: float32 [1024], replicated, may hold values from 0.25 to 1.75
- proxy_gain_out: float32 [1024], replicated, may hold values from 0.25 to 1.75
- gate_weight: bfloat16 [1024, 4096], P('fsdp', 'tp'), may hold values from -0.1875 to 0.1875
- up_weight: bfloat16 [1024, 4096], P('fsdp', 'tp'), may hold values from -0.1875 to 0.1875
- down_weight: bfloat16 [4096, 1024], P('tp', 'fsdp'), may hold values from -0.09375 to 0.09375
- proxy_head: bfloat16 [65536, 1024], P(('fsdp', 'tp')), may hold values from -16 to 16
- domain_weights: float32 [64], replicated, may hold values from 0.7 to 1.4
Outputs:
- log_weights: float32 [64], replicated
- grad_gate: float32 [1024, 4096], P('fsdp', 'tp')
- grad_up: float32 [1024, 4096], P('fsdp', 'tp')
- grad_down: float32 [4096, 1024], P('tp', 'fsdp')
- grad_head: float32 [65536, 1024], P(('fsdp', 'tp'))
All inputs are finite; a program needn't handle non-finite values.
Results may differ from a plain program's by a relative error of at most 0.011.
Values may be sent and summed in bfloat16 or wider, within the bound.
A program may use at most 128 MiB of HBM per device.

v0:
```python
import jax
import jax.numpy as jnp
from jax import lax
from jax.sharding import PartitionSpec as P

EPSILON = 1e-05
STEP_SIZE = 1.0
SMOOTHING = 0.001


def in_one_piece(arrays, axis, dim, along):
    both = jnp.concatenate(arrays, axis=along)
    filled, at, finished = (lax.all_gather(both, axis, axis=dim, tiled=True), 0, [])
    for a in arrays:
        finished.append(lax.slice_in_dim(filled, at, at + a.shape[along], axis=along))
        at += a.shape[along]
    return tuple(finished)


def in_order(pieces, dim):
    pieces = jnp.moveaxis(pieces, 0, dim)
    shape = pieces.shape
    return pieces.reshape(*shape[:dim], shape[dim] * shape[dim + 1], *shape[dim + 2 :])


def from_everyone(array, axis):
    size = lax.axis_size(axis)
    return lax.all_to_all(
        jnp.broadcast_to(array[None], (size, *array.shape)), axis, 0, 0, tiled=True
    )


def gather_directly(array, axis, dim):
    return in_order(from_everyone(array, axis), dim)


def taken_together(array, axis):
    everything = from_everyone(array, axis)
    return jnp.sum(everything, axis=0)


def gather_turned(arrays, axis, dims):
    turned = [jnp.moveaxis(a, dim, 0) for a, dim in zip(arrays, dims)]
    both = jnp.concatenate([t.reshape(len(t), -1) for t in turned], axis=1)
    filled, at, finished = (lax.all_gather(both, axis, axis=0, tiled=True), 0, [])
    for t, dim in zip(turned, dims):
        section = filled[:, at : at + t[0].size].reshape(-1, *t.shape[1:])
        finished.append(jnp.moveaxis(section, 0, dim))
        at += t[0].size
    return tuple(finished)


def collected_together(array, axis):
    leaves = jax.tree.leaves(array)
    order = sorted(range(len(leaves)), key=lambda k: -leaves[k].size)
    width = (1, *leaves[order[0]].shape)[-1]
    lines = [
        jnp.pad(leaves[k].reshape(-1), (0, -leaves[k].size % width)).reshape(-1, width)
        for k in order
    ]
    both, at, found = (from_everyone(jnp.concatenate(lines), axis), 0, {})
    for k, line in zip(order, lines):
        section = both[:, at : at + len(line)].reshape(len(both), -1)
        found[k] = section[:, : leaves[k].size].reshape(-1, *leaves[k].shape)
        at += len(line)
    numbers = iter(range(len(leaves)))
    return jax.tree.map(lambda _: found[next(numbers)], array)


def joined_by_halves(pieces, combine):
    while len(jax.tree.leaves(pieces)[0]) > 1:
        pieces = jax.vmap(combine)(
            *(jax.tree.map(lambda part: part[side::2], pieces) for side in (0, 1))
        )
    return jax.tree.map(lambda part: part[0], pieces)


def combined_all(array, axis, combine):
    pieces = collected_together(array, axis)
    return joined_by_halves(pieces, combine)


def packed_total(arrays, axis):
    ends = [0]
    for a in arrays:
        ends.append(ends[-1] + a.size)
    so_far = taken_together(jnp.concatenate([a.ravel() for a in arrays]), axis)
    return tuple((so_far[b:e].reshape(a.shape) for a, b, e in zip(arrays, ends, ends[1:])))


def total_of_pieces(array, axis):
    pieces = lax.all_gather(array, axis)
    return pieces.sum(axis=0)


def in_blocks(array, dim, size):
    before, after = (array.shape[:dim], array.shape[dim + 1 :])
    return jnp.moveaxis(array.reshape(*before, size, -1, *after), dim, 0)


def summed_on_arrival(array, axis, dim):
    pieces = in_blocks(array, dim, lax.axis_size(axis))
    arrived = lax.all_to_all(pieces, axis, split_axis=0, concat_axis=0, tiled=True)
    return arrived.sum(axis=0)


def rms_scale(values, gain_vec):
    values = values.astype(jnp.float32)
    return (
        values * lax.rsqrt(jnp.mean(values * values, axis=-1, keepdims=True) + EPSILON) * gain_vec
    )


def row_logits(row_block, head):
    return lax.dot_general(
        row_block, head, (((1,), (1,)), ((), ())), preferred_element_type=jnp.float32
    )


def piece_stats(logits, part_targets, vocab_start):
    vocab_cols = vocab_start + jnp.arange(logits.shape[1], dtype=jnp.int32)
    high_val = jnp.max(logits, axis=1)
    exp_total = jnp.sum(jnp.exp(logits - high_val[:, None]), axis=1)
    picked = jnp.sum(jnp.where(vocab_cols[None, :] == part_targets[:, None], logits, 0.0), axis=1)
    return (high_val, exp_total, picked)


def join_stats(earlier, latter):
    high_val = jnp.maximum(earlier[0], latter[0])
    exp_total = earlier[1] * jnp.exp(earlier[0] - high_val) + latter[1] * jnp.exp(
        latter[0] - high_val
    )
    return (high_val, exp_total, earlier[2] + latter[2])


def join_both(earlier, latter):
    return join_stats(earlier[0:3], latter[0:3]) + join_stats(earlier[3:6], latter[3:6])


def norm_backward(mid_sum, gain_vec, d_out):
    inv_rms = lax.rsqrt(jnp.mean(mid_sum * mid_sum, axis=1, keepdims=True) + EPSILON)
    scaled_grad = d_out * gain_vec
    inner_mean = jnp.mean(mid_sum * scaled_grad, axis=1, keepdims=True)
    return (inv_rms * scaled_grad - mid_sum * inv_rms * inv_rms * inv_rms * inner_mean).astype(
        jnp.bfloat16
    )


def gate_grads(d_act, gate_pre, up_pre):
    sigmoid_g = jax.nn.sigmoid(gate_pre)
    d_gate = (d_act * up_pre * sigmoid_g * (1.0 + gate_pre * (1.0 - sigmoid_g))).astype(
        jnp.bfloat16
    )
    d_up = (d_act * gate_pre * sigmoid_g).astype(jnp.bfloat16)
    return (d_gate, d_up)


def domain_update(domain_weights, lang_excess, lang_count):
    excess = lang_excess / jnp.maximum(lang_count, 1.0)
    mixture = jax.nn.softmax(jnp.log(domain_weights) + STEP_SIZE * excess)
    return (1.0 - SMOOTHING) * mixture + SMOOTHING / domain_weights.shape[0]


def local(
    ref_hidden,
    proxy_hidden,
    targets,
    languages,
    ref_gain,
    ref_head,
    proxy_gain_in,
    proxy_gain_out,
    gate_weight,
    up_weight,
    down_weight,
    proxy_head,
    domain_weights,
):
    local_rows = proxy_hidden.shape[0]
    vocab_rows = ref_head.shape[0]
    vocab_start = lax.axis_index(("fsdp", "tp")) * vocab_rows
    group_rows = local_rows * lax.axis_size("fsdp")
    total_rows = group_rows * lax.axis_size("dp")
    width_part = gate_weight.shape[1]
    normed_in = rms_scale(proxy_hidden, proxy_gain_in).astype(jnp.bfloat16)
    pieces = in_one_piece((gate_weight, up_weight), "fsdp", 0, 1)
    columns = normed_in
    gate_pre = jnp.dot(columns, pieces[0], preferred_element_type=jnp.float32)
    up_pre = jnp.dot(columns, pieces[1], preferred_element_type=jnp.float32)
    hidden_act = (gate_pre * jax.nn.sigmoid(gate_pre) * up_pre).astype(jnp.bfloat16)
    ffn_part = jnp.dot(
        hidden_act, gather_directly(down_weight, "fsdp", 1), preferred_element_type=jnp.float32
    )
    mid_sum = proxy_hidden.astype(jnp.float32) + taken_together(ffn_part, "tp")
    final_normed = rms_scale(mid_sum, proxy_gain_out).astype(jnp.bfloat16)
    group_targets, group_langs = gather_turned((targets, languages), "fsdp", (0, 0))
    final_group = gather_directly(final_normed, "fsdp", 0)
    proxy_logits = row_logits(final_group, proxy_head)
    proxy_top, proxy_total, proxy_pick = piece_stats(proxy_logits, group_targets, vocab_start)
    ref_normed = rms_scale(ref_hidden, ref_gain).astype(jnp.bfloat16)
    ref_block = gather_directly(ref_normed, "tp", 0)
    logits = row_logits(lax.all_gather(ref_block, "fsdp", axis=0, tiled=True), ref_head)
    high_val, exp_total, picked = piece_stats(logits, group_targets, vocab_start)
    merged = combined_all(
        (high_val, exp_total, picked, proxy_top, proxy_total, proxy_pick), ("fsdp", "tp"), join_both
    )
    ref_lse = merged[0] + jnp.log(merged[1])
    ref_target = merged[2]
    proxy_lse = merged[3] + jnp.log(merged[4])
    proxy_target = merged[5]
    excess_tok = jnp.maximum(proxy_lse - proxy_target - (ref_lse - ref_target), 0.0)
    lang_ids = jnp.arange(domain_weights.shape[0], dtype=jnp.int32)
    member = (group_langs[:, None] == lang_ids[None, :]).astype(jnp.float32)
    lang_excess, lang_count = packed_total(
        (jnp.sum(member * excess_tok[:, None], axis=0), jnp.sum(member, axis=0)), "dp"
    )
    new_weights = domain_update(domain_weights, lang_excess, lang_count)
    token_weight = (
        jnp.sum(member * (new_weights / jnp.maximum(lang_count, 1.0))[None, :], axis=1) * total_rows
    )
    vocab_cols = vocab_start + jnp.arange(vocab_rows, dtype=jnp.int32)
    onehot = (vocab_cols[None, :] == group_targets[:, None]).astype(jnp.float32)
    dlogits = (
        token_weight[:, None] * (jnp.exp(proxy_logits - proxy_lse[:, None]) - onehot)
    ).astype(jnp.bfloat16)
    head_part = lax.dot_general(
        dlogits, final_group, (((0,), (0,)), ((), ())), preferred_element_type=jnp.float32
    )
    grad_head = total_of_pieces(head_part, "dp")
    d_share = summed_on_arrival(
        jnp.dot(dlogits, proxy_head, preferred_element_type=jnp.float32), "fsdp", 0
    )
    d_final = taken_together(d_share, "tp")
    d_mid = norm_backward(mid_sum, proxy_gain_out, d_final)
    columns = d_mid
    d_act = lax.dot_general(
        columns,
        gather_directly(down_weight, "fsdp", 1),
        (((1,), (1,)), ((), ())),
        preferred_element_type=jnp.float32,
    )
    d_gate, d_up = gate_grads(d_act, gate_pre, up_pre)
    d_both = jnp.concatenate([d_gate, d_up], axis=1)
    down_term = lax.dot_general(
        hidden_act, d_mid, (((0,), (0,)), ((), ())), preferred_element_type=jnp.float32
    )
    down_share = summed_on_arrival(down_term, "fsdp", 1)
    columns = normed_in
    both_share = summed_on_arrival(
        lax.dot_general(
            columns, d_both, (((0,), (0,)), ((), ())), preferred_element_type=jnp.float32
        ),
        "fsdp",
        0,
    )
    grad_gate, grad_up, grad_down = packed_total(
        (both_share[:, :width_part], both_share[:, width_part:], down_share), "dp"
    )
    return (jnp.log(new_weights), grad_gate, grad_up, grad_down, grad_head)


def solution(mesh):
    in_specs = (
        P(("dp", "fsdp", "tp"), None),
        P(("dp", "fsdp"), None),
        P(("dp", "fsdp")),
        P(("dp", "fsdp")),
        P(),
        P(("fsdp", "tp"), None),
        P(),
        P(),
        P("fsdp", "tp"),
        P("fsdp", "tp"),
        P("tp", "fsdp"),
        P(("fsdp", "tp"), None),
        P(),
    )
    out_specs = (P(), P("fsdp", "tp"), P("fsdp", "tp"), P("tp", "fsdp"), P(("fsdp", "tp"), None))
    return jax.shard_map(local, mesh=mesh, in_specs=in_specs, out_specs=out_specs, check_vma=False)
```

profile of v0, /device:TPU:1, one launch (start us, length us, event | category | flops | bytes accessed | tf_op | source)
XLA Modules:
  0.0 540.1 jit_solution(17066146113647526955)
XLA Ops:
  11.4 24.6 %all_to_all.58 = bf16[8,16,4096]{2,1,0:T(8,128)(2,1)} all-to-all(bf16[8,16,4096]{2,1,0:T(8,128)(2,1)S(1)} %broadcast_in_dim.21), channel_id=1, replica_groups=mesh['dp'=2,'fsdp'=8,'tp'=8] {'tp'}, dimensions={0} | all-to-all | bytes 2097152 | tf_op jit(solution)/shard_map/all_to_all | solution.py:28
  37.2 6.3 %all-to-all-start.1 = ((bf16[8,512,128]{1,2,0:T(8,128)(2,1)}), bf16[8,512,128]{1,2,0:T(8,128)(2,1)}, u32[]{:S(2)}, u32[]{:S(2)}) async-start(bf16[8,512,128]{1,2,0:T(8,128)(2,1)} %broadcast_in_dim.23), calls=%async_computation.1 | async-start | bytes 2097152 | tf_op jit(solution)/shard_map/all_to_all | solution.py:28
  48.2 13.0 %all-to-all-done.1 = bf16[8,512,128]{1,2,0:T(8,128)(2,1)} async-done(((bf16[8,512,128]{1,2,0:T(8,128)(2,1)}), bf16[8,512,128]{1,2,0:T(8,128)(2,1)}, u32[]{:S(2)}, u32[]{:S(2)}) %all-to-all-start.1) | async-done | bytes 1048608 | tf_op jit(solution)/shard_map/all_to_all | solution.py:28
  63.5 52.0 %all_to_all.59 = f32[8,128,1024]{2,1,0:T(8,128)} all-to-all(f32[8,128,1024]{2,1,0:T(8,128)S(1)} %broadcast_in_dim.24), channel_id=1, replica_groups=mesh['dp'=2,'fsdp'=8,'tp'=8] {'tp'}, dimensions={0} | all-to-all | bytes 8388608 | tf_op jit(solution)/shard_map/all_to_all | solution.py:28
  120.0 7.4 %all-to-all-start.3 = ((bf16[8,128,1024]{2,1,0:T(8,128)(2,1)}), bf16[8,128,1024]{2,1,0:T(8,128)(2,1)}, u32[]{:S(2)}, u32[]{:S(2)}) async-start(bf16[8,128,1024]{2,1,0:T(8,128)(2,1)} %broadcast_in_dim.25), calls=%async_computation.3 | async-start | bytes 4194304 | tf_op jit(solution)/shard_map/all_to_all | solution.py:28
  127.5 30.0 %all_gather.15 = s32[1024,2]{0,1:T(2,128)S(1)} all-gather(s32[128,2]{0,1:T(2,128)S(1)} %pad_add_fusion), channel_id=1, replica_groups=mesh['dp'=2,'fsdp'=8,'tp'=8] {'fsdp'}, dimensions={0}, use_global_device_ids=true | all-gather | bytes 9216 | tf_op jit(solution)/shard_map/all_gather | solution.py:45
  157.5 6.0 %fusion.38 = (f32[1024]{0:T(1024)S(1)}, f32[1024,1024]{0,1:T(8,128)}) fusion(bf16[1024,1024]{1,0:T(8,128)(2,1)} %bitcast.10, bf16[1024,1024]{1,0:T(8,128)(2,1)S(1)} %copy-done), kind=kOutput, calls=%fused_computation.100 | convolution fusion | flops 2148531200 | bytes 8392704 | tf_op jit(solution)/shard_map/dot_general | solution.py:115
  163.5 13.1 %fusion.37 = (f32[1024]{0:T(1024)S(1)}, f32[1024,1024]{0,1:T(8,128)S(1)}) fusion(bf16[1024,4096]{1,0:T(8,128)(2,1)} %all-gather.5.cloned.1.call-done, bf16[1024,4096]{1,0:T(8,128)(2,1)} %param.18), kind=kOutput, calls=%fused_computation.99 | convolution fusion | flops 8590982144 | bytes 20975616 | tf_op jit(solution)/shard_map/dot_general | solution.py:115
  179.2 34.4 %all_to_all.60 = f32[64,6,1024]{2,1,0:T(8,128)S(1)} all-to-all(f32[64,6,1024]{2,1,0:T(8,128)S(1)} %broadcast_in_dim.26), channel_id=1, replica_groups=mesh['dp'=2,'fsdp'=8,'tp'=8] {'fsdp','tp'}, dimensions={0} | all-to-all | bytes 3145728 | tf_op jit(solution)/shard_map/all_to_all | solution.py:28
  254.7 4.9 all_to_all.61
  263.7 4.9 fusion.32
  268.6 53.0 %all_to_all.62 = f32[8,128,1024]{2,1,0:T(8,128)} all-to-all(f32[8,128,1024]{2,1,0:T(8,128)S(1)} %bitcast.66), channel_id=1, replica_groups=mesh['dp'=2,'fsdp'=8,'tp'=8] {'fsdp'}, dimensions={0} | all-to-all | bytes 8388608 | tf_op jit(solution)/shard_map/all_to_all | solution.py:103
  324.8 53.2 %all_to_all.63 = f32[8,128,1024]{2,1,0:T(8,128)} all-to-all(f32[8,128,1024]{2,1,0:T(8,128)S(1)} %broadcast_in_dim.28), channel_id=1, replica_groups=mesh['dp'=2,'fsdp'=8,'tp'=8] {'tp'}, dimensions={0} | all-to-all | bytes 8388608 | tf_op jit(solution)/shard_map/all_to_all | solution.py:28
  378.0 2.6 reduce_sum.198
  383.0 5.4 %all-to-all-start.9 = ((f32[8,512,128]{2,1,0:T(8,128)}), f32[8,512,128]{2,1,0:T(8,128)S(1)}, u32[]{:S(2)}, u32[]{:S(2)}) async-start(f32[8,512,128]{2,1,0:T(8,128)} %bitcast.65), calls=%async_computation.9 | async-start | bytes 4194304 | tf_op jit(solution)/shard_map/all_to_all | solution.py:103
  388.4 7.3 %fusion.30 = f32[1024,1024]{1,0:T(8,128)} fusion(bf16[1024,1024]{1,0:T(8,128)(2,1)} %bitcast.10, f32[1024,1024]{0,1:T(8,128)} %get-tuple-element.57, f32[1024]{0:T(1024)S(1)} %bitcast.84, f32[1024]{0:T(1024)S(1)} %broadcast_multiply_fusion, s32[1024]{0:T(1024)S(1)} %bitcast.81, s32[1024]{0:T(1024)S(1)} %copy-done.9), kind=kOutput, calls=%fused_computation.94 | convolution fusion | flops 2153775104 | bytes 10502144 | tf_op jit(solution)/shard_map/dot_general | solution.py:226
  398.3 2.8 fusion.15
  401.1 13.5 %all-to-all-done.9 = f32[8,512,128]{2,1,0:T(8,128)S(1)} async-done(((f32[8,512,128]{2,1,0:T(8,128)}), f32[8,512,128]{2,1,0:T(8,128)S(1)}, u32[]{:S(2)}, u32[]{:S(2)}) %all-to-all-start.9) | async-done | bytes 2097184 | tf_op jit(solution)/shard_map/all_to_all | solution.py:103
  414.6 5.4 %all-to-all-start.8 = ((f32[8,128,1024]{2,1,0:T(8,128)}), f32[8,128,1024]{2,1,0:T(8,128)}, u32[]{:S(2)}, u32[]{:S(2)}) async-start(f32[8,128,1024]{2,1,0:T(8,128)} %bitcast.63), calls=%async_computation.8 | async-start | bytes 8388608 | tf_op jit(solution)/shard_map/all_to_all | solution.py:103
  420.2 48.7 %all-to-all-done.8 = f32[8,128,1024]{2,1,0:T(8,128)} async-done(((f32[8,128,1024]{2,1,0:T(8,128)}), f32[8,128,1024]{2,1,0:T(8,128)}, u32[]{:S(2)}, u32[]{:S(2)}) %all-to-all-start.8) | async-done | bytes 4194336 | tf_op jit(solution)/shard_map/all_to_all | solution.py:103
  473.9 4.6 all-to-all-start.10
  479.1 37.0 %all-gather.9.cloned.1.call-done = f32[2048,1024]{1,0:T(8,128)} async-done(((f32[1024,1024]{1,0:T(8,128)}), f32[2048,1024]{1,0:T(8,128)}) %all-gather.9.cloned.1.call-update) | async-done | bytes 8388624 | tf_op jit(solution)/shard_map/all_gather | solution.py:92
  516.1 6.9 %reduce_sum.203 = f32[1024,1024]{1,0:T(8,128)} reduce(f32[2,1024,1024]{2,1,0:T(8,128)} %bitcast.64, f32[]{:T(128)} %constant.13.clone.1), dimensions={0}, to_apply=%region_22.23 | reduce | flops 1048576 | bytes 12582916 | tf_op jit(solution)/shard_map/reduce_sum | solution.py:93
  522.9 8.4 %reduce_sum.202 = f32[196608]{0:T(1024)S(1)} reduce(f32[2,1,196608]{2,1,0:T(1,128)} %all-to-all-done.10, f32[]{:T(128)} %constant.13.clone.1), dimensions={0,1}, to_apply=%region_21.22 | reduce | flops 196608 | bytes 2359300 | tf_op jit(solution)/shard_map/reduce_sum | solution.py:39
  (194 shorter events, 80.3 us)
Async XLA Ops:
  7.2 150.3 %copy-start = (bf16[1024,1024]{1,0:T(8,128)(2,1)S(1)}, bf16[1024,1024]{1,0:T(8,128)(2,1)}, u32[]{:S(2)}) copy-start(bf16[1024,1024]{1,0:T(8,128)(2,1)} %param.24) | copy-start | bytes 6291460
  7.2 28.8 %copy-start.6 = (bf16[512,128]{1,0:T(8,128)(2,1)S(1)}, bf16[512,128]{1,0:T(8,128)(2,1)}, u32[]{:S(2)}) copy-start(bf16[512,128]{1,0:T(8,128)(2,1)} %param.23) | copy-start | bytes 393220
  7.2 36.4 %all-gather.7.cloned.1.call-start = ((), (), s32[]{:S(2)}) async-start(), calls=%async_computation.12 | async-start | bytes 2359296 | tf_op jit(solution)/shard_map/all_gather | solution.py:13
  9.1 34.3 %copy-start.2 = (bf16[128,1024]{1,0:T(8,128)(2,1)S(1)}, bf16[128,1024]{1,0:T(8,128)(2,1)}, u32[]{:S(2)}) copy-start(bf16[128,1024]{1,0:T(8,128)(2,1)} %param.14) | copy-start | bytes 786436
  9.1 154.4 %all-gather.5.cloned.1.call-start = ((), (), s32[]{:S(2)}) async-start(), calls=%async_computation.11 | async-start | bytes 9437184 | tf_op jit(solution)/shard_map/all_gather | solution.py:202
  10.3 33.4 %copy-start.12 = (f32[1024]{0:T(1024)S(1)}, f32[1024]{0:T(1024)}, u32[]{:S(2)}) copy-start(f32[1024]{0:T(1024)} %param.19) | copy-start | bytes 12292
  37.2 24.0 %all-to-all-start.1 = ((bf16[8,512,128]{1,2,0:T(8,128)(2,1)}), bf16[8,512,128]{1,2,0:T(8,128)(2,1)}, u32[]{:S(2)}, u32[]{:S(2)}) async-start(bf16[8,512,128]{1,2,0:T(8,128)(2,1)} %broadcast_in_dim.23), calls=%async_computation.1 | async-start | bytes 2097152 | tf_op jit(solution)/shard_map/all_to_all | solution.py:28
  43.6 19.9 %copy-start.16 = (f32[128]{0:T(128)}, f32[128]{0:T(128)S(1)}, u32[]{:S(2)}) copy-start(f32[128]{0:T(128)S(1)} %add_rsqrt_fusion.1) | copy-start | bytes 1540
  48.2 15.3 %copy-start.4 = (bf16[128,512]{1,0:T(8,128)(2,1)}, bf16[128,512]{1,0:T(8,128)(2,1)S(1)}, u32[]{:S(2)}) copy-start(bf16[128,512]{1,0:T(8,128)(2,1)S(1)} %get-tuple-element.54) | copy-start | bytes 393220
  118.1 9.3 %copy-start.18 = (s32[128]{0:T(128)S(1)}, s32[128]{0:T(128)}, u32[]{:S(2)}) copy-start(s32[128]{0:T(128)} %param.16) | copy-start | bytes 1540
  118.1 9.3 %copy-start.19 = (s32[128]{0:T(128)S(1)}, s32[128]{0:T(128)}, u32[]{:S(2)}) copy-start(s32[128]{0:T(128)} %param.15) | copy-start | bytes 1540
  118.3 9.2 %copy-start.14 = (f32[128]{0:T(128)}, f32[128]{0:T(128)S(1)}, u32[]{:S(2)}) copy-start(f32[128]{0:T(128)S(1)} %add_rsqrt_fusion) | copy-start | bytes 1540
  120.0 37.5 %all-to-all-start.3 = ((bf16[8,128,1024]{2,1,0:T(8,128)(2,1)}), bf16[8,128,1024]{2,1,0:T(8,128)(2,1)}, u32[]{:S(2)}, u32[]{:S(2)}) async-start(bf16[8,128,1024]{2,1,0:T(8,128)(2,1)} %broadcast_in_dim.25), calls=%async_computation.3 | async-start | bytes 4194304 | tf_op jit(solution)/shard_map/all_to_all | solution.py:28
  157.5 19.1 %copy-start.8 = (s32[1024]{0:T(1024)}, s32[1024]{0:T(1024)S(1)}, u32[]{:S(2)}) copy-start(s32[1024]{0:T(1024)S(1)} %iota_add_fusion) | copy-start | bytes 12292
  157.5 19.1 %copy-start.10 = (s32[1024,1]{0,1:T(1,128)}, s32[1024,1]{0,1:T(1,128)S(1)}, u32[]{:S(2)}) copy-start(s32[1024,1]{0,1:T(1,128)S(1)} %get-tuple-element.51) | copy-start | bytes 12292
  163.5 13.1 %copy-start.3 = (f32[1024,1024]{0,1:T(8,128)S(1)}, f32[1024,1024]{0,1:T(8,128)}, u32[]{:S(2)}) copy-start(f32[1024,1024]{0,1:T(8,128)} %get-tuple-element.57) | copy-start | bytes 12582916
  378.0 3.0 copy-start.5
  381.5 6.9 %copy-start.9 = (s32[1024]{0:T(1024)S(1)}, s32[1024]{0:T(1024)}, u32[]{:S(2)}) copy-start(s32[1024]{0:T(1024)} %copy-done.8) | copy-start | bytes 12292
  381.5 6.9 %copy-start.11 = (s32[1024,1]{0,1:T(1,128)S(1)}, s32[1024,1]{0,1:T(1,128)}, u32[]{:S(2)}) copy-start(s32[1024,1]{0,1:T(1,128)} %copy-done.10) | copy-start | bytes 12292
  383.0 31.6 %all-to-all-start.9 = ((f32[8,512,128]{2,1,0:T(8,128)}), f32[8,512,128]{2,1,0:T(8,128)S(1)}, u32[]{:S(2)}, u32[]{:S(2)}) async-start(f32[8,512,128]{2,1,0:T(8,128)} %bitcast.65), calls=%async_computation.9 | async-start | bytes 4194304 | tf_op jit(solution)/shard_map/all_to_all | solution.py:103
  388.4 127.7 %all-gather.9.cloned.1.call-start = ((), (), s32[]{:S(2)}) async-start(), calls=%async_computation.13 | async-start | bytes 12582912 | tf_op jit(solution)/shard_map/all_gather | solution.py:92
  414.6 54.2 %all-to-all-start.8 = ((f32[8,128,1024]{2,1,0:T(8,128)}), f32[8,128,1024]{2,1,0:T(8,128)}, u32[]{:S(2)}, u32[]{:S(2)}) async-start(f32[8,128,1024]{2,1,0:T(8,128)} %bitcast.63), calls=%async_computation.8 | async-start | bytes 8388608 | tf_op jit(solution)/shard_map/all_to_all | solution.py:103
  473.9 49.0 %all-to-all-start.10 = ((f32[2,1,196608]{2,1,0:T(1,128)}), f32[2,1,196608]{2,1,0:T(1,128)}, u32[]{:S(2)}, u32[]{:S(2)}) async-start(f32[2,1,196608]{2,1,0:T(1,128)} %broadcast_in_dim.29), calls=%async_computation.10 | async-start | bytes 3145728 | tf_op jit(solution)/shard_map/all_to_all | solution.py:28
  516.1 17.5 %copy-start.1 = (bf16[1024,1024]{1,0:T(8,128)(2,1)S(1)}, bf16[1024,1024]{1,0:T(8,128)(2,1)}, u32[]{:S(2)}) copy-start(bf16[1024,1024]{1,0:T(8,128)(2,1)} %param.24) | copy-start | bytes 6291460
  (6 other events, 12.5 us)
Sparse Core Ops, SparseCore 0:
  10.3 28.8 all-gather.6
  40.9 53.5 all-gather.4
  395.8 120.2 all-gather.8
where the time goes:
time: 542 us; the launch traced here: 540 us
  blocking collectives  252 us (46%)
  waiting for transfers between devices  112 us (21%)
  other arithmetic  45.3 us (8%)
  local copies, waits for them, and re-layouts  45 us (8%)
  matrix products  41.7 us (8%)
  starting transfers between devices  29.3 us (5%)
  between operations  14.4 us (3%)
    all_to_all x5, blocking collectives, from_everyone(): lax.all_to_all(jnp.broadcast_to(array[None], (size, *array.shape)), axis,...  169 us
    all_to_all x2, waiting for transfers between devices, summed_on_arrival(): lax.all_to_all(pieces, axis, split_axis=0, concat_axis=0, tiled=True)  62.2 us
    all_to_all x1, blocking collectives, summed_on_arrival(): lax.all_to_all(pieces, axis, split_axis=0, concat_axis=0, tiled=True)  53 us
    all_gather x1, waiting for transfers between devices, total_of_pieces(): pieces = lax.all_gather(array, axis)  37 us
    all_gather x1, blocking collectives, gather_turned(): lax.all_gather(both, axis, axis=0, tiled=True)  30 us
    slice x60, local copies, waits for them, and re-layouts, joined_by_halves(): part[side::2]  27 us
    dot_general x2, matrix products, row_logits(): lax.dot_general(row_block, head, (((1,), (1,)), ((), ())), preferred_elem...  19.1 us
    all_to_all x3, starting transfers between devices, from_everyone(): lax.all_to_all(jnp.broadcast_to(array[None], (size, *array.shape)), axis,...  18.4 us
  transfers between devices with their start and end apart: 8, of which 4 were waited for; matrix products, arithmetic and copies ran while one was open for 8% of the time, Pallas kernels for 0%

commit v1 on v0

v1 whole, which is shorter than its diff:
```python
import functools

import jax
import jax.numpy as jnp
from jax import lax
from jax.experimental import pallas as pl
from jax.experimental.pallas import tpu as pltpu
from jax.sharding import PartitionSpec as P

EPSILON = 1e-05
STEP_SIZE = 1.0
SMOOTHING = 0.001
LANGS = 64
MESH = pl.DeviceIdType.MESH
F32, BF16 = jnp.float32, jnp.bfloat16


class Place:
    def __init__(self):
        self.dp = lax.axis_index("dp")
        f, t = lax.axis_index("fsdp"), lax.axis_index("tp")
        self.f, self.t = f, t
        self.y, self.c = lax.div(f, 2), lax.rem(f, 2)
        self.z, self.xh = lax.div(t, 2), lax.rem(t, 2)
        self.p = self.xh
        c = self.c
        self.a = (1 - c) * self.y + c * self.z
        self.b = (1 - c) * self.z + c * self.y

    def at(self, dp=None, y=None, z=None, xh=None, c=None):
        pick = lambda new, old: old if new is None else new
        dp, y, z = pick(dp, self.dp), pick(y, self.y), pick(z, self.z)
        xh, c = pick(xh, self.xh), pick(c, self.c)
        return {"dp": dp, "fsdp": y * 2 + c, "tp": z * 2 + xh}

    def on_a(self, a):
        c = self.c
        return self.at(y=(1 - c) * a + c * self.y, z=(1 - c) * self.z + c * a)

    def on_b(self, b):
        c = self.c
        return self.at(y=(1 - c) * self.y + c * b, z=(1 - c) * b + c * self.z)

    def core(self):
        return self.at(c=1 - self.c)

    def partner(self):
        return self.at(dp=1 - self.dp, xh=1 - self.xh)

    def neighbour(self):
        return self.at(dp=1 - self.dp)

    def opposite(self):
        return self.at(xh=1 - self.xh)


class Copies:
    def __init__(self, send, recv):
        self.send, self.recv, self.n, self.all = send, recv, 0, []

    def start(self, src, dst, to):
        copy = pltpu.make_async_remote_copy(
            src_ref=src,
            dst_ref=dst,
            send_sem=self.send.at[self.n],
            recv_sem=self.recv.at[self.n],
            device_id=to,
            device_id_type=MESH,
        )
        copy.start()
        self.n += 1
        self.all.append(copy)
        return copy

    def drain(self):
        for copy in self.all:
            copy.wait_send()


def greet(peers):
    barrier = pltpu.get_barrier_semaphore()
    for peer in peers:
        pl.semaphore_signal(barrier, inc=1, device_id=peer, device_id_type=MESH)
    pl.semaphore_wait(barrier, len(peers))


def ring(i, k):
    return lax.rem(i + k, 4)


def gather_body(wide, weights, *refs):
    n = len(wide)
    m = 2 if weights else 0
    ins, w_ins = refs[:n], refs[n : n + m]
    outs, w_outs = refs[n + m : 2 * n + m], refs[2 * n + m : 2 * n + 2 * m]
    send, recv, local = refs[2 * n + 2 * m :]
    me = Place()
    a, b, c, p = me.a, me.b, me.c, me.p
    go = Copies(send, recv)
    right_a, left_a = me.on_a(ring(a, 1)), me.on_a(ring(a, 3))
    right_b, left_b = me.on_b(ring(b, 1)), me.on_b(ring(b, 3))
    peers = [me.core(), me.partner(), right_a, left_a, right_b, left_b]
    if any(wide):
        peers += [me.neighbour(), me.opposite()]
    if weights:
        others = [lax.rem(me.f + j, 8) for j in range(1, 8)]
        kept = {"dp": me.dp, "tp": me.t}
        peers = peers[1:] + [{**kept, "fsdp": o} for o in others]
    greet(peers)

    def block(i, g, *at):
        return outs[i].at[(g, *at)] if wide[i] else outs[i].at[at]

    sides = [range(2) if w else range(1) for w in wide]
    locals_, first = [], []
    for i in range(n):
        mine = pltpu.make_async_copy(ins[i], block(i, 0, c, b, a, p), local.at[i])
        mine.start()
        locals_.append(mine)
        first.append(go.start(ins[i], block(i, 0, c, b, a, p), me.partner()))
        if wide[i]:
            first.append(go.start(ins[i], block(i, 1, c, b, a, p), me.neighbour()))
            first.append(go.start(ins[i], block(i, 1, c, b, a, p), me.opposite()))
    w_copies = []
    for k in range(m):
        mine = pltpu.make_async_copy(w_ins[k].at[me.f], w_outs[k].at[me.f], local.at[n + k])
        mine.start()
        locals_.append(mine)
        for o in others if weights else ():
            w_copies.append(go.start(w_ins[k].at[o], w_outs[k].at[me.f], {**kept, "fsdp": o}))
    for copy in first:
        copy.wait_recv()
    for copy in locals_:
        copy.wait()
    steps = [(i, g) for i in range(n) for g in sides[i]]
    near = []
    for i, g in steps:
        unit = block(i, g, c, b, a)
        near.append((go.start(unit, unit, right_a), go.start(unit, unit, left_a)))
    last = []
    for (i, g), (to_right, to_left) in zip(steps, near):
        to_right.wait_recv()
        half = block(i, g, c, b, ring(a, 3), 0)
        last.append(go.start(half, half, right_a))
        to_left.wait_recv()
        half = block(i, g, c, b, ring(a, 1), 1)
        last.append(go.start(half, half, left_a))
    for copy in last:
        copy.wait_recv()
    near, across = [], []
    for i, g in steps:
        unit = block(i, g, c, b)
        near.append((go.start(unit, unit, right_b), go.start(unit, unit, left_b)))
        across.append(go.start(unit, unit, me.core()))
    last = []
    for (i, g), (to_right, to_left) in zip(steps, near):
        to_right.wait_recv()
        half = block(i, g, c, ring(b, 3), pl.ds(0, 2))
        last.append(go.start(half, half, right_b))
        to_left.wait_recv()
        half = block(i, g, c, ring(b, 1), pl.ds(2, 2))
        last.append(go.start(half, half, left_b))
        for k in (3, 1):
            unit = block(i, g, c, ring(b, k))
            across.append(go.start(unit, unit, me.core()))
    for copy in last:
        copy.wait_recv()
    for i, g in steps:
        unit = block(i, g, c, ring(b, 2))
        across.append(go.start(unit, unit, me.core()))
    for copy in across + w_copies:
        copy.wait_recv()
    go.drain()


def gather(blocks, wide, weights, collective_id):
    n, m = len(blocks), len(weights)
    shapes = [
        jax.ShapeDtypeStruct(((2,) if w else ()) + (2, 4, 4, 2) + x.shape, x.dtype)
        for x, w in zip(blocks, wide)
    ] + [jax.ShapeDtypeStruct(w.shape, w.dtype) for w in weights]
    count = sum(27 if w else 13 for w in wide) + 7 * m
    vmem = pl.BlockSpec(memory_space=pltpu.VMEM)
    hbm = pl.BlockSpec(memory_space=pl.ANY)
    return pl.pallas_call(
        functools.partial(gather_body, tuple(wide), bool(weights)),
        out_shape=shapes,
        in_specs=[vmem] * (n + m),
        out_specs=[hbm] * (n + m),
        scratch_shapes=[
            pltpu.SemaphoreType.DMA((count,)),
            pltpu.SemaphoreType.DMA((count,)),
            pltpu.SemaphoreType.DMA((n + m,)),
        ],
        compiler_params=pltpu.CompilerParams(
            collective_id=collective_id, has_side_effects=True
        ),
        name="gather%d" % collective_id,
    )(*blocks, *weights)


def scatter_body(x, out, r0, acc, hr, hl, ur, ul, acc1, ra, acc2, give, rp, send, recv):
    me = Place()
    a, b, c, p = me.a, me.b, me.c, me.p
    go = Copies(send, recv)
    right_a, left_a, far_a = (me.on_a(ring(a, k)) for k in (1, 3, 2))
    right_b, left_b = me.on_b(ring(b, 1)), me.on_b(ring(b, 3))
    greet([me.core(), me.partner(), right_a, left_a, far_a, right_b, left_b])
    halves = x.shape[2] // 2
    lo, hi = pl.ds(0, halves), pl.ds(halves, halves)
    order = (2, 1, 3, 0)
    got = []
    for k in order:
        j = ring(a, k)
        got.append(go.start(x.at[1 - c, j], r0.at[j], me.core()))

    def join(k):
        j = ring(b, order[k])
        got[k].wait_recv()
        acc[j] = (x[c, j].astype(F32) + r0[j].astype(F32)).astype(BF16)
        return j

    far = join(0)
    s_r = go.start(acc.at[far, lo], hr, right_b)
    s_l = go.start(acc.at[far, hi], hl, left_b)
    near_r = join(1)
    t_r = go.start(acc.at[near_r, hi], ul.at[hi], right_b)
    near_l = join(2)
    t_l = go.start(acc.at[near_l, lo], ur.at[lo], left_b)
    s_r.wait_recv()
    acc[near_r, lo] = (acc[near_r, lo].astype(F32) + hr[...].astype(F32)).astype(BF16)
    v_r = go.start(acc.at[near_r, lo], ul.at[lo], right_b)
    s_l.wait_recv()
    acc[near_l, hi] = (acc[near_l, hi].astype(F32) + hl[...].astype(F32)).astype(BF16)
    v_l = go.start(acc.at[near_l, hi], ur.at[hi], left_b)
    own = join(3)
    for copy in (t_r, t_l, v_r, v_l):
        copy.wait_recv()
    total = acc[own].astype(F32) + ul[...].astype(F32) + ur[...].astype(F32)
    acc1[...] = total.astype(BF16).reshape(acc1.shape)
    sends = [
        go.start(acc1.at[ring(a, k)], ra.at[i], to)
        for i, (k, to) in enumerate(((2, far_a), (1, right_a), (3, left_a)))
    ]
    for copy in sends:
        copy.wait_recv()
    total = acc1[a].astype(F32)
    for i in range(3):
        total = total + ra[i].astype(F32)
    acc2[...] = total.reshape(acc2.shape)
    give[...] = acc2[1 - p].astype(BF16)
    swap = go.start(give, rp, me.partner())
    swap.wait_recv()
    out[...] = acc2[p] + rp[...].astype(F32)
    go.drain()


def scatter(x, collective_id):
    rows, width = x.shape
    unit = rows // 8
    block = rows // 64
    x = x.reshape(2, 4, unit, width)
    vmem = pl.BlockSpec(memory_space=pltpu.VMEM)
    return pl.pallas_call(
        scatter_body,
        out_shape=jax.ShapeDtypeStruct((block, width), F32),
        in_specs=[vmem],
        out_specs=vmem,
        scratch_shapes=[
            pltpu.VMEM((4, unit, width), BF16),
            pltpu.VMEM((4, unit, width), BF16),
            pltpu.VMEM((unit // 2, width), BF16),
            pltpu.VMEM((unit // 2, width), BF16),
            pltpu.VMEM((unit, width), BF16),
            pltpu.VMEM((unit, width), BF16),
            pltpu.VMEM((4, unit // 4, width), BF16),
            pltpu.VMEM((3, unit // 4, width), BF16),
            pltpu.VMEM((2, block, width), F32),
            pltpu.VMEM((block, width), BF16),
            pltpu.VMEM((block, width), BF16),
            pltpu.SemaphoreType.DMA((14,)),
            pltpu.SemaphoreType.DMA((14,)),
        ],
        compiler_params=pltpu.CompilerParams(
            collective_id=collective_id, has_side_effects=True
        ),
        name="scatter%d" % collective_id,
    )(x)


def join_all(pieces):
    out = []
    for base in (0, 24):
        high = functools.reduce(jnp.maximum, [s[base : base + 8] for s in pieces])
        total = pick = None
        for s in pieces:
            t = s[base + 8 : base + 16] * jnp.exp(s[base : base + 8] - high)
            k = s[base + 16 : base + 24]
            total, pick = (t, k) if total is None else (total + t, pick + k)
        out += [high, total, pick]
    return jnp.concatenate(out, axis=0)


def stats_body(st, lang, dw, lse, tw, logw, slot_c, slot_z, slot_y, slot_p, pack, other, send, recv):
    me = Place()
    go = Copies(send, recv)
    on_z = [me.at(z=ring(me.z, k)) for k in (1, 2, 3)]
    on_y = [me.at(y=ring(me.y, k)) for k in (1, 2, 3)]
    greet([me.core(), me.partner(), me.neighbour(), *on_z, *on_y])
    mine = st[...]
    for slots, at, peers in (
        (slot_c, me.c, [me.core()]),
        (slot_z, me.z, on_z),
        (slot_y, me.y, on_y),
        (slot_p, me.p, [me.partner()]),
    ):
        slots[at] = mine
        sent = [go.start(slots.at[at], slots.at[at], to) for to in peers]
        for copy in sent:
            copy.wait_recv()
        mine = join_all([slots[j] for j in range(slots.shape[0])])
    ref_loss = mine[0:8] + jnp.log(mine[8:16]) - mine[16:24]
    proxy_lse = mine[24:32] + jnp.log(mine[32:40])
    excess = jnp.maximum(proxy_lse - mine[40:48] - ref_loss, 0.0)
    own_lang = lang[0:8]
    for l in range(LANGS):
        here = own_lang == l
        pack[l : l + 1] = jnp.sum(jnp.where(here, excess, 0.0), axis=0, keepdims=True)
        pack[LANGS + l : LANGS + l + 1] = jnp.sum(
            jnp.where(here, 1.0, 0.0), axis=0, keepdims=True
        )
    pack[2 * LANGS : 2 * LANGS + 8] = proxy_lse
    swap = go.start(pack, other, me.neighbour())
    swap.wait_recv()
    lse[0:8] = proxy_lse
    lse[8:16] = other[2 * LANGS : 2 * LANGS + 8]
    sums = jnp.sum(pack[0 : 2 * LANGS] + other[0 : 2 * LANGS], axis=1, keepdims=True)
    sums = jnp.broadcast_to(sums, (2 * LANGS, 128))
    count = jnp.maximum(sums[LANGS:], 1.0)
    score = jnp.log(dw[...]) + STEP_SIZE * (sums[:LANGS] / count)
    score = jnp.exp(score - jnp.max(score, axis=0, keepdims=True))
    mixture = score / jnp.sum(score, axis=0, keepdims=True)
    new = (1.0 - SMOOTHING) * mixture + SMOOTHING / LANGS
    logw[...] = jnp.log(new)
    share = new / count * 2048.0
    every = lang[...]
    weight = jnp.zeros(every.shape, F32)
    for l in range(LANGS):
        weight = jnp.where(every == l, share[l : l + 1], weight)
    tw[...] = weight
    go.drain()


def join_stats(stats, lang, domain_weights, collective_id):
    vmem = pl.BlockSpec(memory_space=pltpu.VMEM)
    shape = stats.shape
    return pl.pallas_call(
        stats_body,
        out_shape=[
            jax.ShapeDtypeStruct((16, 128), F32),
            jax.ShapeDtypeStruct((16, 128), F32),
            jax.ShapeDtypeStruct((LANGS, 128), F32),
        ],
        in_specs=[vmem] * 3,
        out_specs=[vmem] * 3,
        scratch_shapes=[
            pltpu.VMEM((2, *shape), F32),
            pltpu.VMEM((4, *shape), F32),
            pltpu.VMEM((4, *shape), F32),
            pltpu.VMEM((2, *shape), F32),
            pltpu.VMEM((2 * LANGS + 8, 128), F32),
            pltpu.VMEM((2 * LANGS + 8, 128), F32),
            pltpu.SemaphoreType.DMA((9,)),
            pltpu.SemaphoreType.DMA((9,)),
        ],
        compiler_params=pltpu.CompilerParams(
            collective_id=collective_id, has_side_effects=True
        ),
        name="stats",
    )(stats, lang, jnp.broadcast_to(domain_weights[:, None], (LANGS, 128)))


def home_body(gu, dn, gate, up, down, o_gu, o_dn, s_gu, s_dn, r_gu, r_dn, send, recv):
    me = Place()
    go = Copies(send, recv)
    others = [lax.rem(me.f + j, 8) for j in range(1, 8)]
    to = [{"dp": me.dp, "fsdp": o, "tp": me.t} for o in others]
    greet([me.neighbour(), *to])
    first = [go.start(gu, o_gu, me.neighbour()), go.start(dn, o_dn, me.neighbour())]
    for copy in first:
        copy.wait_recv()
    for j in range(8):
        s_gu[j] = (gu[j].astype(F32) + o_gu[j].astype(F32)).astype(BF16)
        s_dn[j] = (dn[j].astype(F32) + o_dn[j].astype(F32)).astype(BF16)
    sent = []
    for o, dev in zip(others, to):
        sent.append(go.start(s_gu.at[o], r_gu.at[me.f], dev))
        sent.append(go.start(s_dn.at[o], r_dn.at[me.f], dev))
    r_gu[me.f] = s_gu[me.f]
    r_dn[me.f] = s_dn[me.f]
    for copy in sent:
        copy.wait_recv()
    for j in range(8):
        both = r_gu[j].astype(F32)
        gate[:, 64 * j : 64 * (j + 1)] = both[:, :64]
        up[:, 64 * j : 64 * (j + 1)] = both[:, 64:]
        down[64 * j : 64 * (j + 1)] = r_dn[j].astype(F32)
    go.drain()


def home(gu, dn, collective_id):
    vmem = pl.BlockSpec(memory_space=pltpu.VMEM)
    return pl.pallas_call(
        home_body,
        out_shape=[
            jax.ShapeDtypeStruct((128, 512), F32),
            jax.ShapeDtypeStruct((128, 512), F32),
            jax.ShapeDtypeStruct((512, 128), F32),
        ],
        in_specs=[vmem] * 2,
        out_specs=[vmem] * 3,
        scratch_shapes=[pltpu.VMEM(gu.shape, BF16), pltpu.VMEM(dn.shape, BF16)] * 3
        + [pltpu.SemaphoreType.DMA((16,)), pltpu.SemaphoreType.DMA((16,))],
        compiler_params=pltpu.CompilerParams(
            collective_id=collective_id, has_side_effects=True
        ),
        name="home",
    )(gu, dn)


def rms_scale(values, gain_vec):
    values = values.astype(F32)
    return (
        values * lax.rsqrt(jnp.mean(values * values, axis=-1, keepdims=True) + EPSILON) * gain_vec
    )


def row_logits(row_block, head):
    return lax.dot_general(row_block, head, (((1,), (1,)), ((), ())), preferred_element_type=F32)


def piece_stats(logits, part_targets, vocab_start):
    vocab_cols = vocab_start + jnp.arange(logits.shape[1], dtype=jnp.int32)
    high_val = jnp.max(logits, axis=1)
    exp_total = jnp.sum(jnp.exp(logits - high_val[:, None]), axis=1)
    picked = jnp.sum(jnp.where(vocab_cols[None, :] == part_targets[:, None], logits, 0.0), axis=1)
    return (high_val, exp_total, picked)


def norm_backward(mid_sum, gain_vec, d_out):
    inv_rms = lax.rsqrt(jnp.mean(mid_sum * mid_sum, axis=1, keepdims=True) + EPSILON)
    scaled_grad = d_out * gain_vec
    inner_mean = jnp.mean(mid_sum * scaled_grad, axis=1, keepdims=True)
    return (inv_rms * scaled_grad - mid_sum * inv_rms * inv_rms * inv_rms * inner_mean).astype(BF16)


def gate_grads(d_act, gate_pre, up_pre):
    sigmoid_g = jax.nn.sigmoid(gate_pre)
    d_gate = (d_act * up_pre * sigmoid_g * (1.0 + gate_pre * (1.0 - sigmoid_g))).astype(BF16)
    d_up = (d_act * gate_pre * sigmoid_g).astype(BF16)
    return (d_gate, d_up)


def local(
    ref_hidden,
    proxy_hidden,
    targets,
    languages,
    ref_gain,
    ref_head,
    proxy_gain_in,
    proxy_gain_out,
    gate_weight,
    up_weight,
    down_weight,
    proxy_head,
    domain_weights,
):
    tp = lax.axis_index("tp")
    vocab_rows = ref_head.shape[0]
    vocab_start = lax.axis_index(("fsdp", "tp")) * vocab_rows
    mine = lambda v: lax.dynamic_slice_in_dim(v, tp * 16, 16, 0)
    hidden = mine(proxy_hidden)
    normed_own = rms_scale(hidden, proxy_gain_in).astype(BF16)
    ref_own = rms_scale(ref_hidden, ref_gain).astype(BF16)
    ids = jnp.stack([mine(targets), mine(languages)])
    ids = jnp.pad(ids, ((0, 6), (0, 112)))
    rows = gate_weight.shape[0]
    gu_own = jnp.concatenate(
        [w.reshape(rows, 8, 64).transpose(1, 0, 2) for w in (gate_weight, up_weight)], axis=2
    )
    dn_own = down_weight.reshape(8, 64, 128)
    ids, normed_in, ref_all, gu_w, dn_w = gather(
        (ids, normed_own, ref_own), (True, False, False), (gu_own, dn_own), 1
    )
    group_targets = ids[..., 0, :16].reshape(2048)
    group_langs = ids[..., 1, :16].reshape(16, 128)
    normed_in = normed_in.reshape(1024, 1024)
    ref_all = ref_all.reshape(1024, 4096)
    gu_w = gu_w.reshape(1024, 128)
    pre = jnp.dot(normed_in, gu_w, preferred_element_type=F32)
    gate_pre, up_pre = pre[:, :64], pre[:, 64:]
    hidden_act = (gate_pre * jax.nn.sigmoid(gate_pre) * up_pre).astype(BF16)
    down_w = dn_w.transpose(1, 0, 2).reshape(64, 1024)
    ffn_part = jnp.dot(hidden_act, down_w, preferred_element_type=F32).astype(BF16)
    mid_sum = hidden.astype(F32) + scatter(ffn_part, 2)
    final_own = rms_scale(mid_sum, proxy_gain_out).astype(BF16)
    (final_all,) = gather((final_own,), (True,), (), 3)
    final_all = final_all.reshape(2048, 1024)
    proxy_logits = row_logits(final_all, proxy_head)
    proxy_stats = piece_stats(proxy_logits[:1024], group_targets[:1024], vocab_start)
    logits = row_logits(ref_all, ref_head)
    ref_stats = piece_stats(logits, group_targets[:1024], vocab_start)
    stats = jnp.stack(ref_stats + proxy_stats).reshape(48, 128)
    lse, token_weight, log_weights = join_stats(stats, group_langs, domain_weights, 4)
    lse, token_weight = lse.reshape(2048), token_weight.reshape(2048)
    vocab_cols = vocab_start + jnp.arange(vocab_rows, dtype=jnp.int32)
    onehot = (vocab_cols[None, :] == group_targets[:, None]).astype(F32)
    dlogits = (token_weight[:, None] * (jnp.exp(proxy_logits - lse[:, None]) - onehot)).astype(BF16)
    d_part = jnp.dot(dlogits[:1024], proxy_head, preferred_element_type=F32).astype(BF16)
    d_final = scatter(d_part, 5)
    grad_head = lax.dot_general(
        dlogits, final_all, (((0,), (0,)), ((), ())), preferred_element_type=F32
    )
    d_own = norm_backward(mid_sum, proxy_gain_out, d_final)
    (d_mid,) = gather((d_own,), (False,), (), 6)
    d_mid = d_mid.reshape(1024, 1024)
    grad_down = lax.dot_general(
        hidden_act, d_mid, (((0,), (0,)), ((), ())), preferred_element_type=F32
    )
    d_act = lax.dot_general(d_mid, down_w, (((1,), (1,)), ((), ())), preferred_element_type=F32)
    d_both = jnp.concatenate(gate_grads(d_act, gate_pre, up_pre), axis=1)
    grad_gu = lax.dot_general(
        normed_in, d_both, (((0,), (0,)), ((), ())), preferred_element_type=F32
    )
    grad_gu = grad_gu.astype(BF16).reshape(8, 128, 128)
    grad_down = grad_down.astype(BF16).reshape(64, 8, 128).transpose(1, 0, 2)
    grad_gate, grad_up, grad_down = home(grad_gu, grad_down, 7)
    return (log_weights[:, 0], grad_gate, grad_up, grad_down, grad_head)


def solution(mesh):
    in_specs = (
        P(("dp", "fsdp", "tp"), None),
        P(("dp", "fsdp"), None),
        P(("dp", "fsdp")),
        P(("dp", "fsdp")),
        P(),
        P(("fsdp", "tp"), None),
        P(),
        P(),
        P("fsdp", "tp"),
        P("fsdp", "tp"),
        P("tp", "fsdp"),
        P(("fsdp", "tp"), None),
        P(),
    )
    out_specs = (P(), P("fsdp", "tp"), P("fsdp", "tp"), P("tp", "fsdp"), P(("fsdp", "tp"), None))
    return jax.shard_map(local, mesh=mesh, in_specs=in_specs, out_specs=out_specs, check_vma=False)
```

time: 542 us -> 282 us (0.52)
  blocking collectives: 252 us -> 0 us
  Pallas kernels: 0 us -> 199 us
  waiting for transfers between devices: 112 us -> 0 us
  starting transfers between devices: 29.3 us -> 0 us
  other arithmetic: 45.3 us -> 18.5 us
  local copies, waits for them, and re-layouts: 45 us -> 21.5 us
  between operations: 14.4 us -> 0.92 us
    all_to_all x6 -> x0, blocking collectives: 222 us -> none  [the longest x5 169 us: from_everyone(): lax.all_to_all(jnp.broadcast_to(array[None], (size, *array.shape)), axis,...]
    pallas_call x0 -> x7, Pallas kernels: none -> 199 us  [the longest x3 119 us: gather(): pl.pallas_call(functools.partial(gather_body, tuple(wide), bool(weights))...]
    all_to_all x5 -> x0, waiting for transfers between devices: 75.2 us -> none  [the longest x2 62.2 us: summed_on_arrival(): lax.all_to_all(pieces, axis, split_axis=0, concat_axis=0, tiled=True)]
    all_gather x3 -> x0, waiting for transfers between devices: 37 us -> none  [the longest x1 37 us: total_of_pieces(): pieces = lax.all_gather(array, axis)]
    all_gather x1 -> x0, blocking collectives: 30 us -> none  [gather_turned(): lax.all_gather(both, axis, axis=0, tiled=True)]
    all_to_all x5 -> x0, starting transfers between devices: 29.2 us -> none  [the longest x3 18.4 us: from_everyone(): lax.all_to_all(jnp.broadcast_to(array[None], (size, *array.shape)), axis,...]
    reduce_sum x11 -> x0, other arithmetic: 27.3 us -> none  [the longest x4 13.6 us: taken_together(): return jnp.sum(everything, axis=0)]
    slice x65 -> x3, local copies, waits for them, and re-layouts: 31 us -> 4.1 us  [the longest x1 1.67 us: local(): group_targets = ids[..., 0, :16].reshape(2048)]
  transfers between devices with their start and end apart: 8 -> 0, of which waited for: 4 -> 0; matrix products, arithmetic and copies ran while one was open for 8% -> 0% of each run, Pallas kernels for 0% -> 0%
where the time goes in v1:
time: 282 us; the launch traced here: 281 us
  Pallas kernels  199 us (71%)
  matrix products  41.8 us (15%)
  local copies, waits for them, and re-layouts  21.5 us (8%)
  other arithmetic  18.5 us (7%)
    pallas_call x3, Pallas kernels, gather(): pl.pallas_call(functools.partial(gather_body, tuple(wide), bool(weights))...  119 us
    pallas_call x2, Pallas kernels, scatter(): pl.pallas_call(scatter_body, out_shape=jax.ShapeDtypeStruct((block, width...  42.8 us
    dot_general x2, matrix products, row_logits(): lax.dot_general(row_block, head, (((1,), (1,)), ((), ())), preferred_elem...  21.5 us
    pallas_call x1, Pallas kernels, home(): pl.pallas_call(home_body, out_shape=[jax.ShapeDtypeStruct((128, 512), F32...  20.8 us
    pallas_call x1, Pallas kernels, join_stats(): pl.pallas_call(stats_body, out_shape=[jax.ShapeDtypeStruct((16, 128), F32...  16.3 us
    unnamed x25, local copies, waits for them, and re-layouts  12 us
    dot_general x1, matrix products, local(): lax.dot_general(dlogits, final_all, (((0,), (0,)), ((), ())), preferred_e...  6.01 us

profile of v1, /device:TPU:1, one launch (start us, length us, event | category | flops | bytes accessed | tf_op | source)
XLA Modules:
  0.0 281.4 jit_solution(11382099623190380041)
XLA Ops:
  6.9 1.7 fusion.10.refs_2_
  11.9 57.0 %gather1.1 = (s32[2,2,4,4,2,8,128]{6,5,4,3,2,1,0:T(8,128)}, bf16[2,4,4,2,16,1024]{5,4,3,2,1,0:T(8,128)(2,1)}, bf16[2,4,4,2,16,4096]{5,4,3,2,1,0:T(8,128)(2,1)}, ...) custom-call(s32[8,128]{1,0:T(8,128)} %pad.4.refs_0_, bf16[16,1024]{1,0:T(8,128)(2,1)} %fusion.21.refs_1_, ...), custom_call_target="tpu_custom_call" | custom-call | tf_op jit(solution)/shard_map/gather1/pallas_call | solution.py:185
  68.9 15.1 %fusion.23 = (f32[1024]{0:T(1024)S(1)}, f32[1024,1024]{0,1:T(8,128)}) fusion(bf16[1024,4096]{1,0:T(8,128)(2,1)} %bitcast.86, bf16[1024,4096]{1,0:T(8,128)(2,1)} %param.18), kind=kOutput, calls=%fused_computation.57 | convolution fusion | flops 8590982144 | bytes 20975616 | tf_op jit(solution)/shard_map/dot_general | solution.py:439
  85.0 1.7 slice_reduce_fusion.1
  87.7 2.4 fusion.24
  90.2 2.1 convolution_convert_fusion
  92.3 20.0 %scatter2.1 = f32[16,1024]{1,0:T(8,128)} custom-call(bf16[2,4,128,1024]{3,2,1,0:T(8,128)(2,1)} %bitcast.64), custom_call_target="tpu_custom_call" | custom-call | tf_op jit(solution)/shard_map/scatter2/pallas_call | solution.py:264
  114.8 34.5 %gather3.1 = bf16[2,2,4,4,2,16,1024]{6,5,4,3,2,1,0:T(8,128)(2,1)} custom-call(bf16[16,1024]{1,0:T(8,128)(2,1)} %multiply_convert_fusion.4.refs_0_), custom_call_target="tpu_custom_call" | custom-call | tf_op jit(solution)/shard_map/gather3/pallas_call | solution.py:185
  149.3 6.4 %fusion.25 = f32[2048,1024]{0,1:T(8,128)S(1)} fusion(bf16[2048,1024]{1,0:T(8,128)(2,1)} %bitcast.65, bf16[1024,1024]{1,0:T(8,128)(2,1)S(1)} %copy-done), kind=kOutput, calls=%fused_computation.59 | convolution fusion | flops 4294967296 | bytes 14680064 | tf_op jit(solution)/shard_map/dot_general | solution.py:439
  156.0 4.9 %copy-done.3 = f32[1024,1024]{0,1:T(8,128)S(1)} copy-done((f32[1024,1024]{0,1:T(8,128)S(1)}, f32[1024,1024]{0,1:T(8,128)}, u32[]{:S(2)}) %copy-start.3) | copy-done | bytes 4194328
  160.9 2.2 fusion.1
  163.9 16.3 %stats.1 = (f32[16,128]{1,0:T(8,128)}, f32[16,128]{1,0:T(8,128)}, f32[64,128]{1,0:T(8,128)}) custom-call(f32[48,128]{1,0:T(8,128)} %reshape.105.st, s32[16,128]{1,0:T(8,128)} %reshape_squeeze.4.lang, f32[64,128]{1,0:T(8,128)} %broadcast_in_dim.7.dw), custom_call_target="tpu_custom_call" | custom-call | tf_op jit(solution)/shard_map/stats/pallas_call | solution.py:357
  181.6 4.8 %multiply_convert_fusion = bf16[2048,1024]{0,1:T(8,128)(2,1)S(1)} fusion(f32[2048,1024]{0,1:T(8,128)} %copy-done.1, s32[2048]{0:T(1024)S(1)} %eq.42, f32[2048]{0:T(1024)} %bitcast.84, f32[2048]{0:T(1024)} %bitcast.85, s32[1024]{0:T(1024)S(1)} %iota_add_fusion), kind=kLoop, calls=%fused_computation | loop fusion | flops 12582912 | bytes 12611584 | tf_op jit(solution)/shard_map/convert_element_type | solution.py:519
  186.4 6.0 %fusion.26 = f32[1024,1024]{1,0:T(8,128)} fusion(bf16[2048,1024]{0,1:T(8,128)(2,1)S(1)} %multiply_convert_fusion, bf16[2048,1024]{1,0:T(8,128)(2,1)S(1)} %bitcast.66), kind=kOutput, calls=%fused_computation.60 | convolution fusion | flops 4294967296 | bytes 12582912 | tf_op jit(solution)/shard_map/dot_general | solution.py:522
  192.5 3.7 %fusion.4 = bf16[1024,1024]{1,0:T(8,128)(2,1)} fusion(bf16[1024,1024]{1,0:T(8,128)(2,1)S(1)} %copy-done, bf16[2048,1024]{0,1:T(8,128)(2,1)S(1)} %multiply_convert_fusion), kind=kOutput, calls=%fused_computation.10 | convolution fusion | flops 2148532224 | bytes 6291456 | tf_op jit(solution)/shard_map/dot_general | solution.py:520
  196.2 22.7 %scatter5.1 = f32[16,1024]{1,0:T(8,128)} custom-call(bf16[2,4,128,1024]{3,2,1,0:T(8,128)(2,1)} %bitcast.69), custom_call_target="tpu_custom_call" | custom-call | tf_op jit(solution)/shard_map/scatter5/pallas_call | solution.py:264
  219.9 1.5 subtract_convert_fusion.refs_0_
  221.5 27.3 %gather6.1 = bf16[2,4,4,2,16,1024]{5,4,3,2,1,0:T(8,128)(2,1)} custom-call(bf16[16,1024]{1,0:T(8,128)(2,1)} %subtract_convert_fusion.refs_0_), custom_call_target="tpu_custom_call" | custom-call | tf_op jit(solution)/shard_map/gather6/pallas_call | solution.py:185
  248.8 2.5 multiply_convert_fusion.2
  251.3 2.1 fusion.7
  255.5 20.8 %home.1 = (f32[128,512]{1,0:T(8,128)}, f32[128,512]{1,0:T(8,128)}, f32[512,128]{1,0:T(8,128)}) custom-call(bf16[8,128,128]{2,1,0:T(8,128)(2,1)} %bitcast.75, bf16[8,64,128]{2,1,0:T(8,128)(2,1)} %bitcast.72), custom_call_target="tpu_custom_call" | custom-call | tf_op jit(solution)/shard_map/home/pallas_call | solution.py:413
  276.3 1.7 copy.41
  278.0 1.7 copy.42
  279.7 1.7 copy.43
  (50 shorter events, 19.6 us)
Async XLA Ops:
  0.6 148.7 %copy-start = (bf16[1024,1024]{1,0:T(8,128)(2,1)S(1)}, bf16[1024,1024]{1,0:T(8,128)(2,1)}, u32[]{:S(2)}) copy-start(bf16[1024,1024]{1,0:T(8,128)(2,1)} %param.24) | copy-start | bytes 6291460
  68.8 18.8 %copy-start.6 = (bf16[8,128,128]{2,1,0:T(8,128)(2,1)S(1)}, bf16[8,128,128]{2,1,0:T(8,128)(2,1)}, u32[]{:S(2)}) copy-start(bf16[8,128,128]{2,1,0:T(8,128)(2,1)} %get-tuple-element.19) | copy-start | bytes 786436
  68.8 21.3 %copy-start.8 = (bf16[8,64,128]{2,1,0:T(8,128)(2,1)S(1)}, bf16[8,64,128]{2,1,0:T(8,128)(2,1)}, u32[]{:S(2)}) copy-start(bf16[8,64,128]{2,1,0:T(8,128)(2,1)} %get-tuple-element.20) | copy-start | bytes 393220
  85.0 27.3 %copy-start.7 = (bf16[128,1024]{1,0:T(8,128)(2,1)S(1)}, bf16[128,1024]{1,0:T(8,128)(2,1)}, u32[]{:S(2)}) copy-start(bf16[128,1024]{1,0:T(8,128)(2,1)} %param.14) | copy-start | bytes 786436
  86.7 26.6 %copy-start.9 = (f32[1024]{0:T(1024)S(1)}, f32[1024]{0:T(1024)}, u32[]{:S(2)}) copy-start(f32[1024]{0:T(1024)} %param.20) | copy-start | bytes 12292
  155.7 7.5 %copy-start.1 = (f32[2048,1024]{0,1:T(8,128)}, f32[2048,1024]{0,1:T(8,128)S(1)}, u32[]{:S(2)}) copy-start(f32[2048,1024]{0,1:T(8,128)S(1)} %fusion.25) | copy-start | bytes 25165828
  155.7 5.2 %copy-start.3 = (f32[1024,1024]{0,1:T(8,128)S(1)}, f32[1024,1024]{0,1:T(8,128)}, u32[]{:S(2)}) copy-start(f32[1024,1024]{0,1:T(8,128)} %get-tuple-element.38) | copy-start | bytes 12582916
  181.6 4.8 %copy-start.2 = (bf16[2,2,4,4,2,16,1024]{6,5,4,3,2,1,0:T(8,128)(2,1)S(1)}, bf16[2,2,4,4,2,16,1024]{6,5,4,3,2,1,0:T(8,128)(2,1)}, u32[]{:S(2)}) copy-start(bf16[2,2,4,4,2,16,1024]{6,5,4,3,2,1,0:T(8,128)(2,1)} %gather3.1) | copy-start | bytes 12582916
  192.5 26.5 %copy-start.5 = (f32[16,1024]{1,0:T(8,128)S(1)}, f32[16,1024]{1,0:T(8,128)}, u32[]{:S(2)}) copy-start(f32[16,1024]{1,0:T(8,128)} %scatter2.1) | copy-start | bytes 196612
  248.8 5.3 %copy-start.4 = (bf16[2,4,4,2,16,1024]{5,4,3,2,1,0:T(8,128)(2,1)S(1)}, bf16[2,4,4,2,16,1024]{5,4,3,2,1,0:T(8,128)(2,1)}, u32[]{:S(2)}) copy-start(bf16[2,4,4,2,16,1024]{5,4,3,2,1,0:T(8,128)(2,1)} %get-tuple-element.18) | copy-start | bytes 6291460

commit v2 on v1

--- a/solution.py
+++ b/solution.py
@@ -40,6 +40,10 @@
     def on_b(self, b):
         c = self.c
         return self.at(y=(1 - c) * self.y + c * b, z=(1 - c) * b + c * self.z)
+
+    def on_ab(self, a, b):
+        c = self.c
+        return self.at(y=(1 - c) * a + c * b, z=(1 - c) * b + c * a)
 
     def core(self):
         return self.at(c=1 - self.c)
@@ -288,96 +292,349 @@
     )(x)
 
 
+OFFSETS = [(k, i) for k in (2, 1, 3, 0) for i in range(4) if k or i]
+ROWS = (2, 3, 1, 0)
+
+
+def rms_rows(values, gain):
+    values = values.astype(F32)
+    return values * lax.rsqrt(jnp.mean(values * values, axis=-1, keepdims=True) + EPSILON) * gain
+
+
+def to_plane(go, me, view, slot=None):
+    sent = {}
+    for k, i in OFFSETS:
+        to = me.on_ab(ring(me.a, i), ring(me.b, k))
+        sent[k, i] = go.start(view, view if slot is None else slot(k, i), to)
+    return sent
+
+
+def forward_body(
+    ids, hid, gain_in, gain_out, refh, ref_gain, gate, up, down, head,
+    normed, pre, fin, fin_x, mid, ref_st, tgt, lang, dnw,
+    idsg, gus, guw, ref_all, headv, rhs, logit, x, r0, acc, rs, give, rp,
+    send, recv, local,
+):
+    me = Place()
+    a, b, c, p, f = me.a, me.b, me.c, me.p, me.f
+    go = Copies(send, recv)
+    plane = [me.on_ab(ring(a, i), ring(b, k)) for k, i in OFFSETS]
+    x_peers = [me.partner(), me.neighbour(), me.opposite()]
+    flips = [me.at(y=ring(me.y, k), c=1 - c) for k in range(4)]
+    greet(plane + x_peers + flips)
+    take_head = pltpu.make_async_copy(head, headv, local.at[0])
+    take_head.start()
+    normed[c, b, a, p] = rms_rows(hid[...], gain_in[...]).astype(BF16)
+    idsg[c, b, a, 0, p] = ids[...]
+    s1 = [go.start(normed.at[c, b, a, p], normed.at[c, b, a, p], me.partner())]
+    for g, to in zip((0, 1, 1), x_peers):
+        s1.append(go.start(ids, idsg.at[c, b, a, g, p], to))
+    low = lax.broadcasted_iota(jnp.int32, (128, 128), 1) < 64
+    for i in range(4):
+        g = gate[:, 128 * i : 128 * (i + 1)].astype(F32)
+        u = up[:, 128 * i : 128 * (i + 1)].astype(F32)
+        gus[2 * i] = jnp.where(low, g, pltpu.roll(u, 64, 1)).astype(BF16)
+        gus[2 * i + 1] = jnp.where(low, pltpu.roll(g, 64, 1), u).astype(BF16)
+    here = pl.ds(pl.multiple_of(f * 128, 128), 128)
+    w_sent = []
+    for j in range(1, 8):
+        o = lax.rem(f + j, 8)
+        to = {"dp": me.dp, "fsdp": o, "tp": me.t}
+        w_sent.append(go.start(gus.at[o], guw.at[f], to))
+        w_sent.append(go.start(down.at[o], dnw.at[:, here], to))
+    guw[f] = gus[f]
+    dnw[:, here] = down[f]
+    ref_all[c, b, a, p] = rms_rows(refh[...], ref_gain[...]).astype(BF16)
+    r1 = go.start(ref_all.at[c, b, a, p], ref_all.at[c, b, a, p], me.partner())
+    for copy in s1:
+        copy.wait_recv()
+    s2 = to_plane(go, me, normed.at[c, b, a])
+    s2_ids = to_plane(go, me, idsg.at[c, b, a])
+    r1.wait_recv()
+    unit = ref_all.at[c, b, a]
+    r2 = [go.start(unit, unit, me.on_a(ring(a, k))) for k in (1, 3, 2)]
+    s3 = []
+    for k in (2, 1, 3, 0):
+        for i in range(4):
+            if k or i:
+                s2[k, i].wait_recv()
+        row = normed.at[c, ring(b, 4 - k)]
+        s3.append(go.start(row, row, me.core()))
+    for copy in s2_ids.values():
+        copy.wait_recv()
+    ids_across = go.start(idsg.at[c], idsg.at[c], me.core())
+    for copy in w_sent:
+        copy.wait_recv()
+
+    def ffn(cc, bb):
+        h = jnp.dot(
+            normed[cc, bb].reshape(128, 1024), guw[...].reshape(1024, 128),
+            preferred_element_type=F32,
+        )
+        pre[cc, bb] = h
+        h = (h * jax.nn.sigmoid(h) * pltpu.roll(h, 64, 1)).astype(BF16)[:, :64]
+        x[cc, bb] = jnp.dot(h, dnw[...], preferred_element_type=F32).astype(BF16)
+
+    across = []
+    for n, m in enumerate(ROWS):
+        s3[n].wait_recv()
+        bb = ring(a, m)
+        ffn(1 - c, bb)
+        across.append(go.start(x.at[1 - c, bb], r0.at[bb], me.core()))
+    rs_sent = {}
+    for n, m in enumerate(ROWS):
+        bb = ring(b, m)
+        ffn(c, bb)
+        across[n].wait_recv()
+        total = x[c, bb].astype(F32) + r0[bb].astype(F32)
+        acc[bb] = total.astype(BF16).reshape(acc.shape[1:])
+        for i in range(4):
+            if m or i:
+                to = me.on_ab(ring(a, i), bb)
+                rs_sent[m, i] = go.start(acc.at[bb, ring(a, i)], rs.at[4 * m + i], to)
+    for copy in r2:
+        copy.wait_recv()
+    right_b, left_b = me.on_b(ring(b, 1)), me.on_b(ring(b, 3))
+    unit = ref_all.at[c, b]
+    r3 = [go.start(unit, unit, right_b), go.start(unit, unit, left_b)]
+    cross = {0: go.start(unit, unit, me.core())}
+    ids_across.wait_recv()
+    for g in range(2):
+        for cc in range(2):
+            for bb in range(4):
+                row = idsg[cc, bb, 0, g, 0]
+                for j in range(1, 8):
+                    row = row + idsg[cc, bb, j // 2, g, j % 2]
+                tgt[8 * g + 4 * cc + bb] = row[0:1]
+                lang[8 * g + 4 * cc + bb] = row[1:2]
+    vocab = lax.broadcasted_iota(jnp.int32, (1024, 256), 0) + (f * 8 + me.t) * 1024
+
+    def ref_rows(m):
+        b_own, b_far = ring(b, m), ring(a, m)
+        rhs[0:128] = ref_all[c, b_own].reshape(128, 4096)
+        rhs[128:256] = ref_all[1 - c, b_far].reshape(128, 4096)
+
+        @pl.loop(0, 4)
+        def _(n):
+            at = pl.ds(pl.multiple_of(n * 256, 256), 256)
+            logit[at] = lax.dot_general(
+                headv[at], rhs[...], (((1,), (1,)), ((), ())), preferred_element_type=F32
+            )
+
+        value = logit[...]
+        high = jnp.max(value, axis=0, keepdims=True)
+        want = jnp.concatenate([tgt[4 * c + b_own], tgt[4 * (1 - c) + b_far]], axis=1)
+        picked = jnp.sum(jnp.where(vocab == want, value, 0.0), axis=0, keepdims=True)
+        total = jnp.sum(jnp.exp(value - high), axis=0, keepdims=True)
+        for s, got in enumerate((high, total, picked)):
+            ref_st[s, 4 * c + b_own] = got[:, :128]
+            ref_st[s, 4 * (1 - c) + b_far] = got[:, 128:]
+
+    take_head.wait()
+    cross[0].wait_recv()
+    ref_rows(0)
+    for copy in rs_sent.values():
+        copy.wait_recv()
+    total = acc[b, a].astype(F32)
+    for m, i in rs_sent:
+        total = total + rs[4 * m + i].astype(F32)
+    first, second = total[0:16], total[16:32]
+    own = jnp.where(p == 0, first, second)
+    give[...] = jnp.where(p == 0, second, first).astype(BF16)
+    swap = go.start(give, rp, me.partner())
+    swap.wait_recv()
+    middle = hid[...].astype(F32) + (own + rp[...].astype(F32))
+    mid[...] = middle
+    fin[c, b, a, p] = rms_rows(middle, gain_out[...]).astype(BF16)
+    block = fin.at[c, b, a, p]
+    f1 = go.start(block, block, me.partner())
+    f_x = [go.start(block, fin_x.at[p], to) for to in x_peers[1:]]
+    f1.wait_recv()
+    f2 = to_plane(go, me, fin.at[c, b, a])
+    r3[0].wait_recv()
+    half = ref_all.at[c, ring(b, 3), pl.ds(0, 2)]
+    r4 = [go.start(half, half, right_b)]
+    r3[1].wait_recv()
+    half = ref_all.at[c, ring(b, 1), pl.ds(2, 2)]
+    r4.append(go.start(half, half, left_b))
+    for m in (3, 1):
+        unit = ref_all.at[c, ring(b, m)]
+        cross[m] = go.start(unit, unit, me.core())
+    cross[3].wait_recv()
+    ref_rows(3)
+    f3 = []
+    for k in (2, 1, 3, 0):
+        for i in range(4):
+            if k or i:
+                f2[k, i].wait_recv()
+        row = fin.at[c, ring(b, 4 - k)]
+        f3.append(go.start(row, row, me.core()))
+    for copy in r4:
+        copy.wait_recv()
+    unit = ref_all.at[c, ring(b, 2)]
+    cross[2] = go.start(unit, unit, me.core())
+    cross[1].wait_recv()
+    ref_rows(1)
+    cross[2].wait_recv()
+    ref_rows(2)
+    for copy in f3 + f_x:
+        copy.wait_recv()
+    go.drain()
+
+
+def forward(ids, hid, gain_in, gain_out, refh, ref_gain, gate, up, down, head):
+    vmem = pl.BlockSpec(memory_space=pltpu.VMEM)
+    shape = jax.ShapeDtypeStruct
+    return pl.pallas_call(
+        forward_body,
+        out_shape=[
+            shape((2, 4, 4, 2, 16, 1024), BF16),
+            shape((2, 4, 128, 128), F32),
+            shape((2, 4, 4, 2, 16, 1024), BF16),
+            shape((2, 16, 1024), BF16),
+            shape((16, 1024), F32),
+            shape((3, 8, 1, 128), F32),
+            shape((16, 1, 128), jnp.int32),
+            shape((16, 1, 128), jnp.int32),
+            shape((64, 1024), BF16),
+        ],
+        in_specs=[vmem] * 9 + [pl.BlockSpec(memory_space=pl.ANY)],
+        out_specs=[vmem] * 9,
+        scratch_shapes=[
+            pltpu.VMEM((2, 4, 4, 2, 2, 8, 128), jnp.int32),
+            pltpu.VMEM((8, 128, 128), BF16),
+            pltpu.VMEM((8, 128, 128), BF16),
+            pltpu.VMEM((2, 4, 4, 2, 16, 4096), BF16),
+            pltpu.VMEM((1024, 4096), BF16),
+            pltpu.VMEM((256, 4096), BF16),
+            pltpu.VMEM((1024, 256), F32),
+            pltpu.VMEM((2, 4, 128, 1024), BF16),
+            pltpu.VMEM((4, 128, 1024), BF16),
+            pltpu.VMEM((4, 4, 32, 1024), BF16),
+            pltpu.VMEM((16, 32, 1024), BF16),
+            pltpu.VMEM((16, 1024), BF16),
+            pltpu.VMEM((16, 1024), BF16),
+            pltpu.SemaphoreType.DMA((110,)),
+            pltpu.SemaphoreType.DMA((110,)),
+            pltpu.SemaphoreType.DMA((1,)),
+        ],
+        compiler_params=pltpu.CompilerParams(
+            collective_id=1, has_side_effects=True, vmem_limit_bytes=60 * 2**20
+        ),
+        name="forward",
+    )(ids, hid, gain_in, gain_out, refh, ref_gain, gate, up, down, head)
+
+
 def join_all(pieces):
     out = []
-    for base in (0, 24):
-        high = functools.reduce(jnp.maximum, [s[base : base + 8] for s in pieces])
+    for base in (0, 12):
+        high = functools.reduce(jnp.maximum, [s[base : base + 4] for s in pieces])
         total = pick = None
         for s in pieces:
-            t = s[base + 8 : base + 16] * jnp.exp(s[base : base + 8] - high)
-            k = s[base + 16 : base + 24]
+            t = s[base + 4 : base + 8] * jnp.exp(s[base : base + 4] - high)
+            k = s[base + 8 : base + 12]
             total, pick = (t, k) if total is None else (total + t, pick + k)
         out += [high, total, pick]
     return jnp.concatenate(out, axis=0)
 
 
-def stats_body(st, lang, dw, lse, tw, logw, slot_c, slot_z, slot_y, slot_p, pack, other, send, recv):
+def stats_body(
+    st, lang, dw, fin_x, lse, tw, logw, fin, slot_c, slot_yz, slot_x, both, ls, lc, send, recv
+):
     me = Place()
+    a, b, c, p = me.a, me.b, me.c, me.p
     go = Copies(send, recv)
-    on_z = [me.at(z=ring(me.z, k)) for k in (1, 2, 3)]
-    on_y = [me.at(y=ring(me.y, k)) for k in (1, 2, 3)]
-    greet([me.core(), me.partner(), me.neighbour(), *on_z, *on_y])
-    mine = st[...]
-    for slots, at, peers in (
-        (slot_c, me.c, [me.core()]),
-        (slot_z, me.z, on_z),
-        (slot_y, me.y, on_y),
-        (slot_p, me.p, [me.partner()]),
-    ):
-        slots[at] = mine
-        sent = [go.start(slots.at[at], slots.at[at], to) for to in peers]
-        for copy in sent:
-            copy.wait_recv()
-        mine = join_all([slots[j] for j in range(slots.shape[0])])
-    ref_loss = mine[0:8] + jnp.log(mine[8:16]) - mine[16:24]
-    proxy_lse = mine[24:32] + jnp.log(mine[32:40])
-    excess = jnp.maximum(proxy_lse - mine[40:48] - ref_loss, 0.0)
-    own_lang = lang[0:8]
+    plane = [me.on_ab(ring(a, i), ring(b, k)) for k, i in OFFSETS]
+    x_peers = [me.partner(), me.neighbour(), me.opposite()]
+    greet(plane + x_peers + [me.core()])
+    slot_c[c] = st[c]
+    half = go.start(st.at[1 - c], slot_c.at[c], me.core())
+    fin[c, b, a] = fin_x[...]
+    half.wait_recv()
+    yz = me.y * 4 + me.z
+    slot_c_other = slot_c[1 - c]
+    mine = slot_c[c]
+    first = jnp.where(c == 0, mine, slot_c_other)
+    second = jnp.where(c == 0, slot_c_other, mine)
+    slot_yz[yz] = join_all([first, second])
+    sent = to_plane(go, me, slot_yz.at[yz])
+    beside = to_plane(go, me, fin_x, lambda k, i: fin.at[c, b, a])
+    for copy in sent.values():
+        copy.wait_recv()
+    slot_x[0, p] = join_all([slot_yz[j] for j in range(16)])
+    spread = [
+        go.start(slot_x.at[0, p], slot_x.at[g, p], to) for g, to in zip((0, 1, 1), x_peers)
+    ]
+    for copy in spread:
+        copy.wait_recv()
+    both[c, 0] = join_all([slot_x[0, 0], slot_x[0, 1]])
+    both[c, 1] = join_all([slot_x[1, 0], slot_x[1, 1]])
+    share = go.start(both.at[c], both.at[c], me.core())
+    across = []
+    for k in (2, 1, 3, 0):
+        for i in range(4):
+            if k or i:
+                beside[k, i].wait_recv()
+        row = fin.at[c, ring(b, 4 - k)]
+        across.append(go.start(row, row, me.core()))
+    share.wait_recv()
+    group = lax.rem(me.dp + me.xh, 2)
+    excess = [None, None]
+    for g in range(2):
+        now = [jnp.concatenate([both[0, g, 4 * i : 4 * i + 4], both[1, g, 4 * i : 4 * i + 4]]) for i in range(6)]
+        ref_loss = now[0] + jnp.log(now[1]) - now[2]
+        proxy_lse = now[3] + jnp.log(now[4])
+        lse[8 * g : 8 * g + 8] = proxy_lse
+        excess[g] = jnp.maximum(proxy_lse - now[5] - ref_loss, 0.0)
+    every = lang[...]
     for l in range(LANGS):
-        here = own_lang == l
-        pack[l : l + 1] = jnp.sum(jnp.where(here, excess, 0.0), axis=0, keepdims=True)
-        pack[LANGS + l : LANGS + l + 1] = jnp.sum(
-            jnp.where(here, 1.0, 0.0), axis=0, keepdims=True
-        )
-    pack[2 * LANGS : 2 * LANGS + 8] = proxy_lse
-    swap = go.start(pack, other, me.neighbour())
-    swap.wait_recv()
-    lse[0:8] = proxy_lse
-    lse[8:16] = other[2 * LANGS : 2 * LANGS + 8]
-    sums = jnp.sum(pack[0 : 2 * LANGS] + other[0 : 2 * LANGS], axis=1, keepdims=True)
-    sums = jnp.broadcast_to(sums, (2 * LANGS, 128))
-    count = jnp.maximum(sums[LANGS:], 1.0)
-    score = jnp.log(dw[...]) + STEP_SIZE * (sums[:LANGS] / count)
+        here = every == l
+        e = jnp.where(here[:8], excess[0], 0.0) + jnp.where(here[8:], excess[1], 0.0)
+        n = jnp.where(here[:8], 1.0, 0.0) + jnp.where(here[8:], 1.0, 0.0)
+        ls[l : l + 1] = jnp.sum(e, axis=0, keepdims=True)
+        lc[l : l + 1] = jnp.sum(n, axis=0, keepdims=True)
+    wide = lambda v: jnp.broadcast_to(jnp.sum(v[...], axis=1, keepdims=True), (LANGS, 128))
+    count = jnp.maximum(wide(lc), 1.0)
+    score = jnp.log(dw[...]) + STEP_SIZE * (wide(ls) / count)
     score = jnp.exp(score - jnp.max(score, axis=0, keepdims=True))
     mixture = score / jnp.sum(score, axis=0, keepdims=True)
     new = (1.0 - SMOOTHING) * mixture + SMOOTHING / LANGS
     logw[...] = jnp.log(new)
-    share = new / count * 2048.0
-    every = lang[...]
+    per_token = new / count * 2048.0
     weight = jnp.zeros(every.shape, F32)
     for l in range(LANGS):
-        weight = jnp.where(every == l, share[l : l + 1], weight)
+        weight = jnp.where(every == l, per_token[l : l + 1], weight)
     tw[...] = weight
+    for copy in across:
+        copy.wait_recv()
     go.drain()
 
 
-def join_stats(stats, lang, domain_weights, collective_id):
+def join_stats(stats, lang, domain_weights, fin_x):
     vmem = pl.BlockSpec(memory_space=pltpu.VMEM)
-    shape = stats.shape
     return pl.pallas_call(
         stats_body,
         out_shape=[
             jax.ShapeDtypeStruct((16, 128), F32),
             jax.ShapeDtypeStruct((16, 128), F32),
             jax.ShapeDtypeStruct((LANGS, 128), F32),
+            jax.ShapeDtypeStruct((2, 4, 4, 2, 16, 1024), BF16),
         ],
-        in_specs=[vmem] * 3,
-        out_specs=[vmem] * 3,
+        in_specs=[vmem] * 4,
+        out_specs=[vmem] * 4,
         scratch_shapes=[
-            pltpu.VMEM((2, *shape), F32),
-            pltpu.VMEM((4, *shape), F32),
-            pltpu.VMEM((4, *shape), F32),
-            pltpu.VMEM((2, *shape), F32),
-            pltpu.VMEM((2 * LANGS + 8, 128), F32),
-            pltpu.VMEM((2 * LANGS + 8, 128), F32),
-            pltpu.SemaphoreType.DMA((9,)),
-            pltpu.SemaphoreType.DMA((9,)),
+            pltpu.VMEM((2, 24, 128), F32),
+            pltpu.VMEM((16, 24, 128), F32),
+            pltpu.VMEM((2, 2, 24, 128), F32),
+            pltpu.VMEM((2, 2, 24, 128), F32),
+            pltpu.VMEM((LANGS, 128), F32),
+            pltpu.VMEM((LANGS, 128), F32),
+            pltpu.SemaphoreType.DMA((40,)),
+            pltpu.SemaphoreType.DMA((40,)),
         ],
-        compiler_params=pltpu.CompilerParams(
-            collective_id=collective_id, has_side_effects=True
-        ),
+        compiler_params=pltpu.CompilerParams(collective_id=4, has_side_effects=True),
         name="stats",
-    )(stats, lang, jnp.broadcast_to(domain_weights[:, None], (LANGS, 128)))
+    )(stats, lang, jnp.broadcast_to(domain_weights[:, None], (LANGS, 128)), fin_x)
 
 
 def home_body(gu, dn, gate, up, down, o_gu, o_dn, s_gu, s_dn, r_gu, r_dn, send, recv):
@@ -476,54 +733,58 @@
     proxy_head,
     domain_weights,
 ):
-    tp = lax.axis_index("tp")
+    me = Place()
     vocab_rows = ref_head.shape[0]
     vocab_start = lax.axis_index(("fsdp", "tp")) * vocab_rows
-    mine = lambda v: lax.dynamic_slice_in_dim(v, tp * 16, 16, 0)
+    mine = lambda v: lax.dynamic_slice_in_dim(v, me.t * 16, 16, 0)
     hidden = mine(proxy_hidden)
-    normed_own = rms_scale(hidden, proxy_gain_in).astype(BF16)
-    ref_own = rms_scale(ref_hidden, ref_gain).astype(BF16)
-    ids = jnp.stack([mine(targets), mine(languages)])
-    ids = jnp.pad(ids, ((0, 6), (0, 112)))
-    rows = gate_weight.shape[0]
-    gu_own = jnp.concatenate(
-        [w.reshape(rows, 8, 64).transpose(1, 0, 2) for w in (gate_weight, up_weight)], axis=2
+    ids = jnp.tile(jnp.stack([mine(targets), mine(languages)]), (4, 8))
+    lanes = lax.broadcasted_iota(jnp.int32, (8, 128), 1)
+    ids = jnp.where(lax.div(lanes, 16) == me.a * 2 + me.p, ids, 0)
+    normed_in, pre, final_own, fin_x, mid_sum, ref_stats, group_targets, langs, down_w = forward(
+        ids,
+        hidden,
+        proxy_gain_in[None],
+        proxy_gain_out[None],
+        ref_hidden,
+        ref_gain[None],
+        gate_weight,
+        up_weight,
+        down_weight.reshape(8, 64, 128),
+        ref_head,
     )
-    dn_own = down_weight.reshape(8, 64, 128)
-    ids, normed_in, ref_all, gu_w, dn_w = gather(
-        (ids, normed_own, ref_own), (True, False, False), (gu_own, dn_own), 1
-    )
-    group_targets = ids[..., 0, :16].reshape(2048)
-    group_langs = ids[..., 1, :16].reshape(16, 128)
+    group_targets = group_targets.reshape(2048)
     normed_in = normed_in.reshape(1024, 1024)
-    ref_all = ref_all.reshape(1024, 4096)
-    gu_w = gu_w.reshape(1024, 128)
-    pre = jnp.dot(normed_in, gu_w, preferred_element_type=F32)
+    pre = pre.reshape(1024, 128)
     gate_pre, up_pre = pre[:, :64], pre[:, 64:]
     hidden_act = (gate_pre * jax.nn.sigmoid(gate_pre) * up_pre).astype(BF16)
-    down_w = dn_w.transpose(1, 0, 2).reshape(64, 1024)
-    ffn_part = jnp.dot(hidden_act, down_w, preferred_element_type=F32).astype(BF16)
-    mid_sum = hidden.astype(F32) + scatter(ffn_part, 2)
-    final_own = rms_scale(mid_sum, proxy_gain_out).astype(BF16)
-    (final_all,) = gather((final_own,), (True,), (), 3)
-    final_all = final_all.reshape(2048, 1024)
-    proxy_logits = row_logits(final_all, proxy_head)
-    proxy_stats = piece_stats(proxy_logits[:1024], group_targets[:1024], vocab_start)
-    logits = row_logits(ref_all, ref_head)
-    ref_stats = piece_stats(logits, group_targets[:1024], vocab_start)
-    stats = jnp.stack(ref_stats + proxy_stats).reshape(48, 128)
-    lse, token_weight, log_weights = join_stats(stats, group_langs, domain_weights, 4)
+    final_own = final_own.reshape(1024, 1024)
+    logits_own = row_logits(final_own, proxy_head)
+    proxy_stats = piece_stats(logits_own, group_targets[:1024], vocab_start)
+    stats = jnp.concatenate([ref_stats.reshape(3, 8, 128), jnp.stack(proxy_stats).reshape(3, 8, 128)])
+    stats = stats.reshape(6, 2, 4, 128).transpose(1, 0, 2, 3).reshape(2, 24, 128)
+    lse, token_weight, log_weights, final_far = join_stats(
+        stats, langs.reshape(16, 128), domain_weights, fin_x
+    )
+    final_far = final_far.reshape(1024, 1024)
     lse, token_weight = lse.reshape(2048), token_weight.reshape(2048)
     vocab_cols = vocab_start + jnp.arange(vocab_rows, dtype=jnp.int32)
-    onehot = (vocab_cols[None, :] == group_targets[:, None]).astype(F32)
-    dlogits = (token_weight[:, None] * (jnp.exp(proxy_logits - lse[:, None]) - onehot)).astype(BF16)
-    d_part = jnp.dot(dlogits[:1024], proxy_head, preferred_element_type=F32).astype(BF16)
+
+    def to_dlogits(logits, at):
+        onehot = (vocab_cols[None, :] == group_targets[at, None]).astype(F32)
+        share = jnp.exp(logits - lse[at, None]) - onehot
+        return (token_weight[at, None] * share).astype(BF16)
+
+    own, far = slice(0, 1024), slice(1024, 2048)
+    d_own = to_dlogits(logits_own, own)
+    d_part = jnp.dot(d_own, proxy_head, preferred_element_type=F32).astype(BF16)
     d_final = scatter(d_part, 5)
-    grad_head = lax.dot_general(
-        dlogits, final_all, (((0,), (0,)), ((), ())), preferred_element_type=F32
-    )
-    d_own = norm_backward(mid_sum, proxy_gain_out, d_final)
-    (d_mid,) = gather((d_own,), (False,), (), 6)
+    d_far = to_dlogits(row_logits(final_far, proxy_head), far)
+    rows = (((0,), (0,)), ((), ()))
+    grad_head = lax.dot_general(d_own, final_own, rows, preferred_element_type=F32)
+    grad_head = grad_head + lax.dot_general(d_far, final_far, rows, preferred_element_type=F32)
+    d_mid = norm_backward(mid_sum, proxy_gain_out, d_final)
+    (d_mid,) = gather((d_mid,), (False,), (), 6)
     d_mid = d_mid.reshape(1024, 1024)
     grad_down = lax.dot_general(
         hidden_act, d_mid, (((0,), (0,)), ((), ())), preferred_element_type=F32

time: 282 us -> 239 us (0.85)
  Pallas kernels: 199 us -> 184 us
  other arithmetic: 18.5 us -> 6.83 us
  local copies, waits for them, and re-layouts: 21.5 us -> 11 us
  matrix products: 41.8 us -> 35.7 us
    pallas_call x3 -> x1, Pallas kernels: 119 us -> 28.4 us  [gather(): pl.pallas_call(functools.partial(gather_body, tuple(wide), bool(weights))...]
    pallas_call x0 -> x1, Pallas kernels: none -> 87.5 us  [forward(): pl.pallas_call(forward_body, out_shape=[shape((2, 4, 4, 2, 16, 1024), BF1...]
    pallas_call x2 -> x1, Pallas kernels: 42.8 us -> 20.4 us  [scatter(): pl.pallas_call(scatter_body, out_shape=jax.ShapeDtypeStruct((block, width...]
    dot_general x2 -> x1, matrix products: 21.5 us -> 5.91 us  [row_logits(): lax.dot_general(row_block, head, (((1,), (1,)), ((), ())), preferred_elem...]
    pallas_call x1, Pallas kernels: 16.3 us -> 26.7 us  [join_stats(): pl.pallas_call(stats_body, out_shape=[jax.ShapeDtypeStruct((16, 128), F32...]
    convert_element_type x5 -> x0, other arithmetic: 9.55 us -> none  [the longest x1 4.82 us: local(): (token_weight[:, None] * (jnp.exp(proxy_logits - lse[:, None]) - onehot))...]
    dot_general x4 -> x3, matrix products: 14.3 us -> 23.7 us  [the longest x1 8.99 us: local(): lax.dot_general(d_far, final_far, rows, preferred_element_type=F32)]
    unnamed x25 -> x29, local copies, waits for them, and re-layouts: 12 us -> 3.56 us
where the time goes in v2:
time: 239 us; the launch traced here: 238 us
  Pallas kernels  184 us (77%)
  matrix products  35.7 us (15%)
  local copies, waits for them, and re-layouts  11 us (5%)
  other arithmetic  6.83 us (3%)
    pallas_call x1, Pallas kernels, forward(): pl.pallas_call(forward_body, out_shape=[shape((2, 4, 4, 2, 16, 1024), BF1...  87.5 us
    pallas_call x1, Pallas kernels, gather(): pl.pallas_call(functools.partial(gather_body, tuple(wide), bool(weights))...  28.4 us
    pallas_call x1, Pallas kernels, join_stats(): pl.pallas_call(stats_body, out_shape=[jax.ShapeDtypeStruct((16, 128), F32...  26.7 us
    pallas_call x1, Pallas kernels, home(): pl.pallas_call(home_body, out_shape=[jax.ShapeDtypeStruct((128, 512), F32...  20.8 us
    pallas_call x1, Pallas kernels, scatter(): pl.pallas_call(scatter_body, out_shape=jax.ShapeDtypeStruct((block, width...  20.4 us
    dot_general x1, matrix products, local(): lax.dot_general(d_far, final_far, rows, preferred_element_type=F32)  8.99 us
    dot_general x1, matrix products, local(): lax.dot_general(d_own, final_own, rows, preferred_element_type=F32)  8.5 us
    dot_general x1, matrix products, local(): d_part = jnp.dot(d_own, proxy_head, preferred_element_type=F32).astype(BF16)  6.22 us

profile of v2, /device:TPU:1, one launch (start us, length us, event | category | flops | bytes accessed | tf_op | source)
XLA Modules:
  0.0 238.2 jit_solution(1488725946466145633)
XLA Ops:
  0.7 0.9 dynamic-slice_bitcast_fusion
  2.3 1.4 constant_dynamic-slice_fusion.hid
  3.6 87.5 %forward.1 = (bf16[2,4,4,2,16,1024]{5,4,3,2,1,0:T(8,128)(2,1)}, f32[2,4,128,128]{3,2,1,0:T(8,128)}, bf16[2,4,4,2,16,1024]{5,4,3,2,1,0:T(8,128)(2,1)}, bf16[2,16,...) custom-call(s32[8,128]{1,0:T(8,128)} %broadcast_select_fusion.ids, ...), custom_call_target="tpu_custom_call" | custom-call | tf_op jit(solution)/shard_map/forward/pallas_call | solution.py:488
  91.2 5.9 %fusion.22 = (f32[1024]{0:T(1024)S(1)}, f32[1024,1024]{0,1:T(8,128)}) fusion(bf16[1024,1024]{1,0:T(8,128)(2,1)} %bitcast.74, bf16[1024,1024]{1,0:T(8,128)(2,1)S(1)} %copy-done), kind=kOutput, calls=%fused_computation.50 | convolution fusion | flops 2148531200 | bytes 8392704 | tf_op jit(solution)/shard_map/dot_general | solution.py:696
  97.1 3.1 %exponential_reduce_fusion = (f32[1024]{0:T(1024)S(1)}, f32[1024]{0:T(1024)S(1)}) fusion(f32[1024,1024]{0,1:T(8,128)} %get-tuple-element.52, f32[1024]{0:T(1024)S(1)} %get-tuple-element.51, s32[1024]{0:T(1024)S(1)} %bitcast.67, s32[1024]{0:T(1024)S(1)} %iota_add_fusion), kind=kLoop, calls=%fused_computation.7 | loop fusion | flops 5240832 | bytes 4214784 | tf_op jit(solution)/shard_map/reduce_sum | solution.py:702
  100.8 0.7 broadcast_in_dim.21.dw
  101.5 26.7 %stats.1 = (f32[16,128]{1,0:T(8,128)}, f32[16,128]{1,0:T(8,128)}, f32[64,128]{1,0:T(8,128)}, bf16[2,4,4,2,16,1024]{5,4,3,2,1,0:T(8,128)(2,1)}) custom-call(f32[2,24,128]{2,1,0:T(8,128)} %bitcast.61, s32[16,128]{1,0:T(8,128)} %bitcast.71, f32[64,128]{1,0:T(8,128)} %broadcast_in_dim.21.dw, bf16[2,16,1024]{2,1,0:T(8,128)(2,1)} %get-tuple-element.25.fin_x), custom_call_target="tpu_custom_call" | custom-call | tf_op jit(solution)/shard_map/stats/pallas_call | solution.py:615
  128.3 1.4 slice_reduce_fusion
  129.6 0.9 fusion.20
  130.6 1.2 copy.26
  132.0 0.7 slice_bitcast_fusion
  133.4 6.2 %convolution_convert_fusion = bf16[1024,1024]{1,0:T(8,128)(2,1)} fusion(bf16[1024,1024]{1,0:T(8,128)(2,1)S(1)} %copy-done, f32[1024,1024]{0,1:T(8,128)} %get-tuple-element.52, f32[1024]{0:T(1024)S(1)} %get-tuple-element.48, f32[1024]{0:T(1024)S(1)} %get-tuple-element.46, s32[1024]{0:T(1024)S(1)} %bitcast.68, s32[1024]{0:T(1024)S(1)} %iota_add_fusion), kind=kOutput, calls=%fused_computation.14 | convolution fusion | flops 2154823680 | bytes 8404992 | tf_op jit(solution)/shard_map/dot_general | solution.py:780
  139.6 20.4 %scatter5.1 = f32[16,1024]{1,0:T(8,128)} custom-call(bf16[2,4,128,1024]{3,2,1,0:T(8,128)(2,1)} %bitcast.56), custom_call_target="tpu_custom_call" | custom-call | tf_op jit(solution)/shard_map/scatter5/pallas_call | solution.py:268
  160.1 1.0 multiply_reduce_fusion.1
  161.0 1.5 subtract_convert_fusion.refs_0_
  162.6 28.4 %gather6.1 = bf16[2,4,4,2,16,1024]{5,4,3,2,1,0:T(8,128)(2,1)} custom-call(bf16[16,1024]{1,0:T(8,128)(2,1)} %subtract_convert_fusion.refs_0_), custom_call_target="tpu_custom_call" | custom-call | tf_op jit(solution)/shard_map/gather6/pallas_call | solution.py:189
  191.1 2.5 %multiply_convert_fusion.4 = (bf16[1024,64]{0,1:T(8,128)(2,1)S(1)}, bf16[1024,64]{0,1:T(8,128)(2,1)S(1)}) fusion(f32[1024,64]{0,1:T(8,128)S(1)} %copy.26, f32[1024,64]{0,1:T(8,128)S(1)} %copy.25, bf16[1024,1024]{1,0:T(8,128)(2,1)} %bitcast.54, bf16[64,1024]{1,0:T(8,128)(2,1)S(1)} %copy-done.11), kind=kOutput, calls=%fused_computation.24 | convolution fusion | flops 135069696 | bytes 3014656 | tf_op jit(solution)/shard_map/dot_general | solution.py:792
  193.6 3.1 %convolution_convert_fusion.1 = bf16[1024,128]{1,0:T(8,128)(2,1)} fusion(bf16[1024,1024]{1,0:T(8,128)(2,1)} %bitcast.76, bf16[1024,64]{0,1:T(8,128)(2,1)S(1)} %get-tuple-element.42, bf16[1024,64]{0,1:T(8,128)(2,1)S(1)} %get-tuple-element.41), kind=kOutput, calls=%fused_computation.15 | convolution fusion | flops 269090816 | bytes 2621440 | tf_op jit(solution)/shard_map/dot_general | solution.py:794
  197.8 20.8 %home.1 = (f32[128,512]{1,0:T(8,128)}, f32[128,512]{1,0:T(8,128)}, f32[512,128]{1,0:T(8,128)}) custom-call(bf16[8,128,128]{2,1,0:T(8,128)(2,1)} %bitcast.59, bf16[8,64,128]{2,1,0:T(8,128)(2,1)} %bitcast.58), custom_call_target="tpu_custom_call" | custom-call | tf_op jit(solution)/shard_map/home/pallas_call | solution.py:670
  218.6 9.0 %fusion.4 = f32[1024,1024]{1,0:T(8,128)} fusion(bf16[1024,1024]{1,0:T(8,128)(2,1)} %bitcast.77, s32[1024]{0:T(1024)S(1)} %bitcast.73, f32[1024]{0:T(1024)S(1)} %get-tuple-element.47, f32[1024]{0:T(1024)S(1)} %get-tuple-element.45, s32[1024]{0:T(1024)S(1)} %iota_add_fusion, bf16[1024,1024]{1,0:T(8,128)(2,1)S(1)} %copy-done), kind=kOutput, calls=%fused_computation.8 | convolution fusion | flops 4301258752 | bytes 8404992 | tf_op jit(solution)/shard_map/dot_general | solution.py:785
  227.6 8.5 %convolution_add_fusion = f32[1024,1024]{1,0:T(8,128)} fusion(f32[1024,1024]{1,0:T(8,128)} %fusion.4, bf16[1024,1024]{1,0:T(8,128)(2,1)} %bitcast.75, f32[1024,1024]{0,1:T(8,128)} %get-tuple-element.52, f32[1024]{0:T(1024)S(1)} %get-tuple-element.48, f32[1024]{0:T(1024)S(1)} %get-tuple-element.46, s32[1024]{0:T(1024)S(1)} %bitcast.69, ...), kind=kOutput, calls=%fused_computation.13 | convolution fusion | flops 2154823680 | bytes 14696448 | tf_op jit(solution)/shard_map/dot_general | solution.py:784
  236.1 0.7 copy.35
  236.8 0.7 copy.36
  237.5 0.7 copy.37
  (38 shorter events, 3.4 us)
Async XLA Ops:
  0.6 90.5 %copy-start = (bf16[1024,1024]{1,0:T(8,128)(2,1)S(1)}, bf16[1024,1024]{1,0:T(8,128)(2,1)}, u32[]{:S(2)}) copy-start(bf16[1024,1024]{1,0:T(8,128)(2,1)} %param.24) | copy-start | bytes 6291460
  91.2 5.9 %copy-start.9 = (s32[16,1,128]{2,1,0:T(1,128)S(1)}, s32[16,1,128]{2,1,0:T(1,128)}, u32[]{:S(2)}) copy-start(s32[16,1,128]{2,1,0:T(1,128)} %get-tuple-element.23) | copy-start | bytes 24580
  97.1 3.1 %copy-start.8 = (f32[3,8,1,128]{3,2,1,0:T(1,128)S(1)}, f32[3,8,1,128]{3,2,1,0:T(1,128)}, u32[]{:S(2)}) copy-start(f32[3,8,1,128]{3,2,1,0:T(1,128)} %get-tuple-element.21) | copy-start | bytes 36868
  97.1 3.8 %copy-start.10 = (f32[64]{0:T(128)S(1)}, f32[64]{0:T(128)}, u32[]{:S(2)}) copy-start(f32[64]{0:T(128)} %param.25) | copy-start | bytes 772
  97.1 32.6 %copy-start.2 = (f32[2,4,128,128]{3,2,1,0:T(8,128)S(1)}, f32[2,4,128,128]{3,2,1,0:T(8,128)}, u32[]{:S(2)}) copy-start(f32[2,4,128,128]{3,2,1,0:T(8,128)} %get-tuple-element.32) | copy-start | bytes 1572868
  133.4 26.7 %copy-start.6 = (f32[16,1024]{1,0:T(8,128)S(1)}, f32[16,1024]{1,0:T(8,128)}, u32[]{:S(2)}) copy-start(f32[16,1024]{1,0:T(8,128)} %get-tuple-element.28) | copy-start | bytes 196612
  133.4 26.7 %copy-start.7 = (f32[1024]{0:T(1024)S(1)}, f32[1024]{0:T(1024)}, u32[]{:S(2)}) copy-start(f32[1024]{0:T(1024)} %param.20) | copy-start | bytes 12292
  139.6 51.5 %copy-start.11 = (bf16[64,1024]{1,0:T(8,128)(2,1)S(1)}, bf16[64,1024]{1,0:T(8,128)(2,1)}, u32[]{:S(2)}) copy-start(bf16[64,1024]{1,0:T(8,128)(2,1)} %get-tuple-element.31) | copy-start | bytes 393220
  191.0 5.6 %copy-start.1 = (bf16[2,4,4,2,16,1024]{5,4,3,2,1,0:T(8,128)(2,1)S(1)}, bf16[2,4,4,2,16,1024]{5,4,3,2,1,0:T(8,128)(2,1)}, u32[]{:S(2)}) copy-start(bf16[2,4,4,2,16,1024]{5,4,3,2,1,0:T(8,128)(2,1)} %gather6.1) | copy-start | bytes 6291460
  227.6 8.5 %copy-start.5 = (f32[128,512]{1,0:T(8,128)S(1)}, f32[128,512]{1,0:T(8,128)}, u32[]{:S(2)}) copy-start(f32[128,512]{1,0:T(8,128)} %get-tuple-element.61) | copy-start | bytes 786436
  227.6 9.2 %copy-start.4 = (f32[128,512]{1,0:T(8,128)S(1)}, f32[128,512]{1,0:T(8,128)}, u32[]{:S(2)}) copy-start(f32[128,512]{1,0:T(8,128)} %get-tuple-element.62) | copy-start | bytes 786436
  227.6 9.9 %copy-start.3 = (f32[512,128]{1,0:T(8,128)S(1)}, f32[512,128]{1,0:T(8,128)}, u32[]{:S(2)}) copy-start(f32[512,128]{1,0:T(8,128)} %get-tuple-element.63) | copy-start | bytes 786436

commit v3 on v2

--- a/solution.py
+++ b/solution.py
@@ -49,13 +49,13 @@
         return self.at(c=1 - self.c)
 
     def partner(self):
-        return self.at(dp=1 - self.dp, xh=1 - self.xh)
+        return self.at(xh=1 - self.xh)
 
     def neighbour(self):
         return self.at(dp=1 - self.dp)
 
     def opposite(self):
-        return self.at(xh=1 - self.xh)
+        return self.at(dp=1 - self.dp, xh=1 - self.xh)
 
 
 class Copies:
@@ -90,206 +90,6 @@
 
 def ring(i, k):
     return lax.rem(i + k, 4)
-
-
-def gather_body(wide, weights, *refs):
-    n = len(wide)
-    m = 2 if weights else 0
-    ins, w_ins = refs[:n], refs[n : n + m]
-    outs, w_outs = refs[n + m : 2 * n + m], refs[2 * n + m : 2 * n + 2 * m]
-    send, recv, local = refs[2 * n + 2 * m :]
-    me = Place()
-    a, b, c, p = me.a, me.b, me.c, me.p
-    go = Copies(send, recv)
-    right_a, left_a = me.on_a(ring(a, 1)), me.on_a(ring(a, 3))
-    right_b, left_b = me.on_b(ring(b, 1)), me.on_b(ring(b, 3))
-    peers = [me.core(), me.partner(), right_a, left_a, right_b, left_b]
-    if any(wide):
-        peers += [me.neighbour(), me.opposite()]
-    if weights:
-        others = [lax.rem(me.f + j, 8) for j in range(1, 8)]
-        kept = {"dp": me.dp, "tp": me.t}
-        peers = peers[1:] + [{**kept, "fsdp": o} for o in others]
-    greet(peers)
-
-    def block(i, g, *at):
-        return outs[i].at[(g, *at)] if wide[i] else outs[i].at[at]
-
-    sides = [range(2) if w else range(1) for w in wide]
-    locals_, first = [], []
-    for i in range(n):
-        mine = pltpu.make_async_copy(ins[i], block(i, 0, c, b, a, p), local.at[i])
-        mine.start()
-        locals_.append(mine)
-        first.append(go.start(ins[i], block(i, 0, c, b, a, p), me.partner()))
-        if wide[i]:
-            first.append(go.start(ins[i], block(i, 1, c, b, a, p), me.neighbour()))
-            first.append(go.start(ins[i], block(i, 1, c, b, a, p), me.opposite()))
-    w_copies = []
-    for k in range(m):
-        mine = pltpu.make_async_copy(w_ins[k].at[me.f], w_outs[k].at[me.f], local.at[n + k])
-        mine.start()
-        locals_.append(mine)
-        for o in others if weights else ():
-            w_copies.append(go.start(w_ins[k].at[o], w_outs[k].at[me.f], {**kept, "fsdp": o}))
-    for copy in first:
-        copy.wait_recv()
-    for copy in locals_:
-        copy.wait()
-    steps = [(i, g) for i in range(n) for g in sides[i]]
-    near = []
-    for i, g in steps:
-        unit = block(i, g, c, b, a)
-        near.append((go.start(unit, unit, right_a), go.start(unit, unit, left_a)))
-    last = []
-    for (i, g), (to_right, to_left) in zip(steps, near):
-        to_right.wait_recv()
-        half = block(i, g, c, b, ring(a, 3), 0)
-        last.append(go.start(half, half, right_a))
-        to_left.wait_recv()
-        half = block(i, g, c, b, ring(a, 1), 1)
-        last.append(go.start(half, half, left_a))
-    for copy in last:
-        copy.wait_recv()
-    near, across = [], []
-    for i, g in steps:
-        unit = block(i, g, c, b)
-        near.append((go.start(unit, unit, right_b), go.start(unit, unit, left_b)))
-        across.append(go.start(unit, unit, me.core()))
-    last = []
-    for (i, g), (to_right, to_left) in zip(steps, near):
-        to_right.wait_recv()
-        half = block(i, g, c, ring(b, 3), pl.ds(0, 2))
-        last.append(go.start(half, half, right_b))
-        to_left.wait_recv()
-        half = block(i, g, c, ring(b, 1), pl.ds(2, 2))
-        last.append(go.start(half, half, left_b))
-        for k in (3, 1):
-            unit = block(i, g, c, ring(b, k))
-            across.append(go.start(unit, unit, me.core()))
-    for copy in last:
-        copy.wait_recv()
-    for i, g in steps:
-        unit = block(i, g, c, ring(b, 2))
-        across.append(go.start(unit, unit, me.core()))
-    for copy in across + w_copies:
-        copy.wait_recv()
-    go.drain()
-
-
-def gather(blocks, wide, weights, collective_id):
-    n, m = len(blocks), len(weights)
-    shapes = [
-        jax.ShapeDtypeStruct(((2,) if w else ()) + (2, 4, 4, 2) + x.shape, x.dtype)
-        for x, w in zip(blocks, wide)
-    ] + [jax.ShapeDtypeStruct(w.shape, w.dtype) for w in weights]
-    count = sum(27 if w else 13 for w in wide) + 7 * m
-    vmem = pl.BlockSpec(memory_space=pltpu.VMEM)
-    hbm = pl.BlockSpec(memory_space=pl.ANY)
-    return pl.pallas_call(
-        functools.partial(gather_body, tuple(wide), bool(weights)),
-        out_shape=shapes,
-        in_specs=[vmem] * (n + m),
-        out_specs=[hbm] * (n + m),
-        scratch_shapes=[
-            pltpu.SemaphoreType.DMA((count,)),
-            pltpu.SemaphoreType.DMA((count,)),
-            pltpu.SemaphoreType.DMA((n + m,)),
-        ],
-        compiler_params=pltpu.CompilerParams(
-            collective_id=collective_id, has_side_effects=True
-        ),
-        name="gather%d" % collective_id,
-    )(*blocks, *weights)
-
-
-def scatter_body(x, out, r0, acc, hr, hl, ur, ul, acc1, ra, acc2, give, rp, send, recv):
-    me = Place()
-    a, b, c, p = me.a, me.b, me.c, me.p
-    go = Copies(send, recv)
-    right_a, left_a, far_a = (me.on_a(ring(a, k)) for k in (1, 3, 2))
-    right_b, left_b = me.on_b(ring(b, 1)), me.on_b(ring(b, 3))
-    greet([me.core(), me.partner(), right_a, left_a, far_a, right_b, left_b])
-    halves = x.shape[2] // 2
-    lo, hi = pl.ds(0, halves), pl.ds(halves, halves)
-    order = (2, 1, 3, 0)
-    got = []
-    for k in order:
-        j = ring(a, k)
-        got.append(go.start(x.at[1 - c, j], r0.at[j], me.core()))
-
-    def join(k):
-        j = ring(b, order[k])
-        got[k].wait_recv()
-        acc[j] = (x[c, j].astype(F32) + r0[j].astype(F32)).astype(BF16)
-        return j
-
-    far = join(0)
-    s_r = go.start(acc.at[far, lo], hr, right_b)
-    s_l = go.start(acc.at[far, hi], hl, left_b)
-    near_r = join(1)
-    t_r = go.start(acc.at[near_r, hi], ul.at[hi], right_b)
-    near_l = join(2)
-    t_l = go.start(acc.at[near_l, lo], ur.at[lo], left_b)
-    s_r.wait_recv()
-    acc[near_r, lo] = (acc[near_r, lo].astype(F32) + hr[...].astype(F32)).astype(BF16)
-    v_r = go.start(acc.at[near_r, lo], ul.at[lo], right_b)
-    s_l.wait_recv()
-    acc[near_l, hi] = (acc[near_l, hi].astype(F32) + hl[...].astype(F32)).astype(BF16)
-    v_l = go.start(acc.at[near_l, hi], ur.at[hi], left_b)
-    own = join(3)
-    for copy in (t_r, t_l, v_r, v_l):
-        copy.wait_recv()
-    total = acc[own].astype(F32) + ul[...].astype(F32) + ur[...].astype(F32)
-    acc1[...] = total.astype(BF16).reshape(acc1.shape)
-    sends = [
-        go.start(acc1.at[ring(a, k)], ra.at[i], to)
-        for i, (k, to) in enumerate(((2, far_a), (1, right_a), (3, left_a)))
-    ]
-    for copy in sends:
-        copy.wait_recv()
-    total = acc1[a].astype(F32)
-    for i in range(3):
-        total = total + ra[i].astype(F32)
-    acc2[...] = total.reshape(acc2.shape)
-    give[...] = acc2[1 - p].astype(BF16)
-    swap = go.start(give, rp, me.partner())
-    swap.wait_recv()
-    out[...] = acc2[p] + rp[...].astype(F32)
-    go.drain()
-
-
-def scatter(x, collective_id):
-    rows, width = x.shape
-    unit = rows // 8
-    block = rows // 64
-    x = x.reshape(2, 4, unit, width)
-    vmem = pl.BlockSpec(memory_space=pltpu.VMEM)
-    return pl.pallas_call(
-        scatter_body,
-        out_shape=jax.ShapeDtypeStruct((block, width), F32),
-        in_specs=[vmem],
-        out_specs=vmem,
-        scratch_shapes=[
-            pltpu.VMEM((4, unit, width), BF16),
-            pltpu.VMEM((4, unit, width), BF16),
-            pltpu.VMEM((unit // 2, width), BF16),
-            pltpu.VMEM((unit // 2, width), BF16),
-            pltpu.VMEM((unit, width), BF16),
-            pltpu.VMEM((unit, width), BF16),
-            pltpu.VMEM((4, unit // 4, width), BF16),
-            pltpu.VMEM((3, unit // 4, width), BF16),
-            pltpu.VMEM((2, block, width), F32),
-            pltpu.VMEM((block, width), BF16),
-            pltpu.VMEM((block, width), BF16),
-            pltpu.SemaphoreType.DMA((14,)),
-            pltpu.SemaphoreType.DMA((14,)),
-        ],
-        compiler_params=pltpu.CompilerParams(
-            collective_id=collective_id, has_side_effects=True
-        ),
-        name="scatter%d" % collective_id,
-    )(x)
 
 
 OFFSETS = [(k, i) for k in (2, 1, 3, 0) for i in range(4) if k or i]
@@ -578,7 +378,6 @@
         row = fin.at[c, ring(b, 4 - k)]
         across.append(go.start(row, row, me.core()))
     share.wait_recv()
-    group = lax.rem(me.dp + me.xh, 2)
     excess = [None, None]
     for g in range(2):
         now = [jnp.concatenate([both[0, g, 4 * i : 4 * i + 4], both[1, g, 4 * i : 4 * i + 4]]) for i in range(6)]
@@ -637,59 +436,206 @@
     )(stats, lang, jnp.broadcast_to(domain_weights[:, None], (LANGS, 128)), fin_x)
 
 
-def home_body(gu, dn, gate, up, down, o_gu, o_dn, s_gu, s_dn, r_gu, r_dn, send, recv):
+def backward_body(
+    x, mid, gain, lse, tw, tgt, d_t, f_own, f_far, head, normed, pre, down_w,
+    grad_head, gate, up, down,
+    vd, vo, vf, vh, vn, vp, r0, acc, rs, give, rp, dmid, comb, oth, s4, rg, gh,
+    send, recv, hsend, hrecv, local, gsem,
+):
     me = Place()
+    a, b, c, p, f = me.a, me.b, me.c, me.p, me.f
     go = Copies(send, recv)
-    others = [lax.rem(me.f + j, 8) for j in range(1, 8)]
-    to = [{"dp": me.dp, "fsdp": o, "tp": me.t} for o in others]
-    greet([me.neighbour(), *to])
-    first = [go.start(gu, o_gu, me.neighbour()), go.start(dn, o_dn, me.neighbour())]
-    for copy in first:
-        copy.wait_recv()
+    plane = [me.on_ab(ring(a, i), ring(b, k)) for k, i in OFFSETS]
+    homes = [
+        (i, side, {"dp": me.dp if side == 0 else 1 - me.dp, "fsdp": 2 * ring(me.y, i) + me.dp, "tp": me.t})
+        for i in range(4)
+        for side in range(2)
+    ]
+    flips = [me.at(y=ring(me.y, k), c=1 - c) for k in range(4)]
+    across_dp = [me.at(dp=1 - me.dp, y=ring(me.y, k), c=cc) for k in range(4) for cc in range(2)]
+    greet(plane + [me.partner()] + flips + across_dp)
+    loads = [
+        pltpu.make_async_copy(src, dst, local.at[n])
+        for n, (src, dst) in enumerate(
+            ((head, vh), (f_far, vf), (d_t, vd), (f_own, vo), (normed, vn), (pre, vp))
+        )
+    ]
+    across = []
+    for m in ROWS:
+        bb = ring(a, m)
+        across.append(go.start(x.at[1 - c, bb], r0.at[bb], me.core()))
+    for load in loads:
+        load.start()
+    sent = {}
+    for n, m in enumerate(ROWS):
+        bb = ring(b, m)
+        across[n].wait_recv()
+        total = x[c, bb].astype(F32) + r0[bb].astype(F32)
+        acc[bb] = total.astype(BF16).reshape(acc.shape[1:])
+        for i in range(4):
+            if m or i:
+                to = me.on_ab(ring(a, i), bb)
+                sent[m, i] = go.start(acc.at[bb, ring(a, i)], rs.at[4 * m + i], to)
+    for load in loads[:4]:
+        load.wait()
+    lanes = (((1,), (1,)), ((), ()))
+    base = (f * 8 + me.t) * 1024
+
+    def head_rows(n):
+        at = pl.ds(pl.multiple_of(n * 128, 128), 128)
+        logits = lax.dot_general(vh[at], vf[...], lanes, preferred_element_type=F32)
+        vocab = lax.broadcasted_iota(jnp.int32, (128, 1024), 0) + (base + n * 128)
+        hit = jnp.where(vocab == tgt[...], 1.0, 0.0)
+        d = (tw[...] * (jnp.exp(logits - lse[...]) - hit)).astype(BF16)
+        gh[at] = jnp.dot(d, vf[...], preferred_element_type=F32) + jnp.dot(
+            vd[at], vo[...], preferred_element_type=F32
+        )
+        pltpu.make_async_copy(gh.at[at], grad_head.at[at], gsem.at[n]).start()
+
+    pl.loop(0, 4)(head_rows)
+    for copy in sent.values():
+        copy.wait_recv()
+    total = acc[b, a].astype(F32)
+    for m, i in sent:
+        total = total + rs[4 * m + i].astype(F32)
+    first, second = total[0:16], total[16:32]
+    own = jnp.where(p == 0, first, second)
+    give[...] = jnp.where(p == 0, second, first).astype(BF16)
+    swap = go.start(give, rp, me.partner())
+    pl.loop(4, 5)(head_rows)
+    swap.wait_recv()
+    d_final = own + rp[...].astype(F32)
+    middle = mid[...]
+    inv = lax.rsqrt(jnp.mean(middle * middle, axis=1, keepdims=True) + EPSILON)
+    scaled = d_final * gain[...]
+    inner = jnp.mean(middle * scaled, axis=1, keepdims=True)
+    dmid[c, b, a, p] = (inv * scaled - middle * inv * inv * inv * inner).astype(BF16)
+    block = dmid.at[c, b, a, p]
+    d1 = go.start(block, block, me.partner())
+    pl.loop(5, 6)(head_rows)
+    d1.wait_recv()
+    d2 = to_plane(go, me, dmid.at[c, b, a])
+    pl.loop(6, 8)(head_rows)
+    loads[4].wait()
+    loads[5].wait()
+    low = lax.broadcasted_iota(jnp.int32, (1024, 128), 1) < 64
+    h = vp[...]
+    s = jax.nn.sigmoid(h)
+    turned = pltpu.roll(h, 64, 1)
+    act = (h * s * turned).astype(BF16)[:, :64]
+    slope = turned * jnp.where(low, s * (1.0 + h * (1.0 - s)), pltpu.roll(s, 64, 1))
+    d3 = []
+    for k in (2, 1, 3, 0):
+        for i in range(4):
+            if k or i:
+                d2[k, i].wait_recv()
+        row = dmid.at[c, ring(b, 4 - k)]
+        d3.append(go.start(row, row, me.core()))
+    for copy in d3:
+        copy.wait_recv()
+    dm = dmid[...].reshape(1024, 1024)
+    twice = jnp.concatenate([down_w[...], down_w[...]], axis=0)
+    d_act = lax.dot_general(dm, twice, lanes, preferred_element_type=F32)
+    d_both = (d_act * slope).astype(BF16)
+    rows = (((0,), (0,)), ((), ()))
+    g_gu = lax.dot_general(d_both, vn[...], rows, preferred_element_type=F32)
+    g_dn = lax.dot_general(act, dm, rows, preferred_element_type=F32)
     for j in range(8):
-        s_gu[j] = (gu[j].astype(F32) + o_gu[j].astype(F32)).astype(BF16)
-        s_dn[j] = (dn[j].astype(F32) + o_dn[j].astype(F32)).astype(BF16)
-    sent = []
-    for o, dev in zip(others, to):
-        sent.append(go.start(s_gu.at[o], r_gu.at[me.f], dev))
-        sent.append(go.start(s_dn.at[o], r_dn.at[me.f], dev))
-    r_gu[me.f] = s_gu[me.f]
-    r_dn[me.f] = s_dn[me.f]
-    for copy in sent:
-        copy.wait_recv()
+        at = slice(128 * j, 128 * (j + 1))
+        comb[j % 2, j // 2, 0:128] = g_gu[:, at].astype(BF16)
+        comb[j % 2, j // 2, 128:192] = g_dn[:, at].astype(BF16)
+    swap = go.start(comb.at[1 - me.dp], oth, me.neighbour())
+    swap.wait_recv()
+    s4[...] = (comb[me.dp].astype(F32) + oth[...].astype(F32)).astype(BF16)
+
+    def homeward(i, side, to, src=0):
+        n = 2 * i + side
+        return pltpu.make_async_remote_copy(
+            src_ref=s4.at[ring(me.y, i)],
+            dst_ref=rg.at[src],
+            send_sem=hsend.at[n],
+            recv_sem=hrecv.at[src],
+            device_id=to,
+            device_id_type=MESH,
+        )
+
+    for i, side, to in homes:
+        if i == 0 and side == 0:
+            @pl.when(c != me.dp)
+            def _(to=to):
+                homeward(0, 0, to, f).start()
+
+            @pl.when(c == me.dp)
+            def _():
+                rg[f] = s4[me.y]
+        else:
+            homeward(i, side, to, f).start()
     for j in range(8):
-        both = r_gu[j].astype(F32)
-        gate[:, 64 * j : 64 * (j + 1)] = both[:, :64]
-        up[:, 64 * j : 64 * (j + 1)] = both[:, 64:]
-        down[64 * j : 64 * (j + 1)] = r_dn[j].astype(F32)
+        arrived = homeward(1, 0, homes[2][2], j)
+
+        @pl.when(jnp.logical_or(f != j, c != me.dp))
+        def _(arrived=arrived):
+            arrived.wait_recv()
+
+        got = rg[j].astype(F32)
+        gu = got[0:128].T
+        gate[:, 64 * j : 64 * (j + 1)] = gu[:, :64]
+        up[:, 64 * j : 64 * (j + 1)] = gu[:, 64:]
+        down[64 * j : 64 * (j + 1)] = got[128:192]
+    for i, side, to in homes:
+        if i == 0 and side == 0:
+            @pl.when(c != me.dp)
+            def _(to=to):
+                homeward(0, 0, to, f).wait_send()
+        else:
+            homeward(i, side, to, f).wait_send()
+    for n in range(8):
+        at = pl.ds(128 * n, 128)
+        pltpu.make_async_copy(gh.at[at], grad_head.at[at], gsem.at[n]).wait()
     go.drain()
 
 
-def home(gu, dn, collective_id):
+def backward(x, mid, gain, lse, tw, tgt, d_t, f_own, f_far, head, normed, pre, down_w):
     vmem = pl.BlockSpec(memory_space=pltpu.VMEM)
+    hbm = pl.BlockSpec(memory_space=pl.ANY)
+    shape = jax.ShapeDtypeStruct
+    big = pltpu.VMEM((1024, 1024), BF16)
     return pl.pallas_call(
-        home_body,
+        backward_body,
         out_shape=[
-            jax.ShapeDtypeStruct((128, 512), F32),
-            jax.ShapeDtypeStruct((128, 512), F32),
-            jax.ShapeDtypeStruct((512, 128), F32),
+            shape((1024, 1024), F32),
+            shape((128, 512), F32),
+            shape((128, 512), F32),
+            shape((512, 128), F32),
         ],
-        in_specs=[vmem] * 2,
-        out_specs=[vmem] * 3,
-        scratch_shapes=[pltpu.VMEM(gu.shape, BF16), pltpu.VMEM(dn.shape, BF16)] * 3
-        + [pltpu.SemaphoreType.DMA((16,)), pltpu.SemaphoreType.DMA((16,))],
+        in_specs=[vmem] * 6 + [hbm] * 6 + [vmem],
+        out_specs=[hbm] + [vmem] * 3,
+        scratch_shapes=[
+            big, big, big, big, big,
+            pltpu.VMEM((1024, 128), F32),
+            pltpu.VMEM((4, 128, 1024), BF16),
+            pltpu.VMEM((4, 4, 32, 1024), BF16),
+            pltpu.VMEM((16, 32, 1024), BF16),
+            pltpu.VMEM((16, 1024), BF16),
+            pltpu.VMEM((16, 1024), BF16),
+            pltpu.VMEM((2, 4, 4, 2, 16, 1024), BF16),
+            pltpu.VMEM((2, 4, 192, 128), BF16),
+            pltpu.VMEM((4, 192, 128), BF16),
+            pltpu.VMEM((4, 192, 128), BF16),
+            pltpu.VMEM((8, 192, 128), BF16),
+            pltpu.VMEM((1024, 1024), F32),
+            pltpu.SemaphoreType.DMA((50,)),
+            pltpu.SemaphoreType.DMA((50,)),
+            pltpu.SemaphoreType.DMA((8,)),
+            pltpu.SemaphoreType.DMA((8,)),
+            pltpu.SemaphoreType.DMA((6,)),
+            pltpu.SemaphoreType.DMA((8,)),
+        ],
         compiler_params=pltpu.CompilerParams(
-            collective_id=collective_id, has_side_effects=True
+            collective_id=5, has_side_effects=True, vmem_limit_bytes=56 * 2**20
         ),
-        name="home",
-    )(gu, dn)
-
-
-def rms_scale(values, gain_vec):
-    values = values.astype(F32)
-    return (
-        values * lax.rsqrt(jnp.mean(values * values, axis=-1, keepdims=True) + EPSILON) * gain_vec
-    )
+        name="backward",
+    )(x.reshape(2, 4, 128, 1024), mid, gain, lse, tw, tgt, d_t, f_own, f_far, head, normed, pre, down_w)
 
 
 def row_logits(row_block, head):
@@ -697,25 +643,11 @@
 
 
 def piece_stats(logits, part_targets, vocab_start):
-    vocab_cols = vocab_start + jnp.arange(logits.shape[1], dtype=jnp.int32)
-    high_val = jnp.max(logits, axis=1)
-    exp_total = jnp.sum(jnp.exp(logits - high_val[:, None]), axis=1)
-    picked = jnp.sum(jnp.where(vocab_cols[None, :] == part_targets[:, None], logits, 0.0), axis=1)
+    vocab_rows = vocab_start + jnp.arange(logits.shape[0], dtype=jnp.int32)
+    high_val = jnp.max(logits, axis=0)
+    exp_total = jnp.sum(jnp.exp(logits - high_val[None, :]), axis=0)
+    picked = jnp.sum(jnp.where(vocab_rows[:, None] == part_targets[None, :], logits, 0.0), axis=0)
     return (high_val, exp_total, picked)
-
-
-def norm_backward(mid_sum, gain_vec, d_out):
-    inv_rms = lax.rsqrt(jnp.mean(mid_sum * mid_sum, axis=1, keepdims=True) + EPSILON)
-    scaled_grad = d_out * gain_vec
-    inner_mean = jnp.mean(mid_sum * scaled_grad, axis=1, keepdims=True)
-    return (inv_rms * scaled_grad - mid_sum * inv_rms * inv_rms * inv_rms * inner_mean).astype(BF16)
-
-
-def gate_grads(d_act, gate_pre, up_pre):
-    sigmoid_g = jax.nn.sigmoid(gate_pre)
-    d_gate = (d_act * up_pre * sigmoid_g * (1.0 + gate_pre * (1.0 - sigmoid_g))).astype(BF16)
-    d_up = (d_act * gate_pre * sigmoid_g).astype(BF16)
-    return (d_gate, d_up)
 
 
 def local(
@@ -756,11 +688,9 @@
     group_targets = group_targets.reshape(2048)
     normed_in = normed_in.reshape(1024, 1024)
     pre = pre.reshape(1024, 128)
-    gate_pre, up_pre = pre[:, :64], pre[:, 64:]
-    hidden_act = (gate_pre * jax.nn.sigmoid(gate_pre) * up_pre).astype(BF16)
     final_own = final_own.reshape(1024, 1024)
-    logits_own = row_logits(final_own, proxy_head)
-    proxy_stats = piece_stats(logits_own, group_targets[:1024], vocab_start)
+    logits_t = row_logits(proxy_head, final_own)
+    proxy_stats = piece_stats(logits_t, group_targets[:1024], vocab_start)
     stats = jnp.concatenate([ref_stats.reshape(3, 8, 128), jnp.stack(proxy_stats).reshape(3, 8, 128)])
     stats = stats.reshape(6, 2, 4, 128).transpose(1, 0, 2, 3).reshape(2, 24, 128)
     lse, token_weight, log_weights, final_far = join_stats(
@@ -769,34 +699,26 @@
     final_far = final_far.reshape(1024, 1024)
     lse, token_weight = lse.reshape(2048), token_weight.reshape(2048)
     vocab_cols = vocab_start + jnp.arange(vocab_rows, dtype=jnp.int32)
-
-    def to_dlogits(logits, at):
-        onehot = (vocab_cols[None, :] == group_targets[at, None]).astype(F32)
-        share = jnp.exp(logits - lse[at, None]) - onehot
-        return (token_weight[at, None] * share).astype(BF16)
-
-    own, far = slice(0, 1024), slice(1024, 2048)
-    d_own = to_dlogits(logits_own, own)
-    d_part = jnp.dot(d_own, proxy_head, preferred_element_type=F32).astype(BF16)
-    d_final = scatter(d_part, 5)
-    d_far = to_dlogits(row_logits(final_far, proxy_head), far)
-    rows = (((0,), (0,)), ((), ()))
-    grad_head = lax.dot_general(d_own, final_own, rows, preferred_element_type=F32)
-    grad_head = grad_head + lax.dot_general(d_far, final_far, rows, preferred_element_type=F32)
-    d_mid = norm_backward(mid_sum, proxy_gain_out, d_final)
-    (d_mid,) = gather((d_mid,), (False,), (), 6)
-    d_mid = d_mid.reshape(1024, 1024)
-    grad_down = lax.dot_general(
-        hidden_act, d_mid, (((0,), (0,)), ((), ())), preferred_element_type=F32
+    hit = (vocab_cols[:, None] == group_targets[None, :1024]).astype(F32)
+    d_t = (token_weight[None, :1024] * (jnp.exp(logits_t - lse[None, :1024]) - hit)).astype(BF16)
+    d_part = lax.dot_general(
+        d_t, proxy_head, (((0,), (0,)), ((), ())), preferred_element_type=F32
+    ).astype(BF16)
+    grad_head, grad_gate, grad_up, grad_down = backward(
+        d_part,
+        mid_sum,
+        proxy_gain_out[None],
+        lse[None, 1024:],
+        token_weight[None, 1024:],
+        group_targets[None, 1024:],
+        d_t,
+        final_own,
+        final_far,
+        proxy_head,
+        normed_in,
+        pre,
+        down_w,
     )
-    d_act = lax.dot_general(d_mid, down_w, (((1,), (1,)), ((), ())), preferred_element_type=F32)
-    d_both = jnp.concatenate(gate_grads(d_act, gate_pre, up_pre), axis=1)
-    grad_gu = lax.dot_general(
-        normed_in, d_both, (((0,), (0,)), ((), ())), preferred_element_type=F32
-    )
-    grad_gu = grad_gu.astype(BF16).reshape(8, 128, 128)
-    grad_down = grad_down.astype(BF16).reshape(64, 8, 128).transpose(1, 0, 2)
-    grad_gate, grad_up, grad_down = home(grad_gu, grad_down, 7)
     return (log_weights[:, 0], grad_gate, grad_up, grad_down, grad_head)
 
 

time: 239 us -> 210 us (0.88)
  matrix products: 35.7 us -> 7.68 us
  Pallas kernels: 184 us -> 175 us
  local copies, waits for them, and re-layouts: 11 us -> 19.9 us
    dot_general x6 -> x1, matrix products: 29.7 us -> 3.71 us  [local(): lax.dot_general(d_t, proxy_head, (((0,), (0,)), ((), ())), preferred_elem...]
    pallas_call x3 -> x1, Pallas kernels: 69.6 us -> 60.8 us  [backward(): pl.pallas_call(backward_body, out_shape=[shape((1024, 1024), F32), shape(...]
    unnamed x29 -> x14, local copies, waits for them, and re-layouts: 3.56 us -> 11.8 us
    reduce_sum x2 -> x1, other arithmetic: 4.05 us -> 1.56 us  [piece_stats(): exp_total = jnp.sum(jnp.exp(logits - high_val[None, :]), axis=0)]
where the time goes in v3:
time: 210 us
  Pallas kernels  175 us (83%)
  local copies, waits for them, and re-layouts  19.9 us (9%)
  matrix products  7.68 us (4%)
  other arithmetic  6.03 us (3%)
    pallas_call x1, Pallas kernels, forward(): pl.pallas_call(forward_body, out_shape=[shape((2, 4, 4, 2, 16, 1024), BF1...  87.9 us
    pallas_call x1, Pallas kernels, backward(): pl.pallas_call(backward_body, out_shape=[shape((1024, 1024), F32), shape(...  60.8 us
    pallas_call x1, Pallas kernels, join_stats(): pl.pallas_call(stats_body, out_shape=[jax.ShapeDtypeStruct((16, 128), F32...  26.8 us
    unnamed x14, local copies, waits for them, and re-layouts  11.8 us

profile of v3, /device:TPU:1, one launch (start us, length us, event | category | flops | bytes accessed | tf_op | source)
XLA Modules:
  0.0 209.8 jit_solution(14969596039169148903)
XLA Ops:
  0.6 0.0 copy-start
  0.7 0.8 dynamic-slice_bitcast_fusion
  1.5 0.1 tile.10
  1.6 0.6 broadcast_select_fusion.ids
  2.2 0.6 constant_dynamic-slice_fusion.hid
  2.8 1.3 broadcast_in_dim.45.dw
  4.1 87.9 %forward.1 = (bf16[2,4,4,2,16,1024]{5,4,3,2,1,0:T(8,128)(2,1)}, f32[2,4,128,128]{3,2,1,0:T(8,128)}, bf16[2,4,4,2,16,1024]{5,4,3,2,1,0:T(8,128)(2,1)}, bf16[2,16,...) custom-call(s32[8,128]{1,0:T(8,128)} %broadcast_select_fusion.ids, ...), custom_call_target="tpu_custom_call" | custom-call | tf_op jit(solution)/shard_map/forward/pallas_call | solution.py:288
  92.1 1.3 slice_bitcast_fusion
  93.3 4.0 %fusion.9 = (f32[1024]{0:T(1024)S(1)}, f32[1024,1024]{0,1:T(8,128)S(1)}) fusion(bf16[1024,1024]{1,0:T(8,128)(2,1)} %bitcast.49, bf16[1024,1024]{1,0:T(8,128)(2,1)S(1)} %copy-done.3), kind=kOutput, calls=%fused_computation.26 | convolution fusion | flops 2148531200 | bytes 8392704 | tf_op jit(solution)/shard_map/dot_general | solution.py:642
  97.3 0.0 copy-start.1
  97.3 2.0 copy-done.1
  99.3 1.6 fusion.5
  100.9 0.6 pad_maximum_fusion
  101.5 26.8 %stats.1 = (f32[16,128]{1,0:T(8,128)}, f32[16,128]{1,0:T(8,128)}, f32[64,128]{1,0:T(8,128)}, bf16[2,4,4,2,16,1024]{5,4,3,2,1,0:T(8,128)(2,1)}) custom-call(f32[2,24,128]{2,1,0:T(8,128)} %bitcast.55, s32[16,128]{1,0:T(8,128)} %bitcast.67, f32[64,128]{1,0:T(8,128)} %broadcast_in_dim.45.dw, bf16[2,16,1024]{2,1,0:T(8,128)(2,1)} %get-tuple-element.26.fin_x), custom_call_target="tpu_custom_call" | custom-call | tf_op jit(solution)/shard_map/stats/pallas_call | solution.py:414
  128.3 1.4 slice_reduce_fusion
  129.7 1.3 fusion.7
  130.9 1.3 fusion.8
  132.2 3.2 %fusion.3.d_t = bf16[1024,1024]{1,0:T(8,128)(2,1)S(1)} fusion(f32[1024,1024]{0,1:T(8,128)} %copy-done.1, f32[1024]{0:T(1024)S(1)} %get-tuple-element.46, f32[1024]{0:T(1024)S(1)} %get-tuple-element.44, s32[1024]{0:T(1024)S(1)} %bitcast.57, s32[1024]{0:T(1024)S(1)} %iota_add_fusion), kind=kLoop, calls=%fused_computation.5 | loop fusion | flops 6291456 | bytes 6307840 | tf_op jit(solution)/shard_map/convert_element_type | solution.py:703
  135.5 3.7 %convolution_convert_fusion = bf16[1024,1024]{1,0:T(8,128)(2,1)} fusion(bf16[1024,1024]{1,0:T(8,128)(2,1)S(1)} %fusion.3.d_t, bf16[1024,1024]{1,0:T(8,128)(2,1)S(1)} %copy-done.3), kind=kOutput, calls=%fused_computation.11 | convolution fusion | flops 2148532224 | bytes 6291456 | tf_op jit(solution)/shard_map/dot_general | solution.py:704
  139.2 60.8 %backward.1 = (f32[1024,1024]{1,0:T(8,128)}, f32[128,512]{1,0:T(8,128)}, f32[128,512]{1,0:T(8,128)}, f32[512,128]{1,0:T(8,128)}) custom-call(bf16[2,4,128,1024]{3,2,1,0:T(8,128)(2,1)} %bitcast.52, f32[16,1024]{1,0:T(8,128)} %get-tuple-element.30.mid, f32[1,1024]{1,0:T(1,128)} %bitcast.59, f32[1,1024]{1,0:T(1,128)} %bitcast.61, f32[1,1024]{1,0:T(1,128)} %bitcast.60, ...), custom_call_target="tpu_custom_call" | custom-call | tf_op jit(solution)/shard_map/backward/pallas_call | solution.py:603
  200.0 1.7 copy.26
  201.6 1.7 copy.27
  203.3 1.7 copy.28
  205.0 4.8 %copy.29 = f32[1024,1024]{1,0:T(8,128)} copy(f32[1024,1024]{1,0:T(8,128)} %get-tuple-element.60) | data formatting | bytes 8388608
  (11 shorter events, 0.0 us)
Async XLA Ops:
  0.6 1.5 copy-start
  4.1 89.2 %copy-start.3 = (bf16[1024,1024]{1,0:T(8,128)(2,1)S(1)}, bf16[1024,1024]{1,0:T(8,128)(2,1)}, u32[]{:S(2)}) copy-start(bf16[1024,1024]{1,0:T(8,128)(2,1)} %head.3) | copy-start | bytes 6291460
  97.3 2.0 copy-start.1
  97.3 3.6 %copy-start.4 = (f32[3,8,1,128]{3,2,1,0:T(1,128)S(1)}, f32[3,8,1,128]{3,2,1,0:T(1,128)}, u32[]{:S(2)}) copy-start(f32[3,8,1,128]{3,2,1,0:T(1,128)} %get-tuple-element.22) | copy-start | bytes 36868
  135.5 3.7 %copy-start.2 = (bf16[1024,1024]{1,0:T(8,128)(2,1)}, bf16[1024,1024]{1,0:T(8,128)(2,1)S(1)}, u32[]{:S(2)}) copy-start(bf16[1024,1024]{1,0:T(8,128)(2,1)S(1)} %fusion.3.d_t) | copy-start | bytes 6291460

commit v4 on v3

--- a/solution.py
+++ b/solution.py
@@ -111,102 +111,80 @@
 
 def forward_body(
     ids, hid, gain_in, gain_out, refh, ref_gain, gate, up, down, head,
-    normed, pre, fin, fin_x, mid, ref_st, tgt, lang, dnw,
-    idsg, gus, guw, ref_all, headv, rhs, logit, x, r0, acc, rs, give, rp,
+    normed, pre, fin, fin_x, mid, ref_st, tl, dnw,
+    idsg, guw, ref_all, headv, rhs, logit, x, rs, give, rp,
     send, recv, local,
 ):
     me = Place()
     a, b, c, p, f = me.a, me.b, me.c, me.p, me.f
     go = Copies(send, recv)
     plane = [me.on_ab(ring(a, i), ring(b, k)) for k, i in OFFSETS]
-    x_peers = [me.partner(), me.neighbour(), me.opposite()]
     flips = [me.at(y=ring(me.y, k), c=1 - c) for k in range(4)]
-    greet(plane + x_peers + flips)
+    greet(plane + flips + [me.partner(), me.neighbour()])
     take_head = pltpu.make_async_copy(head, headv, local.at[0])
     take_head.start()
-    normed[c, b, a, p] = rms_rows(hid[...], gain_in[...]).astype(BF16)
-    idsg[c, b, a, 0, p] = ids[...]
-    s1 = [go.start(normed.at[c, b, a, p], normed.at[c, b, a, p], me.partner())]
-    for g, to in zip((0, 1, 1), x_peers):
-        s1.append(go.start(ids, idsg.at[c, b, a, g, p], to))
-    low = lax.broadcasted_iota(jnp.int32, (128, 128), 1) < 64
-    for i in range(4):
-        g = gate[:, 128 * i : 128 * (i + 1)].astype(F32)
-        u = up[:, 128 * i : 128 * (i + 1)].astype(F32)
-        gus[2 * i] = jnp.where(low, g, pltpu.roll(u, 64, 1)).astype(BF16)
-        gus[2 * i + 1] = jnp.where(low, pltpu.roll(g, 64, 1), u).astype(BF16)
+    normed[b, a] = rms_rows(hid[...], gain_in[...]).astype(BF16).reshape(2, 16, 1024)
+    s2 = to_plane(go, me, normed.at[b, a])
+    idsg[b, a] = ids[...]
+    s2_ids = to_plane(go, me, idsg.at[b, a])
     here = pl.ds(pl.multiple_of(f * 128, 128), 128)
     w_sent = []
-    for j in range(1, 8):
-        o = lax.rem(f + j, 8)
-        to = {"dp": me.dp, "fsdp": o, "tp": me.t}
-        w_sent.append(go.start(gus.at[o], guw.at[f], to))
-        w_sent.append(go.start(down.at[o], dnw.at[:, here], to))
-    guw[f] = gus[f]
-    dnw[:, here] = down[f]
+    for k in range(4):
+        yy = ring(me.y, k)
+        part = pl.ds(pl.multiple_of(yy * 128, 128), 128)
+        for cc in (c, 1 - c) if k else (1 - c,):
+            to = me.at(y=yy, c=cc)
+            w_sent.append(go.start(gate.at[:, part], guw.at[f, :, pl.ds(0, 128)], to))
+            w_sent.append(go.start(up.at[:, part], guw.at[f, :, pl.ds(128, 128)], to))
+            w_sent.append(go.start(down.at[part], dnw.at[:, here], to))
+    part = pl.ds(pl.multiple_of(me.y * 128, 128), 128)
+    guw[f, :, 0:128] = gate[:, part]
+    guw[f, :, 128:256] = up[:, part]
+    dnw[:, here] = down[part]
     ref_all[c, b, a, p] = rms_rows(refh[...], ref_gain[...]).astype(BF16)
     r1 = go.start(ref_all.at[c, b, a, p], ref_all.at[c, b, a, p], me.partner())
-    for copy in s1:
-        copy.wait_recv()
-    s2 = to_plane(go, me, normed.at[c, b, a])
-    s2_ids = to_plane(go, me, idsg.at[c, b, a])
+    for copy in w_sent:
+        copy.wait_recv()
+    rs_sent = {}
+    for n, k in enumerate((2, 1, 3, 0)):
+        for i in range(4):
+            if k or i:
+                s2[k, i].wait_recv()
+        m = (4 - k) % 4
+        bb = ring(b, m)
+        h = jnp.dot(
+            normed[bb].reshape(128, 1024), guw[...].reshape(1024, 256),
+            preferred_element_type=F32,
+        )
+        pre[bb] = h
+        g = h[:, :128]
+        h = (g * jax.nn.sigmoid(g) * h[:, 128:]).astype(BF16)
+        h = jnp.dot(h, dnw[...], preferred_element_type=F32).astype(BF16)
+        x[bb] = h.reshape(4, 32, 1024)
+        for i in range(4):
+            if m or i:
+                to = me.on_ab(ring(a, i), bb)
+                rs_sent[m, i] = go.start(x.at[bb, ring(a, i)], rs.at[4 * m + i], to)
     r1.wait_recv()
     unit = ref_all.at[c, b, a]
     r2 = [go.start(unit, unit, me.on_a(ring(a, k))) for k in (1, 3, 2)]
-    s3 = []
-    for k in (2, 1, 3, 0):
-        for i in range(4):
-            if k or i:
-                s2[k, i].wait_recv()
-        row = normed.at[c, ring(b, 4 - k)]
-        s3.append(go.start(row, row, me.core()))
     for copy in s2_ids.values():
         copy.wait_recv()
-    ids_across = go.start(idsg.at[c], idsg.at[c], me.core())
-    for copy in w_sent:
-        copy.wait_recv()
-
-    def ffn(cc, bb):
-        h = jnp.dot(
-            normed[cc, bb].reshape(128, 1024), guw[...].reshape(1024, 128),
-            preferred_element_type=F32,
-        )
-        pre[cc, bb] = h
-        h = (h * jax.nn.sigmoid(h) * pltpu.roll(h, 64, 1)).astype(BF16)[:, :64]
-        x[cc, bb] = jnp.dot(h, dnw[...], preferred_element_type=F32).astype(BF16)
-
-    across = []
-    for n, m in enumerate(ROWS):
-        s3[n].wait_recv()
-        bb = ring(a, m)
-        ffn(1 - c, bb)
-        across.append(go.start(x.at[1 - c, bb], r0.at[bb], me.core()))
-    rs_sent = {}
-    for n, m in enumerate(ROWS):
-        bb = ring(b, m)
-        ffn(c, bb)
-        across[n].wait_recv()
-        total = x[c, bb].astype(F32) + r0[bb].astype(F32)
-        acc[bb] = total.astype(BF16).reshape(acc.shape[1:])
-        for i in range(4):
-            if m or i:
-                to = me.on_ab(ring(a, i), bb)
-                rs_sent[m, i] = go.start(acc.at[bb, ring(a, i)], rs.at[4 * m + i], to)
-    for copy in r2:
-        copy.wait_recv()
+    for bb in range(4):
+        row = idsg[bb, 0] + idsg[bb, 1] + idsg[bb, 2] + idsg[bb, 3]
+        tl[0, 0, 4 * c + bb] = row[0:1]
+        tl[0, 1, 4 * c + bb] = row[1:2]
+    mine = pl.ds(4 * c, 4)
+    ids_across = [
+        go.start(tl.at[0, n, mine], tl.at[0, n, mine], me.core()) for n in range(2)
+    ]
+    for copy in r2 + ids_across:
+        copy.wait_recv()
+    ids_far = go.start(tl.at[0], tl.at[1], me.neighbour())
     right_b, left_b = me.on_b(ring(b, 1)), me.on_b(ring(b, 3))
     unit = ref_all.at[c, b]
     r3 = [go.start(unit, unit, right_b), go.start(unit, unit, left_b)]
     cross = {0: go.start(unit, unit, me.core())}
-    ids_across.wait_recv()
-    for g in range(2):
-        for cc in range(2):
-            for bb in range(4):
-                row = idsg[cc, bb, 0, g, 0]
-                for j in range(1, 8):
-                    row = row + idsg[cc, bb, j // 2, g, j % 2]
-                tgt[8 * g + 4 * cc + bb] = row[0:1]
-                lang[8 * g + 4 * cc + bb] = row[1:2]
     vocab = lax.broadcasted_iota(jnp.int32, (1024, 256), 0) + (f * 8 + me.t) * 1024
 
     def ref_rows(m):
@@ -223,7 +201,7 @@
 
         value = logit[...]
         high = jnp.max(value, axis=0, keepdims=True)
-        want = jnp.concatenate([tgt[4 * c + b_own], tgt[4 * (1 - c) + b_far]], axis=1)
+        want = jnp.concatenate([tl[0, 0, 4 * c + b_own], tl[0, 0, 4 * (1 - c) + b_far]], axis=1)
         picked = jnp.sum(jnp.where(vocab == want, value, 0.0), axis=0, keepdims=True)
         total = jnp.sum(jnp.exp(value - high), axis=0, keepdims=True)
         for s, got in enumerate((high, total, picked)):
@@ -231,26 +209,21 @@
             ref_st[s, 4 * (1 - c) + b_far] = got[:, 128:]
 
     take_head.wait()
+    for copy in rs_sent.values():
+        copy.wait_recv()
+    total = x[b, a].astype(F32)
+    for m, i in rs_sent:
+        total = total + rs[4 * m + i].astype(F32)
+    give[...] = total.astype(BF16)
+    swap = go.start(give, rp, me.partner())
     cross[0].wait_recv()
     ref_rows(0)
-    for copy in rs_sent.values():
-        copy.wait_recv()
-    total = acc[b, a].astype(F32)
-    for m, i in rs_sent:
-        total = total + rs[4 * m + i].astype(F32)
-    first, second = total[0:16], total[16:32]
-    own = jnp.where(p == 0, first, second)
-    give[...] = jnp.where(p == 0, second, first).astype(BF16)
-    swap = go.start(give, rp, me.partner())
     swap.wait_recv()
-    middle = hid[...].astype(F32) + (own + rp[...].astype(F32))
+    middle = hid[...].astype(F32) + (give[...].astype(F32) + rp[...].astype(F32))
     mid[...] = middle
-    fin[c, b, a, p] = rms_rows(middle, gain_out[...]).astype(BF16)
-    block = fin.at[c, b, a, p]
-    f1 = go.start(block, block, me.partner())
-    f_x = [go.start(block, fin_x.at[p], to) for to in x_peers[1:]]
-    f1.wait_recv()
+    fin[c, b, a] = rms_rows(middle, gain_out[...]).astype(BF16).reshape(2, 16, 1024)
     f2 = to_plane(go, me, fin.at[c, b, a])
+    f_x = go.start(fin.at[c, b, a], fin_x, me.neighbour())
     r3[0].wait_recv()
     half = ref_all.at[c, ring(b, 3), pl.ds(0, 2)]
     r4 = [go.start(half, half, right_b)]
@@ -277,7 +250,7 @@
     ref_rows(1)
     cross[2].wait_recv()
     ref_rows(2)
-    for copy in f3 + f_x:
+    for copy in f3 + [f_x, ids_far]:
         copy.wait_recv()
     go.drain()
 
@@ -288,32 +261,28 @@
     return pl.pallas_call(
         forward_body,
         out_shape=[
-            shape((2, 4, 4, 2, 16, 1024), BF16),
-            shape((2, 4, 128, 128), F32),
+            shape((4, 4, 2, 16, 1024), BF16),
+            shape((4, 128, 256), F32),
             shape((2, 4, 4, 2, 16, 1024), BF16),
             shape((2, 16, 1024), BF16),
-            shape((16, 1024), F32),
+            shape((32, 1024), F32),
             shape((3, 8, 1, 128), F32),
-            shape((16, 1, 128), jnp.int32),
-            shape((16, 1, 128), jnp.int32),
-            shape((64, 1024), BF16),
+            shape((2, 2, 8, 1, 128), jnp.int32),
+            shape((128, 1024), BF16),
         ],
         in_specs=[vmem] * 9 + [pl.BlockSpec(memory_space=pl.ANY)],
-        out_specs=[vmem] * 9,
+        out_specs=[vmem] * 8,
         scratch_shapes=[
-            pltpu.VMEM((2, 4, 4, 2, 2, 8, 128), jnp.int32),
-            pltpu.VMEM((8, 128, 128), BF16),
-            pltpu.VMEM((8, 128, 128), BF16),
+            pltpu.VMEM((4, 4, 8, 128), jnp.int32),
+            pltpu.VMEM((8, 128, 256), BF16),
             pltpu.VMEM((2, 4, 4, 2, 16, 4096), BF16),
             pltpu.VMEM((1024, 4096), BF16),
             pltpu.VMEM((256, 4096), BF16),
             pltpu.VMEM((1024, 256), F32),
-            pltpu.VMEM((2, 4, 128, 1024), BF16),
-            pltpu.VMEM((4, 128, 1024), BF16),
             pltpu.VMEM((4, 4, 32, 1024), BF16),
             pltpu.VMEM((16, 32, 1024), BF16),
-            pltpu.VMEM((16, 1024), BF16),
-            pltpu.VMEM((16, 1024), BF16),
+            pltpu.VMEM((32, 1024), BF16),
+            pltpu.VMEM((32, 1024), BF16),
             pltpu.SemaphoreType.DMA((110,)),
             pltpu.SemaphoreType.DMA((110,)),
             pltpu.SemaphoreType.DMA((1,)),
@@ -439,21 +408,15 @@
 def backward_body(
     x, mid, gain, lse, tw, tgt, d_t, f_own, f_far, head, normed, pre, down_w,
     grad_head, gate, up, down,
-    vd, vo, vf, vh, vn, vp, r0, acc, rs, give, rp, dmid, comb, oth, s4, rg, gh,
+    vd, vo, vf, vh, vn, vp, r0, acc, rs, give, rp, dmid, comb, oc, sc, ox, sx, rg, gh,
     send, recv, hsend, hrecv, local, gsem,
 ):
     me = Place()
     a, b, c, p, f = me.a, me.b, me.c, me.p, me.f
     go = Copies(send, recv)
     plane = [me.on_ab(ring(a, i), ring(b, k)) for k, i in OFFSETS]
-    homes = [
-        (i, side, {"dp": me.dp if side == 0 else 1 - me.dp, "fsdp": 2 * ring(me.y, i) + me.dp, "tp": me.t})
-        for i in range(4)
-        for side in range(2)
-    ]
-    flips = [me.at(y=ring(me.y, k), c=1 - c) for k in range(4)]
-    across_dp = [me.at(dp=1 - me.dp, y=ring(me.y, k), c=cc) for k in range(4) for cc in range(2)]
-    greet(plane + [me.partner()] + flips + across_dp)
+    across_dp = [me.at(dp=1 - me.dp, y=ring(me.y, k)) for k in range(4)]
+    greet(plane + [me.partner(), me.core()] + across_dp)
     loads = [
         pltpu.make_async_copy(src, dst, local.at[n])
         for n, (src, dst) in enumerate(
@@ -498,97 +461,92 @@
     total = acc[b, a].astype(F32)
     for m, i in sent:
         total = total + rs[4 * m + i].astype(F32)
-    first, second = total[0:16], total[16:32]
-    own = jnp.where(p == 0, first, second)
-    give[...] = jnp.where(p == 0, second, first).astype(BF16)
+    give[...] = total.astype(BF16)
     swap = go.start(give, rp, me.partner())
     pl.loop(4, 5)(head_rows)
     swap.wait_recv()
-    d_final = own + rp[...].astype(F32)
+    d_final = give[...].astype(F32) + rp[...].astype(F32)
     middle = mid[...]
     inv = lax.rsqrt(jnp.mean(middle * middle, axis=1, keepdims=True) + EPSILON)
     scaled = d_final * gain[...]
     inner = jnp.mean(middle * scaled, axis=1, keepdims=True)
-    dmid[c, b, a, p] = (inv * scaled - middle * inv * inv * inv * inner).astype(BF16)
-    block = dmid.at[c, b, a, p]
-    d1 = go.start(block, block, me.partner())
-    pl.loop(5, 6)(head_rows)
-    d1.wait_recv()
-    d2 = to_plane(go, me, dmid.at[c, b, a])
-    pl.loop(6, 8)(head_rows)
+    d_mid = (inv * scaled - middle * inv * inv * inv * inner).astype(BF16)
+    dmid[b, a] = d_mid.reshape(2, 16, 1024)
+    d2 = to_plane(go, me, dmid.at[b, a])
+    pl.loop(5, 8)(head_rows)
     loads[4].wait()
     loads[5].wait()
-    low = lax.broadcasted_iota(jnp.int32, (1024, 128), 1) < 64
-    h = vp[...]
-    s = jax.nn.sigmoid(h)
-    turned = pltpu.roll(h, 64, 1)
-    act = (h * s * turned).astype(BF16)[:, :64]
-    slope = turned * jnp.where(low, s * (1.0 + h * (1.0 - s)), pltpu.roll(s, 64, 1))
-    d3 = []
-    for k in (2, 1, 3, 0):
-        for i in range(4):
-            if k or i:
-                d2[k, i].wait_recv()
-        row = dmid.at[c, ring(b, 4 - k)]
-        d3.append(go.start(row, row, me.core()))
-    for copy in d3:
-        copy.wait_recv()
-    dm = dmid[...].reshape(1024, 1024)
-    twice = jnp.concatenate([down_w[...], down_w[...]], axis=0)
-    d_act = lax.dot_general(dm, twice, lanes, preferred_element_type=F32)
-    d_both = (d_act * slope).astype(BF16)
+    g, u = vp[:, :128], vp[:, 128:]
+    s = jax.nn.sigmoid(g)
+    act = (g * s * u).astype(BF16)
+    gate_slope = u * s * (1.0 + g * (1.0 - s))
+    up_slope = g * s
+    for copy in d2.values():
+        copy.wait_recv()
+    dm = dmid[...].reshape(512, 1024)
+    d_act = lax.dot_general(dm, down_w[...], lanes, preferred_element_type=F32)
     rows = (((0,), (0,)), ((), ()))
-    g_gu = lax.dot_general(d_both, vn[...], rows, preferred_element_type=F32)
-    g_dn = lax.dot_general(act, dm, rows, preferred_element_type=F32)
-    for j in range(8):
-        at = slice(128 * j, 128 * (j + 1))
-        comb[j % 2, j // 2, 0:128] = g_gu[:, at].astype(BF16)
-        comb[j % 2, j // 2, 128:192] = g_dn[:, at].astype(BF16)
-    swap = go.start(comb.at[1 - me.dp], oth, me.neighbour())
+    for n, (left, right) in enumerate(
+        (
+            ((d_act * gate_slope).astype(BF16), vn[...]),
+            ((d_act * up_slope).astype(BF16), vn[...]),
+            (act, dm),
+        )
+    ):
+        grad = lax.dot_general(left, right, rows, preferred_element_type=F32).astype(BF16)
+        for j in range(8):
+            comb[j % 2, j // 2 % 2, j // 4, 128 * n : 128 * (n + 1)] = grad[
+                :, 128 * j : 128 * (j + 1)
+            ]
+    swap = go.start(comb.at[1 - c], oc, me.core())
     swap.wait_recv()
-    s4[...] = (comb[me.dp].astype(F32) + oth[...].astype(F32)).astype(BF16)
-
-    def homeward(i, side, to, src=0):
-        n = 2 * i + side
+    sc[...] = (comb[c].astype(F32) + oc[...].astype(F32)).astype(BF16)
+    swap = go.start(sc.at[1 - me.dp], ox, me.neighbour())
+    swap.wait_recv()
+    sx[...] = (sc[me.dp].astype(F32) + ox[...].astype(F32)).astype(BF16)
+    half, odd = lax.div(me.y, 2), lax.rem(me.y, 2)
+
+    def homeward(e, side, src):
+        h = lax.rem(half + e, 2)
         return pltpu.make_async_remote_copy(
-            src_ref=s4.at[ring(me.y, i)],
+            src_ref=sx.at[h],
             dst_ref=rg.at[src],
-            send_sem=hsend.at[n],
+            send_sem=hsend.at[2 * e + side],
             recv_sem=hrecv.at[src],
-            device_id=to,
+            device_id=me.at(dp=1 - me.dp if side else me.dp, y=2 * h + me.dp),
             device_id_type=MESH,
         )
 
-    for i, side, to in homes:
-        if i == 0 and side == 0:
-            @pl.when(c != me.dp)
-            def _(to=to):
-                homeward(0, 0, to, f).start()
-
-            @pl.when(c == me.dp)
-            def _():
-                rg[f] = s4[me.y]
-        else:
-            homeward(i, side, to, f).start()
-    for j in range(8):
-        arrived = homeward(1, 0, homes[2][2], j)
-
-        @pl.when(jnp.logical_or(f != j, c != me.dp))
-        def _(arrived=arrived):
-            arrived.wait_recv()
-
+    stays = odd == me.dp
+    for e, side in ((1, 1), (1, 0), (0, 1)):
+        homeward(e, side, me.y).start()
+
+    @pl.when(jnp.logical_not(stays))
+    def _():
+        homeward(0, 0, me.y).start()
+
+    @pl.when(stays)
+    def _():
+        rg[me.y] = sx[half]
+
+    for j in range(4):
+
+        @pl.when(jnp.logical_or(me.y != j, jnp.logical_not(stays)))
+        def _(j=j):
+            homeward(1, 1, j).wait_recv()
+
+        at = slice(128 * j, 128 * (j + 1))
         got = rg[j].astype(F32)
-        gu = got[0:128].T
-        gate[:, 64 * j : 64 * (j + 1)] = gu[:, :64]
-        up[:, 64 * j : 64 * (j + 1)] = gu[:, 64:]
-        down[64 * j : 64 * (j + 1)] = got[128:192]
-    for i, side, to in homes:
-        if i == 0 and side == 0:
-            @pl.when(c != me.dp)
-            def _(to=to):
-                homeward(0, 0, to, f).wait_send()
-        else:
-            homeward(i, side, to, f).wait_send()
+        gate[:, at] = got[0:128].T
+        up[:, at] = got[128:256].T
+        down[at] = got[256:384]
+    for e, side in ((1, 1), (1, 0), (0, 1)):
+        homeward(e, side, me.y).wait_send()
+
+    @pl.when(jnp.logical_not(stays))
+    def _():
+        homeward(0, 0, me.y).wait_send()
+
     for n in range(8):
         at = pl.ds(128 * n, 128)
         pltpu.make_async_copy(gh.at[at], grad_head.at[at], gsem.at[n]).wait()
@@ -611,23 +569,26 @@
         in_specs=[vmem] * 6 + [hbm] * 6 + [vmem],
         out_specs=[hbm] + [vmem] * 3,
         scratch_shapes=[
-            big, big, big, big, big,
-            pltpu.VMEM((1024, 128), F32),
+            big, big, big, big,
+            pltpu.VMEM((512, 1024), BF16),
+            pltpu.VMEM((512, 256), F32),
             pltpu.VMEM((4, 128, 1024), BF16),
             pltpu.VMEM((4, 4, 32, 1024), BF16),
             pltpu.VMEM((16, 32, 1024), BF16),
-            pltpu.VMEM((16, 1024), BF16),
-            pltpu.VMEM((16, 1024), BF16),
-            pltpu.VMEM((2, 4, 4, 2, 16, 1024), BF16),
-            pltpu.VMEM((2, 4, 192, 128), BF16),
-            pltpu.VMEM((4, 192, 128), BF16),
-            pltpu.VMEM((4, 192, 128), BF16),
-            pltpu.VMEM((8, 192, 128), BF16),
+            pltpu.VMEM((32, 1024), BF16),
+            pltpu.VMEM((32, 1024), BF16),
+            pltpu.VMEM((4, 4, 2, 16, 1024), BF16),
+            pltpu.VMEM((2, 2, 2, 384, 128), BF16),
+            pltpu.VMEM((2, 2, 384, 128), BF16),
+            pltpu.VMEM((2, 2, 384, 128), BF16),
+            pltpu.VMEM((2, 384, 128), BF16),
+            pltpu.VMEM((2, 384, 128), BF16),
+            pltpu.VMEM((4, 384, 128), BF16),
             pltpu.VMEM((1024, 1024), F32),
             pltpu.SemaphoreType.DMA((50,)),
             pltpu.SemaphoreType.DMA((50,)),
-            pltpu.SemaphoreType.DMA((8,)),
-            pltpu.SemaphoreType.DMA((8,)),
+            pltpu.SemaphoreType.DMA((4,)),
+            pltpu.SemaphoreType.DMA((4,)),
             pltpu.SemaphoreType.DMA((6,)),
             pltpu.SemaphoreType.DMA((8,)),
         ],
@@ -668,33 +629,32 @@
     me = Place()
     vocab_rows = ref_head.shape[0]
     vocab_start = lax.axis_index(("fsdp", "tp")) * vocab_rows
-    mine = lambda v: lax.dynamic_slice_in_dim(v, me.t * 16, 16, 0)
-    hidden = mine(proxy_hidden)
-    ids = jnp.tile(jnp.stack([mine(targets), mine(languages)]), (4, 8))
+    mine = lambda v: lax.dynamic_slice_in_dim(v, me.z * 32, 32, 0)
+    ids = jnp.tile(jnp.stack([mine(targets), mine(languages)]), (4, 4))
     lanes = lax.broadcasted_iota(jnp.int32, (8, 128), 1)
-    ids = jnp.where(lax.div(lanes, 16) == me.a * 2 + me.p, ids, 0)
-    normed_in, pre, final_own, fin_x, mid_sum, ref_stats, group_targets, langs, down_w = forward(
+    ids = jnp.where(lax.div(lanes, 32) == me.a, ids, 0)
+    normed_in, pre, final_own, fin_x, mid_sum, ref_stats, ids, down_w = forward(
         ids,
-        hidden,
+        mine(proxy_hidden),
         proxy_gain_in[None],
         proxy_gain_out[None],
         ref_hidden,
         ref_gain[None],
         gate_weight,
         up_weight,
-        down_weight.reshape(8, 64, 128),
+        down_weight,
         ref_head,
     )
-    group_targets = group_targets.reshape(2048)
-    normed_in = normed_in.reshape(1024, 1024)
-    pre = pre.reshape(1024, 128)
+    group_targets, langs = ids[:, 0].reshape(2048), ids[:, 1].reshape(16, 128)
+    normed_in = normed_in.reshape(512, 1024)
+    pre = pre.reshape(512, 256)
     final_own = final_own.reshape(1024, 1024)
     logits_t = row_logits(proxy_head, final_own)
     proxy_stats = piece_stats(logits_t, group_targets[:1024], vocab_start)
     stats = jnp.concatenate([ref_stats.reshape(3, 8, 128), jnp.stack(proxy_stats).reshape(3, 8, 128)])
     stats = stats.reshape(6, 2, 4, 128).transpose(1, 0, 2, 3).reshape(2, 24, 128)
     lse, token_weight, log_weights, final_far = join_stats(
-        stats, langs.reshape(16, 128), domain_weights, fin_x
+        stats, langs, domain_weights, fin_x
     )
     final_far = final_far.reshape(1024, 1024)
     lse, token_weight = lse.reshape(2048), token_weight.reshape(2048)

time: 210 us -> 213 us (1.014)
    pallas_call x1, Pallas kernels: 87.9 us -> 93.9 us  [forward(): pl.pallas_call(forward_body, out_shape=[shape((4, 4, 2, 16, 1024), BF16),...]
    pallas_call x1, Pallas kernels: 60.8 us -> 56.1 us  [backward(): pl.pallas_call(backward_body, out_shape=[shape((1024, 1024), F32), shape(...]
where the time goes in v4:
time: 213 us; the launch traced here: 211 us
  Pallas kernels  175 us (82%)
  local copies, waits for them, and re-layouts  21.2 us (10%)
  matrix products  7.68 us (4%)
  other arithmetic  6.03 us (3%)
    pallas_call x1, Pallas kernels, forward(): pl.pallas_call(forward_body, out_shape=[shape((4, 4, 2, 16, 1024), BF16),...  93.9 us
    pallas_call x1, Pallas kernels, backward(): pl.pallas_call(backward_body, out_shape=[shape((1024, 1024), F32), shape(...  56.1 us
    pallas_call x1, Pallas kernels, join_stats(): pl.pallas_call(stats_body, out_shape=[jax.ShapeDtypeStruct((16, 128), F32...  25.4 us
    unnamed x14, local copies, waits for them, and re-layouts  11.8 us

profile of v4, /device:TPU:1, one launch (start us, length us, event | category | flops | bytes accessed | tf_op | source)
XLA Modules:
  0.0 211.1 jit_solution(6285725740238824994)
XLA Ops:
  0.6 0.0 copy-start
  0.7 0.8 dynamic-slice_bitcast_fusion
  1.5 0.1 tile.10
  1.6 0.6 broadcast_select_fusion.ids
  2.2 1.3 broadcast_in_dim.45.dw
  3.5 0.6 constant_dynamic-slice_fusion.hid
  4.2 93.9 %forward.1 = (bf16[4,4,2,16,1024]{4,3,2,1,0:T(8,128)(2,1)}, f32[4,128,256]{2,1,0:T(8,128)}, bf16[2,4,4,2,16,1024]{5,4,3,2,1,0:T(8,128)(2,1)}, bf16[2,16,1024]{2,...) custom-call(s32[8,128]{1,0:T(8,128)} %broadcast_select_fusion.ids, ...), custom_call_target="tpu_custom_call" | custom-call | tf_op jit(solution)/shard_map/forward/pallas_call | solution.py:261
  98.1 1.3 slice.35
  99.4 1.3 slice_bitcast_fusion
  100.6 4.0 %fusion.9 = (f32[1024]{0:T(1024)S(1)}, f32[1024,1024]{0,1:T(8,128)S(1)}) fusion(bf16[1024,1024]{1,0:T(8,128)(2,1)} %bitcast.45, bf16[1024,1024]{1,0:T(8,128)(2,1)S(1)} %copy-done.3), kind=kOutput, calls=%fused_computation.26 | convolution fusion | flops 2148531200 | bytes 8392704 | tf_op jit(solution)/shard_map/dot_general | solution.py:603
  104.6 2.0 copy-done.1
  106.6 1.6 fusion.5
  108.2 0.6 pad_maximum_fusion
  108.8 25.4 %stats.1 = (f32[16,128]{1,0:T(8,128)}, f32[16,128]{1,0:T(8,128)}, f32[64,128]{1,0:T(8,128)}, bf16[2,4,4,2,16,1024]{5,4,3,2,1,0:T(8,128)(2,1)}) custom-call(f32[2,24,128]{2,1,0:T(8,128)} %bitcast.51, s32[16,128]{1,0:T(8,128)} %bitcast.54, f32[64,128]{1,0:T(8,128)} %broadcast_in_dim.45.dw, bf16[2,16,1024]{2,1,0:T(8,128)(2,1)} %get-tuple-element.24.fin_x), custom_call_target="tpu_custom_call" | custom-call | tf_op jit(solution)/shard_map/stats/pallas_call | solution.py:383
  134.3 1.4 slice_reduce_fusion
  135.7 1.3 fusion.7
  136.9 1.3 fusion.8
  138.2 3.2 %fusion.3.d_t = bf16[1024,1024]{1,0:T(8,128)(2,1)S(1)} fusion(f32[1024,1024]{0,1:T(8,128)} %copy-done.1, f32[1024]{0:T(1024)S(1)} %get-tuple-element.44, f32[1024]{0:T(1024)S(1)} %get-tuple-element.42, s32[1024]{0:T(1024)S(1)} %bitcast.53, s32[1024]{0:T(1024)S(1)} %iota_add_fusion), kind=kLoop, calls=%fused_computation.5 | loop fusion | flops 6291456 | bytes 6307840 | tf_op jit(solution)/shard_map/convert_element_type | solution.py:663
  141.5 3.7 %convolution_convert_fusion = bf16[1024,1024]{1,0:T(8,128)(2,1)} fusion(bf16[1024,1024]{1,0:T(8,128)(2,1)S(1)} %fusion.3.d_t, bf16[1024,1024]{1,0:T(8,128)(2,1)S(1)} %copy-done.3), kind=kOutput, calls=%fused_computation.11 | convolution fusion | flops 2148532224 | bytes 6291456 | tf_op jit(solution)/shard_map/dot_general | solution.py:664
  145.2 56.1 %backward.1 = (f32[1024,1024]{1,0:T(8,128)}, f32[128,512]{1,0:T(8,128)}, f32[128,512]{1,0:T(8,128)}, f32[512,128]{1,0:T(8,128)}) custom-call(bf16[2,4,128,1024]{3,2,1,0:T(8,128)(2,1)} %bitcast.48, f32[32,1024]{1,0:T(8,128)} %get-tuple-element.28.mid, f32[1,1024]{1,0:T(1,128)} %bitcast.57, f32[1,1024]{1,0:T(1,128)} %bitcast.62, f32[1,1024]{1,0:T(1,128)} %bitcast.61, ...), custom_call_target="tpu_custom_call" | custom-call | tf_op jit(solution)/shard_map/backward/pallas_call | solution.py:561
  201.3 1.7 copy.26
  203.0 1.7 copy.27
  204.7 1.7 copy.28
  206.3 4.8 %copy.29 = f32[1024,1024]{1,0:T(8,128)} copy(f32[1024,1024]{1,0:T(8,128)} %get-tuple-element.58) | data formatting | bytes 8388608
  (12 shorter events, 0.0 us)
Async XLA Ops:
  0.6 2.9 %copy-start = (bf16[128,1024]{1,0:T(8,128)(2,1)S(1)}, bf16[128,1024]{1,0:T(8,128)(2,1)}, u32[]{:S(2)}) copy-start(bf16[128,1024]{1,0:T(8,128)(2,1)} %param.14) | copy-start | bytes 786436
  4.2 96.5 %copy-start.3 = (bf16[1024,1024]{1,0:T(8,128)(2,1)S(1)}, bf16[1024,1024]{1,0:T(8,128)(2,1)}, u32[]{:S(2)}) copy-start(bf16[1024,1024]{1,0:T(8,128)(2,1)} %head.3) | copy-start | bytes 6291460
  104.6 2.0 copy-start.1
  104.6 3.6 %copy-start.4 = (f32[3,8,1,128]{3,2,1,0:T(1,128)S(1)}, f32[3,8,1,128]{3,2,1,0:T(1,128)}, u32[]{:S(2)}) copy-start(f32[3,8,1,128]{3,2,1,0:T(1,128)} %get-tuple-element.21) | copy-start | bytes 36868
  141.4 3.7 %copy-start.2 = (bf16[1024,1024]{1,0:T(8,128)(2,1)}, bf16[1024,1024]{1,0:T(8,128)(2,1)S(1)}, u32[]{:S(2)}) copy-start(bf16[1024,1024]{1,0:T(8,128)(2,1)S(1)} %fusion.3.d_t) | copy-start | bytes 6291460

commit v5 on v4

v5 whole, which is shorter than its diff:
```python
import functools

import jax
import jax.numpy as jnp
from jax import lax
from jax.experimental import pallas as pl
from jax.experimental.pallas import tpu as pltpu
from jax.sharding import PartitionSpec as P

EPSILON = 1e-05
STEP_SIZE = 1.0
SMOOTHING = 0.001
LANGS = 64
MESH = pl.DeviceIdType.MESH
F32, BF16 = jnp.float32, jnp.bfloat16


class Place:
    def __init__(self):
        self.dp = lax.axis_index("dp")
        f, t = lax.axis_index("fsdp"), lax.axis_index("tp")
        self.f, self.t = f, t
        self.y, self.c = lax.div(f, 2), lax.rem(f, 2)
        self.z, self.xh = lax.div(t, 2), lax.rem(t, 2)
        self.p = self.xh
        c = self.c
        self.a = (1 - c) * self.y + c * self.z
        self.b = (1 - c) * self.z + c * self.y

    def at(self, dp=None, y=None, z=None, xh=None, c=None):
        pick = lambda new, old: old if new is None else new
        dp, y, z = pick(dp, self.dp), pick(y, self.y), pick(z, self.z)
        xh, c = pick(xh, self.xh), pick(c, self.c)
        return {"dp": dp, "fsdp": y * 2 + c, "tp": z * 2 + xh}

    def on_a(self, a):
        c = self.c
        return self.at(y=(1 - c) * a + c * self.y, z=(1 - c) * self.z + c * a)

    def on_b(self, b):
        c = self.c
        return self.at(y=(1 - c) * self.y + c * b, z=(1 - c) * b + c * self.z)

    def on_ab(self, a, b):
        c = self.c
        return self.at(y=(1 - c) * a + c * b, z=(1 - c) * b + c * a)

    def core(self):
        return self.at(c=1 - self.c)

    def partner(self):
        return self.at(xh=1 - self.xh)

    def neighbour(self):
        return self.at(dp=1 - self.dp)

    def opposite(self):
        return self.at(dp=1 - self.dp, xh=1 - self.xh)


class Copies:
    def __init__(self, send, recv):
        self.send, self.recv, self.n, self.all = send, recv, 0, []

    def start(self, src, dst, to):
        copy = pltpu.make_async_remote_copy(
            src_ref=src,
            dst_ref=dst,
            send_sem=self.send.at[self.n],
            recv_sem=self.recv.at[self.n],
            device_id=to,
            device_id_type=MESH,
        )
        copy.start()
        self.n += 1
        self.all.append(copy)
        return copy

    def drain(self):
        for copy in self.all:
            copy.wait_send()


def greet(peers):
    barrier = pltpu.get_barrier_semaphore()
    for peer in peers:
        pl.semaphore_signal(barrier, inc=1, device_id=peer, device_id_type=MESH)
    pl.semaphore_wait(barrier, len(peers))


def ring(i, k):
    return lax.rem(i + k, 4)


OFFSETS = [(k, i) for k in (2, 1, 3, 0) for i in range(4) if k or i]
ROWS = (2, 3, 1, 0)


def rms_rows(values, gain):
    values = values.astype(F32)
    return values * lax.rsqrt(jnp.mean(values * values, axis=-1, keepdims=True) + EPSILON) * gain


def to_plane(go, me, view):
    sent = {}
    for k, i in OFFSETS:
        to = me.on_ab(ring(me.a, i), ring(me.b, k))
        sent[k, i] = go.start(view, view, to)
    return sent


class Spread:
    def __init__(self, go, me, view):
        self.go, self.me, self.view = go, me, view
        own = view(me.b, me.a)
        self.near = {i: go.start(own, own, me.on_a(ring(me.a, i))) for i in (2, 1, 3)}
        self.along = {(k, 0): go.start(own, own, me.on_b(ring(me.b, k))) for k in (2, 1, 3)}

    def hand_on(self):
        me = self.me
        for i in (1, 3, 2):
            self.near[i].wait_recv()
            unit = self.view(me.b, ring(me.a, 4 - i))
            for k in (2, 1, 3):
                self.along[k, i] = self.go.start(unit, unit, me.on_b(ring(me.b, k)))

    def row(self, k):
        if k:
            for i in range(4):
                self.along[k, i].wait_recv()
        return ring(self.me.b, (4 - k) % 4)


class Collect:
    def __init__(self, go, me, rb, ra):
        self.go, self.me, self.rb, self.ra, self.sent = go, me, rb, ra, []

    def row(self, m, view):
        if m:
            self.sent.append(self.go.start(view, self.rb.at[m], self.me.on_b(ring(self.me.b, m))))

    def total(self, own, units):
        go, me = self.go, self.me
        for copy in self.sent:
            copy.wait_recv()
        row = own[...].astype(F32)
        for m in (1, 2, 3):
            row = row + self.rb[m].astype(F32)
        units[...] = row.astype(BF16)
        swaps = [
            go.start(units.at[ring(me.a, i)], self.ra.at[i], me.on_a(ring(me.a, i))) for i in (2, 1, 3)
        ]
        for copy in swaps:
            copy.wait_recv()
        total = units[me.a].astype(F32)
        for i in (1, 2, 3):
            total = total + self.ra[i].astype(F32)
        return total


def forward_body(
    ids, hid, gain_in, gain_out, refh, ref_gain, gate, up, down, head,
    normed, pre, fin, fin_x, mid, ref_st, tl, dnw,
    idsg, guw, ref_all, headv, rhs, logit, x, rb, ra, units, give, rp,
    send, recv, local,
):
    me = Place()
    a, b, c, p, f = me.a, me.b, me.c, me.p, me.f
    go = Copies(send, recv)
    rings = [me.on_a(ring(a, k)) for k in (1, 2, 3)] + [me.on_b(ring(b, k)) for k in (1, 2, 3)]
    greet(rings + [me.core(), me.partner(), me.neighbour()])
    take_head = pltpu.make_async_copy(head, headv, local.at[0])
    take_head.start()
    normed[b, a] = rms_rows(hid[...], gain_in[...]).astype(BF16).reshape(2, 16, 1024)
    s2 = Spread(go, me, lambda bb, aa: normed.at[bb, aa])
    idsg[b, a] = ids[...]
    s2_ids = Spread(go, me, lambda bb, aa: idsg.at[bb, aa])
    here = pl.ds(pl.multiple_of(f * 128, 128), 128)

    def weights(ff, to, y=None):
        lanes = pl.ds(pl.multiple_of(ff * 128, 128), 128)
        pieces = [guw.at[ff], dnw.at[:, lanes]]
        if y is None:
            return [go.start(v, v, to) for v in pieces]
        part = pl.ds(pl.multiple_of(y * 128, 128), 128)
        return [
            go.start(gate.at[:, part], guw.at[ff, :, pl.ds(0, 128)], to),
            go.start(up.at[:, part], guw.at[ff, :, pl.ds(128, 128)], to),
            go.start(down.at[part], pieces[1], to),
        ]

    w_sent = {k: weights(f, me.at(y=ring(me.y, k)), ring(me.y, k)) for k in (2, 1, 3)}
    w_core = weights(f, me.core(), me.y)
    part = pl.ds(pl.multiple_of(me.y * 128, 128), 128)
    guw[f, :, 0:128] = gate[:, part]
    guw[f, :, 128:256] = up[:, part]
    dnw[:, here] = down[part]
    ref_all[c, b, a, p] = rms_rows(refh[...], ref_gain[...]).astype(BF16)
    r1 = go.start(ref_all.at[c, b, a, p], ref_all.at[c, b, a, p], me.partner())
    s2.hand_on()
    s2_ids.hand_on()
    r1.wait_recv()
    unit = ref_all.at[c, b, a]
    r2 = [go.start(unit, unit, me.on_a(ring(a, k))) for k in (1, 3, 2)]
    for k in (1, 3, 2):
        for copy in w_sent[k]:
            copy.wait_recv()
        w_core += weights(2 * ring(me.y, 4 - k) + c, me.core())
    for copy in w_core:
        copy.wait_recv()
    collect = Collect(go, me, rb, ra)
    for k in (0, 1, 3, 2):
        bb = s2.row(k)
        h = jnp.dot(
            normed[bb].reshape(128, 1024), guw[...].reshape(1024, 256),
            preferred_element_type=F32,
        )
        pre[bb] = h
        g = h[:, :128]
        h = (g * jax.nn.sigmoid(g) * h[:, 128:]).astype(BF16)
        h = jnp.dot(h, dnw[...], preferred_element_type=F32).astype(BF16)
        x[bb] = h.reshape(4, 32, 1024)
        collect.row((4 - k) % 4, x.at[bb])
    for copy in r2:
        copy.wait_recv()
    right_b, left_b = me.on_b(ring(b, 1)), me.on_b(ring(b, 3))
    unit = ref_all.at[c, b]
    cross = {0: go.start(unit, unit, me.core())}
    r3 = [go.start(unit, unit, right_b), go.start(unit, unit, left_b)]
    for k in (1, 2, 3):
        s2_ids.row(k)
    for bb in range(4):
        row = idsg[bb, 0] + idsg[bb, 1] + idsg[bb, 2] + idsg[bb, 3]
        tl[0, 0, 4 * c + bb] = row[0:1]
        tl[0, 1, 4 * c + bb] = row[1:2]
    mine = pl.ds(4 * c, 4)
    ids_across = [
        go.start(tl.at[0, n, mine], tl.at[0, n, mine], me.core()) for n in range(2)
    ]
    for copy in ids_across:
        copy.wait_recv()
    ids_far = go.start(tl.at[0], tl.at[1], me.neighbour())
    vocab = lax.broadcasted_iota(jnp.int32, (1024, 256), 0) + (f * 8 + me.t) * 1024

    def ref_rows(m):
        b_own, b_far = ring(b, m), ring(a, m)
        rhs[0:128] = ref_all[c, b_own].reshape(128, 4096)
        rhs[128:256] = ref_all[1 - c, b_far].reshape(128, 4096)

        @pl.loop(0, 4)
        def _(n):
            at = pl.ds(pl.multiple_of(n * 256, 256), 256)
            logit[at] = lax.dot_general(
                headv[at], rhs[...], (((1,), (1,)), ((), ())), preferred_element_type=F32
            )

        value = logit[...]
        high = jnp.max(value, axis=0, keepdims=True)
        want = jnp.concatenate([tl[0, 0, 4 * c + b_own], tl[0, 0, 4 * (1 - c) + b_far]], axis=1)
        picked = jnp.sum(jnp.where(vocab == want, value, 0.0), axis=0, keepdims=True)
        total = jnp.sum(jnp.exp(value - high), axis=0, keepdims=True)
        for s, got in enumerate((high, total, picked)):
            ref_st[s, 4 * c + b_own] = got[:, :128]
            ref_st[s, 4 * (1 - c) + b_far] = got[:, 128:]

    take_head.wait()
    cross[0].wait_recv()
    ref_rows(0)
    give[...] = collect.total(x.at[b], units).astype(BF16)
    swap = go.start(give, rp, me.partner())
    swap.wait_recv()
    middle = hid[...].astype(F32) + (give[...].astype(F32) + rp[...].astype(F32))
    mid[...] = middle
    fin[c, b, a] = rms_rows(middle, gain_out[...]).astype(BF16).reshape(2, 16, 1024)
    f2 = Spread(go, me, lambda bb, aa: fin.at[c, bb, aa])
    f_x = go.start(fin.at[c, b, a], fin_x, me.neighbour())
    f2.hand_on()
    r3[0].wait_recv()
    half = ref_all.at[c, ring(b, 3), pl.ds(0, 2)]
    r4 = [go.start(half, half, right_b)]
    r3[1].wait_recv()
    half = ref_all.at[c, ring(b, 1), pl.ds(2, 2)]
    r4.append(go.start(half, half, left_b))
    for m in (3, 1):
        unit = ref_all.at[c, ring(b, m)]
        cross[m] = go.start(unit, unit, me.core())
    cross[3].wait_recv()
    ref_rows(3)
    f3 = []
    for k in (0, 1, 3, 2):
        row = fin.at[c, f2.row(k)]
        f3.append(go.start(row, row, me.core()))
    for copy in r4:
        copy.wait_recv()
    unit = ref_all.at[c, ring(b, 2)]
    cross[2] = go.start(unit, unit, me.core())
    cross[1].wait_recv()
    ref_rows(1)
    cross[2].wait_recv()
    ref_rows(2)
    for copy in f3 + [f_x, ids_far]:
        copy.wait_recv()
    go.drain()


def forward(ids, hid, gain_in, gain_out, refh, ref_gain, gate, up, down, head):
    vmem = pl.BlockSpec(memory_space=pltpu.VMEM)
    shape = jax.ShapeDtypeStruct
    return pl.pallas_call(
        forward_body,
        out_shape=[
            shape((4, 4, 2, 16, 1024), BF16),
            shape((4, 128, 256), F32),
            shape((2, 4, 4, 2, 16, 1024), BF16),
            shape((2, 16, 1024), BF16),
            shape((32, 1024), F32),
            shape((3, 8, 1, 128), F32),
            shape((2, 2, 8, 1, 128), jnp.int32),
            shape((128, 1024), BF16),
        ],
        in_specs=[vmem] * 9 + [pl.BlockSpec(memory_space=pl.ANY)],
        out_specs=[vmem] * 8,
        scratch_shapes=[
            pltpu.VMEM((4, 4, 8, 128), jnp.int32),
            pltpu.VMEM((8, 128, 256), BF16),
            pltpu.VMEM((2, 4, 4, 2, 16, 4096), BF16),
            pltpu.VMEM((1024, 4096), BF16),
            pltpu.VMEM((256, 4096), BF16),
            pltpu.VMEM((1024, 256), F32),
            pltpu.VMEM((4, 4, 32, 1024), BF16),
            pltpu.VMEM((4, 4, 32, 1024), BF16),
            pltpu.VMEM((4, 32, 1024), BF16),
            pltpu.VMEM((4, 32, 1024), BF16),
            pltpu.VMEM((32, 1024), BF16),
            pltpu.VMEM((32, 1024), BF16),
            pltpu.SemaphoreType.DMA((110,)),
            pltpu.SemaphoreType.DMA((110,)),
            pltpu.SemaphoreType.DMA((1,)),
        ],
        compiler_params=pltpu.CompilerParams(
            collective_id=1, has_side_effects=True, vmem_limit_bytes=60 * 2**20
        ),
        name="forward",
    )(ids, hid, gain_in, gain_out, refh, ref_gain, gate, up, down, head)


def join_all(pieces):
    out = []
    for base in (0, 12):
        high = functools.reduce(jnp.maximum, [s[base : base + 4] for s in pieces])
        total = pick = None
        for s in pieces:
            t = s[base + 4 : base + 8] * jnp.exp(s[base : base + 4] - high)
            k = s[base + 8 : base + 12]
            total, pick = (t, k) if total is None else (total + t, pick + k)
        out += [high, total, pick]
    return jnp.concatenate(out, axis=0)


def rest_body(
    ref_st, ids, dw, fin, fin_x, mid, gain, head, normed, pre, down_w,
    logw, grad_head, gate, up, down,
    vd, vo, vf, vh, vn, vp, lg, st, slot_c, slot_yz, slot_x, both, lse, tw, ls, lc,
    x, r0, acc, rb, ra, units, give, rp, dmid, comb, oc, sc, ox, sx, rg,
    send, recv, hsend, hrecv, local, gsem,
):
    me = Place()
    a, b, c, p, f = me.a, me.b, me.c, me.p, me.f
    go = Copies(send, recv)
    loads = [
        pltpu.make_async_copy(src, dst, local.at[n])
        for n, (src, dst) in enumerate(((head, vh), (fin, vo), (normed, vn), (pre, vp)))
    ]
    for load in loads:
        load.start()
    plane = [me.on_ab(ring(a, i), ring(b, k)) for k, i in OFFSETS]
    x_peers = [me.partner(), me.neighbour(), me.opposite()]
    across_dp = [me.at(dp=1 - me.dp, y=ring(me.y, k)) for k in (1, 2, 3)]
    greet(plane + x_peers + [me.core()] + across_dp)
    loads[0].wait()
    loads[1].wait()
    lanes = (((1,), (1,)), ((), ()))
    rows = (((0,), (0,)), ((), ()))
    base = (f * 8 + me.t) * 1024
    tile = lambda n: pl.ds(pl.multiple_of(n * 128, 128), 128)

    def line(v):
        return jnp.concatenate([v(r) for r in range(8)], axis=1)

    def own_rows(n, high):
        logits = lax.dot_general(vh[tile(n)], vo[...], lanes, preferred_element_type=F32)
        lg[tile(n)] = logits
        return jnp.maximum(high, jnp.max(logits, axis=0, keepdims=True))

    high = lax.fori_loop(0, 8, own_rows, jnp.full((1, 1024), -jnp.inf, F32))
    own_tgt = line(lambda r: ids[0, 0, r])

    def own_sums(n, carry):
        total, picked = carry
        logits = lg[tile(n)]
        vocab = lax.broadcasted_iota(jnp.int32, (128, 1024), 0) + (base + n * 128)
        total += jnp.sum(jnp.exp(logits - high), axis=0, keepdims=True)
        picked += jnp.sum(jnp.where(vocab == own_tgt, logits, 0.0), axis=0, keepdims=True)
        return total, picked

    zero = jnp.zeros((1, 1024), F32)
    total, picked = lax.fori_loop(0, 8, own_sums, (zero, zero))
    for r in range(8):
        h, q = r // 4, r % 4
        for s in range(3):
            st[h, 4 * s + q : 4 * s + q + 1] = ref_st[s, r]
        for s, v in enumerate((high, total, picked)):
            st[h, 12 + 4 * s + q : 13 + 4 * s + q] = v[:, 128 * r : 128 * (r + 1)]
    slot_c[c] = st[c]
    half = go.start(st.at[1 - c], slot_c.at[c], me.core())
    half.wait_recv()
    yz = me.y * 4 + me.z
    slot_yz[yz] = join_all([slot_c[0], slot_c[1]])
    sent = to_plane(go, me, slot_yz.at[yz])
    vf[c, b, a] = fin_x[...]
    beside = Spread(go, me, lambda bb, aa: vf.at[c, bb, aa])
    for copy in sent.values():
        copy.wait_recv()
    slot_x[0, p] = join_all([slot_yz[j] for j in range(16)])
    spread = [
        go.start(slot_x.at[0, p], slot_x.at[g, p], to) for g, to in zip((0, 1, 1), x_peers)
    ]
    beside.hand_on()
    for copy in spread:
        copy.wait_recv()
    both[c, 0] = join_all([slot_x[0, 0], slot_x[0, 1]])
    both[c, 1] = join_all([slot_x[1, 0], slot_x[1, 1]])
    share = go.start(both.at[c], both.at[c], me.core())
    share.wait_recv()
    excess = [None, None]
    for g in range(2):
        now = [
            jnp.concatenate([both[0, g, 4 * i : 4 * i + 4], both[1, g, 4 * i : 4 * i + 4]])
            for i in range(6)
        ]
        ref_loss = now[0] + jnp.log(now[1]) - now[2]
        proxy_lse = now[3] + jnp.log(now[4])
        lse[8 * g : 8 * g + 8] = proxy_lse
        excess[g] = jnp.maximum(proxy_lse - now[5] - ref_loss, 0.0)
    every = jnp.concatenate([ids[g, 1, r] for g in range(2) for r in range(8)], axis=0)
    for l in range(LANGS):
        here = every == l
        e = jnp.where(here[:8], excess[0], 0.0) + jnp.where(here[8:], excess[1], 0.0)
        n = jnp.where(here[:8], 1.0, 0.0) + jnp.where(here[8:], 1.0, 0.0)
        ls[l : l + 1] = jnp.sum(e, axis=0, keepdims=True)
        lc[l : l + 1] = jnp.sum(n, axis=0, keepdims=True)
    wide = lambda v: jnp.broadcast_to(jnp.sum(v[...], axis=1, keepdims=True), (LANGS, 128))
    count = jnp.maximum(wide(lc), 1.0)
    score = jnp.log(dw[...]) + STEP_SIZE * (wide(ls) / count)
    score = jnp.exp(score - jnp.max(score, axis=0, keepdims=True))
    mixture = score / jnp.sum(score, axis=0, keepdims=True)
    new = (1.0 - SMOOTHING) * mixture + SMOOTHING / LANGS
    logw[...] = jnp.log(new)
    per_token = new / count * 2048.0
    weight = jnp.zeros(every.shape, F32)
    for l in range(LANGS):
        weight = jnp.where(every == l, per_token[l : l + 1], weight)
    tw[...] = weight
    lse_own, tw_own = line(lambda r: lse[r : r + 1]), line(lambda r: tw[r : r + 1])

    @pl.loop(0, 8)
    def _(n):
        vocab = lax.broadcasted_iota(jnp.int32, (128, 1024), 0) + (base + n * 128)
        hit = jnp.where(vocab == own_tgt, 1.0, 0.0)
        vd[tile(n)] = (tw_own * (jnp.exp(lg[tile(n)] - lse_own) - hit)).astype(BF16)

    def d_rows(cc):
        at = pl.ds(pl.multiple_of(cc * 512, 512), 512)
        part = lax.dot_general(vd[:, at], vh[...], rows, preferred_element_type=F32)
        x[cc] = part.astype(BF16).reshape(4, 128, 1024)

    d_rows(1 - c)
    across = {}
    for m in ROWS:
        bb = ring(a, m)
        across[m] = go.start(x.at[1 - c, bb], r0.at[bb], me.core())
    d_rows(c)
    collect = Collect(go, me, rb, ra)
    for m in ROWS:
        bb = ring(b, m)
        across[m].wait_recv()
        joined = x[c, bb].astype(F32) + r0[bb].astype(F32)
        acc[bb] = joined.astype(BF16).reshape(acc.shape[1:])
        collect.row(m, acc.at[bb])
    far = []
    for k in (0, 1, 3, 2):
        row = vf.at[c, beside.row(k)]
        far.append(go.start(row, row, me.core()))
    for copy in far:
        copy.wait_recv()
    far_tgt = line(lambda r: ids[1, 0, r])

    def head_rows(n):
        at = tile(n)
        states = vf[...].reshape(1024, 1024)
        logits = lax.dot_general(vh[at], states, lanes, preferred_element_type=F32)
        vocab = lax.broadcasted_iota(jnp.int32, (128, 1024), 0) + (base + n * 128)
        hit = jnp.where(vocab == far_tgt, 1.0, 0.0)
        lse_far = line(lambda r: lse[8 + r : 9 + r])
        tw_far = line(lambda r: tw[8 + r : 9 + r])
        d = (tw_far * (jnp.exp(logits - lse_far) - hit)).astype(BF16)
        lg[at] = jnp.dot(d, states, preferred_element_type=F32) + jnp.dot(
            vd[at], vo[...], preferred_element_type=F32
        )
        pltpu.make_async_copy(lg.at[at], grad_head.at[at], gsem.at[n]).start()

    pl.loop(0, 4)(head_rows)
    give[...] = collect.total(acc.at[b], units).astype(BF16)
    swap = go.start(give, rp, me.partner())
    pl.loop(4, 6)(head_rows)
    swap.wait_recv()
    d_final = give[...].astype(F32) + rp[...].astype(F32)
    middle = mid[...]
    inv = lax.rsqrt(jnp.mean(middle * middle, axis=1, keepdims=True) + EPSILON)
    scaled = d_final * gain[...]
    inner = jnp.mean(middle * scaled, axis=1, keepdims=True)
    d_mid = (inv * scaled - middle * inv * inv * inv * inner).astype(BF16)
    dmid[b, a] = d_mid.reshape(2, 16, 1024)
    d2 = Spread(go, me, lambda bb, aa: dmid.at[bb, aa])
    pl.loop(6, 8)(head_rows)
    d2.hand_on()
    loads[2].wait()
    loads[3].wait()
    g, u = vp[:, :128], vp[:, 128:]
    s = jax.nn.sigmoid(g)
    act = (g * s * u).astype(BF16)
    gate_slope = u * s * (1.0 + g * (1.0 - s))
    up_slope = g * s
    for k in (1, 3, 2):
        d2.row(k)
    dm = dmid[...].reshape(512, 1024)
    d_act = lax.dot_general(dm, down_w[...], lanes, preferred_element_type=F32)
    for n, (left, right) in enumerate(
        (
            ((d_act * gate_slope).astype(BF16), vn[...]),
            ((d_act * up_slope).astype(BF16), vn[...]),
            (act, dm),
        )
    ):
        grad = lax.dot_general(left, right, rows, preferred_element_type=F32).astype(BF16)
        for j in range(8):
            comb[j % 2, j // 2 % 2, j // 4, 128 * n : 128 * (n + 1)] = grad[
                :, 128 * j : 128 * (j + 1)
            ]
    swap = go.start(comb.at[1 - c], oc, me.core())
    swap.wait_recv()
    sc[...] = (comb[c].astype(F32) + oc[...].astype(F32)).astype(BF16)
    swap = go.start(sc.at[1 - me.dp], ox, me.neighbour())
    swap.wait_recv()
    sx[...] = (sc[me.dp].astype(F32) + ox[...].astype(F32)).astype(BF16)
    half, odd = lax.div(me.y, 2), lax.rem(me.y, 2)

    def homeward(e, side, src):
        h = lax.rem(half + e, 2)
        return pltpu.make_async_remote_copy(
            src_ref=sx.at[h],
            dst_ref=rg.at[src],
            send_sem=hsend.at[2 * e + side],
            recv_sem=hrecv.at[src],
            device_id=me.at(dp=1 - me.dp if side else me.dp, y=2 * h + me.dp),
            device_id_type=MESH,
        )

    stays = odd == me.dp
    for e, side in ((1, 1), (1, 0), (0, 1)):
        homeward(e, side, me.y).start()

    @pl.when(jnp.logical_not(stays))
    def _():
        homeward(0, 0, me.y).start()

    @pl.when(stays)
    def _():
        rg[me.y] = sx[half]

    for j in range(4):

        @pl.when(jnp.logical_or(me.y != j, jnp.logical_not(stays)))
        def _(j=j):
            homeward(1, 1, j).wait_recv()

        at = slice(128 * j, 128 * (j + 1))
        got = rg[j].astype(F32)
        gate[:, at] = got[0:128].T
        up[:, at] = got[128:256].T
        down[at] = got[256:384]
    for e, side in ((1, 1), (1, 0), (0, 1)):
        homeward(e, side, me.y).wait_send()

    @pl.when(jnp.logical_not(stays))
    def _():
        homeward(0, 0, me.y).wait_send()

    for n in range(8):
        at = pl.ds(128 * n, 128)
        pltpu.make_async_copy(lg.at[at], grad_head.at[at], gsem.at[n]).wait()
    go.drain()


def rest(ref_st, ids, domain_weights, fin, fin_x, mid, gain, head, normed, pre, down_w):
    vmem = pl.BlockSpec(memory_space=pltpu.VMEM)
    hbm = pl.BlockSpec(memory_space=pl.ANY)
    shape = jax.ShapeDtypeStruct
    big = pltpu.VMEM((1024, 1024), BF16)
    return pl.pallas_call(
        rest_body,
        out_shape=[
            shape((LANGS, 128), F32),
            shape((1024, 1024), F32),
            shape((128, 512), F32),
            shape((128, 512), F32),
            shape((512, 128), F32),
        ],
        in_specs=[vmem] * 3 + [hbm] + [vmem] * 3 + [hbm] * 3 + [vmem],
        out_specs=[vmem, hbm] + [vmem] * 3,
        scratch_shapes=[
            big, big,
            pltpu.VMEM((2, 4, 4, 2, 16, 1024), BF16),
            big,
            pltpu.VMEM((512, 1024), BF16),
            pltpu.VMEM((512, 256), F32),
            pltpu.VMEM((1024, 1024), F32),
            pltpu.VMEM((2, 24, 128), F32),
            pltpu.VMEM((2, 24, 128), F32),
            pltpu.VMEM((16, 24, 128), F32),
            pltpu.VMEM((2, 2, 24, 128), F32),
            pltpu.VMEM((2, 2, 24, 128), F32),
            pltpu.VMEM((16, 128), F32),
            pltpu.VMEM((16, 128), F32),
            pltpu.VMEM((LANGS, 128), F32),
            pltpu.VMEM((LANGS, 128), F32),
            pltpu.VMEM((2, 4, 128, 1024), BF16),
            pltpu.VMEM((4, 128, 1024), BF16),
            pltpu.VMEM((4, 4, 32, 1024), BF16),
            pltpu.VMEM((4, 4, 32, 1024), BF16),
            pltpu.VMEM((4, 32, 1024), BF16),
            pltpu.VMEM((4, 32, 1024), BF16),
            pltpu.VMEM((32, 1024), BF16),
            pltpu.VMEM((32, 1024), BF16),
            pltpu.VMEM((4, 4, 2, 16, 1024), BF16),
            pltpu.VMEM((2, 2, 2, 384, 128), BF16),
            pltpu.VMEM((2, 2, 384, 128), BF16),
            pltpu.VMEM((2, 2, 384, 128), BF16),
            pltpu.VMEM((2, 384, 128), BF16),
            pltpu.VMEM((2, 384, 128), BF16),
            pltpu.VMEM((4, 384, 128), BF16),
            pltpu.SemaphoreType.DMA((90,)),
            pltpu.SemaphoreType.DMA((90,)),
            pltpu.SemaphoreType.DMA((4,)),
            pltpu.SemaphoreType.DMA((4,)),
            pltpu.SemaphoreType.DMA((4,)),
            pltpu.SemaphoreType.DMA((8,)),
        ],
        compiler_params=pltpu.CompilerParams(
            collective_id=5, has_side_effects=True, vmem_limit_bytes=44 * 2**20
        ),
        name="rest",
    )(
        ref_st, ids, jnp.broadcast_to(domain_weights[:, None], (LANGS, 128)), fin, fin_x,
        mid, gain, head, normed, pre, down_w,
    )


def local(
    ref_hidden,
    proxy_hidden,
    targets,
    languages,
    ref_gain,
    ref_head,
    proxy_gain_in,
    proxy_gain_out,
    gate_weight,
    up_weight,
    down_weight,
    proxy_head,
    domain_weights,
):
    me = Place()
    mine = lambda v: lax.dynamic_slice_in_dim(v, me.z * 32, 32, 0)
    ids = jnp.tile(jnp.stack([mine(targets), mine(languages)]), (4, 4))
    lanes = lax.broadcasted_iota(jnp.int32, (8, 128), 1)
    ids = jnp.where(lax.div(lanes, 32) == me.a, ids, 0)
    normed_in, pre, final_own, fin_x, mid_sum, ref_stats, ids, down_w = forward(
        ids,
        mine(proxy_hidden),
        proxy_gain_in[None],
        proxy_gain_out[None],
        ref_hidden,
        ref_gain[None],
        gate_weight,
        up_weight,
        down_weight,
        ref_head,
    )
    log_weights, grad_head, grad_gate, grad_up, grad_down = rest(
        ref_stats,
        ids,
        domain_weights,
        final_own.reshape(1024, 1024),
        fin_x,
        mid_sum,
        proxy_gain_out[None],
        proxy_head,
        normed_in.reshape(512, 1024),
        pre.reshape(512, 256),
        down_w,
    )
    return (log_weights[:, 0], grad_gate, grad_up, grad_down, grad_head)


def solution(mesh):
    in_specs = (
        P(("dp", "fsdp", "tp"), None),
        P(("dp", "fsdp"), None),
        P(("dp", "fsdp")),
        P(("dp", "fsdp")),
        P(),
        P(("fsdp", "tp"), None),
        P(),
        P(),
        P("fsdp", "tp"),
        P("fsdp", "tp"),
        P("tp", "fsdp"),
        P(("fsdp", "tp"), None),
        P(),
    )
    out_specs = (P(), P("fsdp", "tp"), P("fsdp", "tp"), P("tp", "fsdp"), P(("fsdp", "tp"), None))
    return jax.shard_map(local, mesh=mesh, in_specs=in_specs, out_specs=out_specs, check_vma=False)
```

time: 213 us -> 167 us (0.78)
  Pallas kernels: 175 us -> 147 us
  matrix products: 7.68 us -> 0 us
  other arithmetic: 6.03 us -> 0.62 us
  local copies, waits for them, and re-layouts: 21.2 us -> 17.7 us
    pallas_call x1, Pallas kernels: 93.9 us -> 73.2 us  [forward(): pl.pallas_call(forward_body, out_shape=[shape((4, 4, 2, 16, 1024), BF16),...]
    dot_general x2 -> x0, matrix products: 7.68 us -> none  [the longest x1 3.96 us: row_logits(): lax.dot_general(row_block, head, (((1,), (1,)), ((), ())), preferred_elem...]
    pallas_call x2 -> x1, Pallas kernels: 81.6 us -> 74 us  [rest(): pl.pallas_call(rest_body, out_shape=[shape((LANGS, 128), F32), shape((102...]
    slice x3 -> x0, local copies, waits for them, and re-layouts: 3.86 us -> none  [the longest x1 1.3 us: local(): group_targets, langs = (ids[:, 0].reshape(2048), ids[:, 1].reshape(16, 128))]
    convert_element_type x1 -> x0, other arithmetic: 3.24 us -> none  [local(): (token_weight[None, :1024] * (jnp.exp(logits_t - lse[None, :1024]) - hit)...]
    unnamed x14 -> x26, local copies, waits for them, and re-layouts: 11.8 us -> 14.9 us
where the time goes in v5:
time: 167 us; the launch traced here: 166 us
  Pallas kernels  147 us (88%)
  local copies, waits for them, and re-layouts  17.7 us (11%)
    pallas_call x1, Pallas kernels, rest(): pl.pallas_call(rest_body, out_shape=[shape((LANGS, 128), F32), shape((102...  74 us
    pallas_call x1, Pallas kernels, forward(): pl.pallas_call(forward_body, out_shape=[shape((4, 4, 2, 16, 1024), BF16),...  73.2 us
    unnamed x26, local copies, waits for them, and re-layouts  14.9 us

profile of v5, /device:TPU:1, one launch (start us, length us, event | category | flops | bytes accessed | tf_op | source)
XLA Modules:
  0.0 166.2 jit_solution(2963034807925142880)
XLA Ops:
  0.6 0.0 copy-start
  0.7 0.8 dynamic-slice_bitcast_fusion
  1.5 0.1 tile.10
  1.6 0.6 broadcast_select_fusion.ids
  2.2 0.7 broadcast_in_dim.24.dw
  2.9 0.0 copy-done
  2.9 0.6 constant_dynamic-slice_fusion.hid
  3.5 73.2 %forward.1 = (bf16[4,4,2,16,1024]{4,3,2,1,0:T(8,128)(2,1)}, f32[4,128,256]{2,1,0:T(8,128)}, bf16[2,4,4,2,16,1024]{5,4,3,2,1,0:T(8,128)(2,1)}, bf16[2,16,1024]{2,...) custom-call(s32[8,128]{1,0:T(8,128)} %broadcast_select_fusion.ids, ...), custom_call_target="tpu_custom_call" | custom-call | tf_op jit(solution)/shard_map/forward/pallas_call | solution.py:309
  76.7 0.0 copy-done.1
  76.7 0.0 copy-done.9
  76.8 1.6 copy-done.2
  78.3 1.2 copy-done.3
  79.6 1.0 copy-done.4
  80.6 0.9 copy-done.5
  81.6 0.9 copy-done.6
  82.5 0.8 copy-done.7
  83.3 0.7 copy-done.8
  84.0 0.7 copy-done.10
  84.7 74.0 %rest.1 = (f32[64,128]{1,0:T(8,128)S(1)}, f32[1024,1024]{1,0:T(8,128)}, f32[128,512]{1,0:T(8,128)S(1)}, f32[128,512]{1,0:T(8,128)S(1)}, f32[512,128]{1,0:T(8,128)S(1)}) custom-call(f32[3,8,1,128]{3,2,1,0:T(1,128)S(1)} %copy-done.10, s32[2,2,8,1,128]{4,3,2,1,0:T(1,128)S(1)} %copy-done.8, f32[64,128]{1,0:T(8,128)S(1)} %broadcast_in_dim.24.dw, ...), custom_call_target="tpu_custom_call" | custom-call | tf_op jit(solution)/shard_map/rest/pallas_call | solution.py:610
  158.7 0.6 slice_reduce_fusion
  159.3 0.7 copy.22
  160.0 0.7 copy.23
  160.7 0.7 copy.24
  161.4 4.8 %copy.25 = f32[1024,1024]{1,0:T(8,128)} copy(f32[1024,1024]{1,0:T(8,128)} %get-tuple-element.42) | data formatting | bytes 8388608
  (13 shorter events, 0.0 us)
Async XLA Ops:
  0.6 2.3 %copy-start = (bf16[128,1024]{1,0:T(8,128)(2,1)S(1)}, bf16[128,1024]{1,0:T(8,128)(2,1)}, u32[]{:S(2)}) copy-start(bf16[128,1024]{1,0:T(8,128)(2,1)} %param.14) | copy-start | bytes 786436
  3.5 73.2 %copy-start.1 = (bf16[1024,1024]{1,0:T(8,128)(2,1)S(1)}, bf16[1024,1024]{1,0:T(8,128)(2,1)}, u32[]{:S(2)}) copy-start(bf16[1024,1024]{1,0:T(8,128)(2,1)} %head.3) | copy-start | bytes 6291460
  3.5 73.2 %copy-start.9 = (f32[1024]{0:T(1024)S(1)}, f32[1024]{0:T(1024)}, u32[]{:S(2)}) copy-start(f32[1024]{0:T(1024)} %param.20) | copy-start | bytes 12292
  76.8 1.6 copy-start.2
  78.3 1.2 copy-start.3
  79.6 1.0 copy-start.4
  80.6 0.9 copy-start.5
  81.6 0.9 copy-start.6
  82.5 0.8 copy-start.7
  83.3 0.7 copy-start.8
  84.0 0.7 copy-start.10

commit v6 on v5

--- a/solution.py
+++ b/solution.py
@@ -11,6 +11,7 @@
 STEP_SIZE = 1.0
 SMOOTHING = 0.001
 LANGS = 64
+VMEM_LIMIT = 58
 MESH = pl.DeviceIdType.MESH
 F32, BF16 = jnp.float32, jnp.bfloat16
 
@@ -158,19 +159,40 @@
         return total
 
 
-def forward_body(
-    ids, hid, gain_in, gain_out, refh, ref_gain, gate, up, down, head,
+def join_all(pieces):
+    out = []
+    for base in (0, 12):
+        high = functools.reduce(jnp.maximum, [s[base : base + 4] for s in pieces])
+        total = pick = None
+        for s in pieces:
+            t = s[base + 4 : base + 8] * jnp.exp(s[base : base + 4] - high)
+            k = s[base + 8 : base + 12]
+            total, pick = (t, k) if total is None else (total + t, pick + k)
+        out += [high, total, pick]
+    return jnp.concatenate(out, axis=0)
+
+
+def step_body(
+    ids, hid, gain_in, gain_out, refh, ref_gain, gate, up, down, dw, head, proxy_head,
+    logw, grad_head, g_gate, g_up, g_down,
     normed, pre, fin, fin_x, mid, ref_st, tl, dnw,
     idsg, guw, ref_all, headv, rhs, logit, x, rb, ra, units, give, rp,
-    send, recv, local,
+    vf, vh, lg, st, slot_c, slot_yz, slot_x, both, lse, tw, ls, lc,
+    d_x, r0, acc, d_rb, d_ra, d_units, d_give, d_rp, dmid, comb, oc, sc, ox, sx, rg,
+    send, recv, hsend, hrecv, local,
 ):
     me = Place()
     a, b, c, p, f = me.a, me.b, me.c, me.p, me.f
     go = Copies(send, recv)
-    rings = [me.on_a(ring(a, k)) for k in (1, 2, 3)] + [me.on_b(ring(b, k)) for k in (1, 2, 3)]
-    greet(rings + [me.core(), me.partner(), me.neighbour()])
+    plane = [me.on_ab(ring(a, i), ring(b, k)) for k, i in OFFSETS]
+    x_peers = [me.partner(), me.neighbour(), me.opposite()]
+    across_dp = [me.at(dp=1 - me.dp, y=ring(me.y, k)) for k in (1, 2, 3)]
+    vd = headv.at[:, pl.ds(0, 1024)]
+    take_proxy = pltpu.make_async_copy(proxy_head, vh, local.at[1])
+    greet(plane + x_peers + [me.core()] + across_dp)
     take_head = pltpu.make_async_copy(head, headv, local.at[0])
     take_head.start()
+    take_proxy.start()
     normed[b, a] = rms_rows(hid[...], gain_in[...]).astype(BF16).reshape(2, 16, 1024)
     s2 = Spread(go, me, lambda bb, aa: normed.at[bb, aa])
     idsg[b, a] = ids[...]
@@ -290,95 +312,9 @@
     for k in (0, 1, 3, 2):
         row = fin.at[c, f2.row(k)]
         f3.append(go.start(row, row, me.core()))
-    for copy in r4:
-        copy.wait_recv()
-    unit = ref_all.at[c, ring(b, 2)]
-    cross[2] = go.start(unit, unit, me.core())
-    cross[1].wait_recv()
-    ref_rows(1)
-    cross[2].wait_recv()
-    ref_rows(2)
     for copy in f3 + [f_x, ids_far]:
         copy.wait_recv()
-    go.drain()
-
-
-def forward(ids, hid, gain_in, gain_out, refh, ref_gain, gate, up, down, head):
-    vmem = pl.BlockSpec(memory_space=pltpu.VMEM)
-    shape = jax.ShapeDtypeStruct
-    return pl.pallas_call(
-        forward_body,
-        out_shape=[
-            shape((4, 4, 2, 16, 1024), BF16),
-            shape((4, 128, 256), F32),
-            shape((2, 4, 4, 2, 16, 1024), BF16),
-            shape((2, 16, 1024), BF16),
-            shape((32, 1024), F32),
-            shape((3, 8, 1, 128), F32),
-            shape((2, 2, 8, 1, 128), jnp.int32),
-            shape((128, 1024), BF16),
-        ],
-        in_specs=[vmem] * 9 + [pl.BlockSpec(memory_space=pl.ANY)],
-        out_specs=[vmem] * 8,
-        scratch_shapes=[
-            pltpu.VMEM((4, 4, 8, 128), jnp.int32),
-            pltpu.VMEM((8, 128, 256), BF16),
-            pltpu.VMEM((2, 4, 4, 2, 16, 4096), BF16),
-            pltpu.VMEM((1024, 4096), BF16),
-            pltpu.VMEM((256, 4096), BF16),
-            pltpu.VMEM((1024, 256), F32),
-            pltpu.VMEM((4, 4, 32, 1024), BF16),
-            pltpu.VMEM((4, 4, 32, 1024), BF16),
-            pltpu.VMEM((4, 32, 1024), BF16),
-            pltpu.VMEM((4, 32, 1024), BF16),
-            pltpu.VMEM((32, 1024), BF16),
-            pltpu.VMEM((32, 1024), BF16),
-            pltpu.SemaphoreType.DMA((110,)),
-            pltpu.SemaphoreType.DMA((110,)),
-            pltpu.SemaphoreType.DMA((1,)),
-        ],
-        compiler_params=pltpu.CompilerParams(
-            collective_id=1, has_side_effects=True, vmem_limit_bytes=60 * 2**20
-        ),
-        name="forward",
-    )(ids, hid, gain_in, gain_out, refh, ref_gain, gate, up, down, head)
-
-
-def join_all(pieces):
-    out = []
-    for base in (0, 12):
-        high = functools.reduce(jnp.maximum, [s[base : base + 4] for s in pieces])
-        total = pick = None
-        for s in pieces:
-            t = s[base + 4 : base + 8] * jnp.exp(s[base : base + 4] - high)
-            k = s[base + 8 : base + 12]
-            total, pick = (t, k) if total is None else (total + t, pick + k)
-        out += [high, total, pick]
-    return jnp.concatenate(out, axis=0)
-
-
-def rest_body(
-    ref_st, ids, dw, fin, fin_x, mid, gain, head, normed, pre, down_w,
-    logw, grad_head, gate, up, down,
-    vd, vo, vf, vh, vn, vp, lg, st, slot_c, slot_yz, slot_x, both, lse, tw, ls, lc,
-    x, r0, acc, rb, ra, units, give, rp, dmid, comb, oc, sc, ox, sx, rg,
-    send, recv, hsend, hrecv, local, gsem,
-):
-    me = Place()
-    a, b, c, p, f = me.a, me.b, me.c, me.p, me.f
-    go = Copies(send, recv)
-    loads = [
-        pltpu.make_async_copy(src, dst, local.at[n])
-        for n, (src, dst) in enumerate(((head, vh), (fin, vo), (normed, vn), (pre, vp)))
-    ]
-    for load in loads:
-        load.start()
-    plane = [me.on_ab(ring(a, i), ring(b, k)) for k, i in OFFSETS]
-    x_peers = [me.partner(), me.neighbour(), me.opposite()]
-    across_dp = [me.at(dp=1 - me.dp, y=ring(me.y, k)) for k in (1, 2, 3)]
-    greet(plane + x_peers + [me.core()] + across_dp)
-    loads[0].wait()
-    loads[1].wait()
+    take_proxy.wait()
     lanes = (((1,), (1,)), ((), ()))
     rows = (((0,), (0,)), ((), ()))
     base = (f * 8 + me.t) * 1024
@@ -388,12 +324,16 @@
         return jnp.concatenate([v(r) for r in range(8)], axis=1)
 
     def own_rows(n, high):
-        logits = lax.dot_general(vh[tile(n)], vo[...], lanes, preferred_element_type=F32)
+        logits = lax.dot_general(vh[tile(n)], fin[...].reshape(1024, 1024), lanes, preferred_element_type=F32)
         lg[tile(n)] = logits
         return jnp.maximum(high, jnp.max(logits, axis=0, keepdims=True))
 
     high = lax.fori_loop(0, 8, own_rows, jnp.full((1, 1024), -jnp.inf, F32))
-    own_tgt = line(lambda r: ids[0, 0, r])
+    for copy in r4:
+        copy.wait_recv()
+    unit = ref_all.at[c, ring(b, 2)]
+    cross[2] = go.start(unit, unit, me.core())
+    own_tgt = line(lambda r: tl[0, 0, r])
 
     def own_sums(n, carry):
         total, picked = carry
@@ -405,6 +345,10 @@
 
     zero = jnp.zeros((1, 1024), F32)
     total, picked = lax.fori_loop(0, 8, own_sums, (zero, zero))
+    cross[1].wait_recv()
+    ref_rows(1)
+    cross[2].wait_recv()
+    ref_rows(2)
     for r in range(8):
         h, q = r // 4, r % 4
         for s in range(3):
@@ -442,7 +386,7 @@
         proxy_lse = now[3] + jnp.log(now[4])
         lse[8 * g : 8 * g + 8] = proxy_lse
         excess[g] = jnp.maximum(proxy_lse - now[5] - ref_loss, 0.0)
-    every = jnp.concatenate([ids[g, 1, r] for g in range(2) for r in range(8)], axis=0)
+    every = jnp.concatenate([tl[g, 1, r] for g in range(2) for r in range(8)], axis=0)
     for l in range(LANGS):
         here = every == l
         e = jnp.where(here[:8], excess[0], 0.0) + jnp.where(here[8:], excess[1], 0.0)
@@ -472,19 +416,19 @@
     def d_rows(cc):
         at = pl.ds(pl.multiple_of(cc * 512, 512), 512)
         part = lax.dot_general(vd[:, at], vh[...], rows, preferred_element_type=F32)
-        x[cc] = part.astype(BF16).reshape(4, 128, 1024)
+        d_x[cc] = part.astype(BF16).reshape(4, 128, 1024)
 
     d_rows(1 - c)
     across = {}
     for m in ROWS:
         bb = ring(a, m)
-        across[m] = go.start(x.at[1 - c, bb], r0.at[bb], me.core())
+        across[m] = go.start(d_x.at[1 - c, bb], r0.at[bb], me.core())
     d_rows(c)
-    collect = Collect(go, me, rb, ra)
+    collect = Collect(go, me, d_rb, d_ra)
     for m in ROWS:
         bb = ring(b, m)
         across[m].wait_recv()
-        joined = x[c, bb].astype(F32) + r0[bb].astype(F32)
+        joined = d_x[c, bb].astype(F32) + r0[bb].astype(F32)
         acc[bb] = joined.astype(BF16).reshape(acc.shape[1:])
         collect.row(m, acc.at[bb])
     far = []
@@ -493,7 +437,7 @@
         far.append(go.start(row, row, me.core()))
     for copy in far:
         copy.wait_recv()
-    far_tgt = line(lambda r: ids[1, 0, r])
+    far_tgt = line(lambda r: tl[1, 0, r])
 
     def head_rows(n):
         at = tile(n)
@@ -504,29 +448,27 @@
         lse_far = line(lambda r: lse[8 + r : 9 + r])
         tw_far = line(lambda r: tw[8 + r : 9 + r])
         d = (tw_far * (jnp.exp(logits - lse_far) - hit)).astype(BF16)
-        lg[at] = jnp.dot(d, states, preferred_element_type=F32) + jnp.dot(
-            vd[at], vo[...], preferred_element_type=F32
+        grad_head[at] = jnp.dot(d, states, preferred_element_type=F32) + jnp.dot(
+            vd[at], fin[...].reshape(1024, 1024), preferred_element_type=F32
         )
-        pltpu.make_async_copy(lg.at[at], grad_head.at[at], gsem.at[n]).start()
 
     pl.loop(0, 4)(head_rows)
-    give[...] = collect.total(acc.at[b], units).astype(BF16)
-    swap = go.start(give, rp, me.partner())
+    d_give[...] = collect.total(acc.at[b], d_units).astype(BF16)
+    swap = go.start(d_give, d_rp, me.partner())
     pl.loop(4, 6)(head_rows)
     swap.wait_recv()
-    d_final = give[...].astype(F32) + rp[...].astype(F32)
+    d_final = d_give[...].astype(F32) + d_rp[...].astype(F32)
     middle = mid[...]
     inv = lax.rsqrt(jnp.mean(middle * middle, axis=1, keepdims=True) + EPSILON)
-    scaled = d_final * gain[...]
+    scaled = d_final * gain_out[...]
     inner = jnp.mean(middle * scaled, axis=1, keepdims=True)
     d_mid = (inv * scaled - middle * inv * inv * inv * inner).astype(BF16)
     dmid[b, a] = d_mid.reshape(2, 16, 1024)
     d2 = Spread(go, me, lambda bb, aa: dmid.at[bb, aa])
     pl.loop(6, 8)(head_rows)
     d2.hand_on()
-    loads[2].wait()
-    loads[3].wait()
-    g, u = vp[:, :128], vp[:, 128:]
+    h = pre[...].reshape(512, 256)
+    g, u = h[:, :128], h[:, 128:]
     s = jax.nn.sigmoid(g)
     act = (g * s * u).astype(BF16)
     gate_slope = u * s * (1.0 + g * (1.0 - s))
@@ -534,11 +476,12 @@
     for k in (1, 3, 2):
         d2.row(k)
     dm = dmid[...].reshape(512, 1024)
-    d_act = lax.dot_general(dm, down_w[...], lanes, preferred_element_type=F32)
+    states_in = normed[...].reshape(512, 1024)
+    d_act = lax.dot_general(dm, dnw[...], lanes, preferred_element_type=F32)
     for n, (left, right) in enumerate(
         (
-            ((d_act * gate_slope).astype(BF16), vn[...]),
-            ((d_act * up_slope).astype(BF16), vn[...]),
+            ((d_act * gate_slope).astype(BF16), states_in),
+            ((d_act * up_slope).astype(BF16), states_in),
             (act, dm),
         )
     ):
@@ -586,9 +529,9 @@
 
         at = slice(128 * j, 128 * (j + 1))
         got = rg[j].astype(F32)
-        gate[:, at] = got[0:128].T
-        up[:, at] = got[128:256].T
-        down[at] = got[256:384]
+        g_gate[:, at] = got[0:128].T
+        g_up[:, at] = got[128:256].T
+        g_down[at] = got[256:384]
     for e, side in ((1, 1), (1, 0), (0, 1)):
         homeward(e, side, me.y).wait_send()
 
@@ -596,19 +539,18 @@
     def _():
         homeward(0, 0, me.y).wait_send()
 
-    for n in range(8):
-        at = pl.ds(128 * n, 128)
-        pltpu.make_async_copy(lg.at[at], grad_head.at[at], gsem.at[n]).wait()
     go.drain()
 
 
-def rest(ref_st, ids, domain_weights, fin, fin_x, mid, gain, head, normed, pre, down_w):
+def step(ids, hid, gain_in, gain_out, refh, ref_gain, gate, up, down, domain_weights, head, proxy_head):
     vmem = pl.BlockSpec(memory_space=pltpu.VMEM)
     hbm = pl.BlockSpec(memory_space=pl.ANY)
     shape = jax.ShapeDtypeStruct
-    big = pltpu.VMEM((1024, 1024), BF16)
+    half = lambda *s: pltpu.VMEM(s, BF16)
+    full = lambda *s: pltpu.VMEM(s, F32)
+    ints = lambda *s: pltpu.VMEM(s, jnp.int32)
     return pl.pallas_call(
-        rest_body,
+        step_body,
         out_shape=[
             shape((LANGS, 128), F32),
             shape((1024, 1024), F32),
@@ -616,53 +558,69 @@
             shape((128, 512), F32),
             shape((512, 128), F32),
         ],
-        in_specs=[vmem] * 3 + [hbm] + [vmem] * 3 + [hbm] * 3 + [vmem],
-        out_specs=[vmem, hbm] + [vmem] * 3,
+        in_specs=[vmem] * 10 + [hbm] * 2,
+        out_specs=[vmem] * 5,
         scratch_shapes=[
-            big, big,
-            pltpu.VMEM((2, 4, 4, 2, 16, 1024), BF16),
-            big,
-            pltpu.VMEM((512, 1024), BF16),
-            pltpu.VMEM((512, 256), F32),
-            pltpu.VMEM((1024, 1024), F32),
-            pltpu.VMEM((2, 24, 128), F32),
-            pltpu.VMEM((2, 24, 128), F32),
-            pltpu.VMEM((16, 24, 128), F32),
-            pltpu.VMEM((2, 2, 24, 128), F32),
-            pltpu.VMEM((2, 2, 24, 128), F32),
-            pltpu.VMEM((16, 128), F32),
-            pltpu.VMEM((16, 128), F32),
-            pltpu.VMEM((LANGS, 128), F32),
-            pltpu.VMEM((LANGS, 128), F32),
-            pltpu.VMEM((2, 4, 128, 1024), BF16),
-            pltpu.VMEM((4, 128, 1024), BF16),
-            pltpu.VMEM((4, 4, 32, 1024), BF16),
-            pltpu.VMEM((4, 4, 32, 1024), BF16),
-            pltpu.VMEM((4, 32, 1024), BF16),
-            pltpu.VMEM((4, 32, 1024), BF16),
-            pltpu.VMEM((32, 1024), BF16),
-            pltpu.VMEM((32, 1024), BF16),
-            pltpu.VMEM((4, 4, 2, 16, 1024), BF16),
-            pltpu.VMEM((2, 2, 2, 384, 128), BF16),
-            pltpu.VMEM((2, 2, 384, 128), BF16),
-            pltpu.VMEM((2, 2, 384, 128), BF16),
-            pltpu.VMEM((2, 384, 128), BF16),
-            pltpu.VMEM((2, 384, 128), BF16),
-            pltpu.VMEM((4, 384, 128), BF16),
-            pltpu.SemaphoreType.DMA((90,)),
-            pltpu.SemaphoreType.DMA((90,)),
+            half(4, 4, 2, 16, 1024),
+            full(4, 128, 256),
+            half(2, 4, 4, 2, 16, 1024),
+            half(2, 16, 1024),
+            full(32, 1024),
+            full(3, 8, 1, 128),
+            ints(2, 2, 8, 1, 128),
+            half(128, 1024),
+            ints(4, 4, 8, 128),
+            half(8, 128, 256),
+            half(2, 4, 4, 2, 16, 4096),
+            half(1024, 4096),
+            half(256, 4096),
+            full(1024, 256),
+            half(4, 4, 32, 1024),
+            half(4, 4, 32, 1024),
+            half(4, 32, 1024),
+            half(4, 32, 1024),
+            half(32, 1024),
+            half(32, 1024),
+            half(2, 4, 4, 2, 16, 1024),
+            half(1024, 1024),
+            full(1024, 1024),
+            full(2, 24, 128),
+            full(2, 24, 128),
+            full(16, 24, 128),
+            full(2, 2, 24, 128),
+            full(2, 2, 24, 128),
+            full(16, 128),
+            full(16, 128),
+            full(LANGS, 128),
+            full(LANGS, 128),
+            half(2, 4, 128, 1024),
+            half(4, 128, 1024),
+            half(4, 4, 32, 1024),
+            half(4, 4, 32, 1024),
+            half(4, 32, 1024),
+            half(4, 32, 1024),
+            half(32, 1024),
+            half(32, 1024),
+            half(4, 4, 2, 16, 1024),
+            half(2, 2, 2, 384, 128),
+            half(2, 2, 384, 128),
+            half(2, 2, 384, 128),
+            half(2, 384, 128),
+            half(2, 384, 128),
+            half(4, 384, 128),
+            pltpu.SemaphoreType.DMA((200,)),
+            pltpu.SemaphoreType.DMA((200,)),
             pltpu.SemaphoreType.DMA((4,)),
             pltpu.SemaphoreType.DMA((4,)),
-            pltpu.SemaphoreType.DMA((4,)),
-            pltpu.SemaphoreType.DMA((8,)),
+            pltpu.SemaphoreType.DMA((2,)),
         ],
         compiler_params=pltpu.CompilerParams(
-            collective_id=5, has_side_effects=True, vmem_limit_bytes=44 * 2**20
+            collective_id=1, has_side_effects=True, vmem_limit_bytes=VMEM_LIMIT * 2**20
         ),
-        name="rest",
+        name="step",
     )(
-        ref_st, ids, jnp.broadcast_to(domain_weights[:, None], (LANGS, 128)), fin, fin_x,
-        mid, gain, head, normed, pre, down_w,
+        ids, hid, gain_in, gain_out, refh, ref_gain, gate, up, down,
+        jnp.broadcast_to(domain_weights[:, None], (LANGS, 128)), head, proxy_head,
     )
 
 
@@ -686,7 +644,7 @@
     ids = jnp.tile(jnp.stack([mine(targets), mine(languages)]), (4, 4))
     lanes = lax.broadcasted_iota(jnp.int32, (8, 128), 1)
     ids = jnp.where(lax.div(lanes, 32) == me.a, ids, 0)
-    normed_in, pre, final_own, fin_x, mid_sum, ref_stats, ids, down_w = forward(
+    log_weights, grad_head, grad_gate, grad_up, grad_down = step(
         ids,
         mine(proxy_hidden),
         proxy_gain_in[None],
@@ -696,20 +654,9 @@
         gate_weight,
         up_weight,
         down_weight,
+        domain_weights,
         ref_head,
-    )
-    log_weights, grad_head, grad_gate, grad_up, grad_down = rest(
-        ref_stats,
-        ids,
-        domain_weights,
-        final_own.reshape(1024, 1024),
-        fin_x,
-        mid_sum,
-        proxy_gain_out[None],
         proxy_head,
-        normed_in.reshape(512, 1024),
-        pre.reshape(512, 256),
-        down_w,
     )
     return (log_weights[:, 0], grad_gate, grad_up, grad_down, grad_head)
 

time: 167 us -> 155 us (0.928)
  Pallas kernels: 147 us -> 140 us
  local copies, waits for them, and re-layouts: 17.7 us -> 14 us
    pallas_call x2 -> x1, Pallas kernels: 147 us -> 140 us  [step(): pl.pallas_call(step_body, out_shape=[shape((LANGS, 128), F32), shape((102...]
    unnamed x26 -> x6, local copies, waits for them, and re-layouts: 14.9 us -> 9.8 us
where the time goes in v6:
time: 155 us
  Pallas kernels  140 us (90%)
  local copies, waits for them, and re-layouts  14 us (9%)
    pallas_call x1, Pallas kernels, step(): pl.pallas_call(step_body, out_shape=[shape((LANGS, 128), F32), shape((102...  140 us
    unnamed x6, local copies, waits for them, and re-layouts  9.8 us

profile of v6, /device:TPU:1, one launch (start us, length us, event | category | flops | bytes accessed | tf_op | source)
XLA Modules:
  0.0 155.0 jit_solution(1806750904367867261)
XLA Ops:
  0.6 0.0 copy-start
  0.7 0.8 dynamic-slice_bitcast_fusion
  1.5 0.1 tile.10
  1.6 0.6 broadcast_select_fusion.ids
  2.2 1.3 broadcast_in_dim.23.dw
  3.5 0.0 copy-done
  3.5 0.6 constant_dynamic-slice_fusion.hid
  4.1 139.6 %step.1 = (f32[64,128]{1,0:T(8,128)}, f32[1024,1024]{1,0:T(8,128)}, f32[128,512]{1,0:T(8,128)}, f32[128,512]{1,0:T(8,128)}, f32[512,128]{1,0:T(8,128)}) custom-call(s32[8,128]{1,0:T(8,128)} %broadcast_select_fusion.ids, bf16[32,1024]{1,0:T(8,128)(2,1)} %constant_dynamic-slice_fusion.hid, f32[1,1024]{1,0:T(1,128)} %bitcast.8, f32[1,1024]{1,0:T(1,128)} %bitcast.9, ...), custom_call_target="tpu_custom_call" | custom-call | tf_op jit(solution)/shard_map/step/pallas_call | solution.py:552
  143.8 1.4 slice_reduce_fusion
  145.2 1.7 %copy.22 = f32[128,512]{1,0:T(8,128)} copy(f32[128,512]{1,0:T(8,128)} %get-tuple-element.23) | data formatting | bytes 524288
  146.8 1.7 %copy.23 = f32[128,512]{1,0:T(8,128)} copy(f32[128,512]{1,0:T(8,128)} %get-tuple-element.24) | data formatting | bytes 524288
  148.5 1.7 %copy.24 = f32[512,128]{1,0:T(8,128)} copy(f32[512,128]{1,0:T(8,128)} %get-tuple-element.25) | data formatting | bytes 524288
  150.2 4.8 %copy.25 = f32[1024,1024]{1,0:T(8,128)} copy(f32[1024,1024]{1,0:T(8,128)} %get-tuple-element.26) | data formatting | bytes 8388608
  (3 shorter events, 0.0 us)
Async XLA Ops:
  0.6 2.9 %copy-start = (bf16[128,1024]{1,0:T(8,128)(2,1)S(1)}, bf16[128,1024]{1,0:T(8,128)(2,1)}, u32[]{:S(2)}) copy-start(bf16[128,1024]{1,0:T(8,128)(2,1)} %param.14) | copy-start | bytes 786436

commit v7 on v6

--- a/solution.py
+++ b/solution.py
@@ -140,7 +140,7 @@
         if m:
             self.sent.append(self.go.start(view, self.rb.at[m], self.me.on_b(ring(self.me.b, m))))
 
-    def total(self, own, units):
+    def turn(self, own, units):
         go, me = self.go, self.me
         for copy in self.sent:
             copy.wait_recv()
@@ -148,12 +148,14 @@
         for m in (1, 2, 3):
             row = row + self.rb[m].astype(F32)
         units[...] = row.astype(BF16)
-        swaps = [
+        self.swaps = [
             go.start(units.at[ring(me.a, i)], self.ra.at[i], me.on_a(ring(me.a, i))) for i in (2, 1, 3)
         ]
-        for copy in swaps:
+
+    def total(self, units):
+        for copy in self.swaps:
             copy.wait_recv()
-        total = units[me.a].astype(F32)
+        total = units[self.me.a].astype(F32)
         for i in (1, 2, 3):
             total = total + self.ra[i].astype(F32)
         return total
@@ -173,7 +175,7 @@
 
 
 def step_body(
-    ids, hid, gain_in, gain_out, refh, ref_gain, gate, up, down, dw, head, proxy_head,
+    targets, languages, hid, gain_in, gain_out, refh, ref_gain, gate, up, down, dw, head, proxy_head,
     logw, grad_head, g_gate, g_up, g_down,
     normed, pre, fin, fin_x, mid, ref_st, tl, dnw,
     idsg, guw, ref_all, headv, rhs, logit, x, rb, ra, units, give, rp,
@@ -193,9 +195,16 @@
     take_head = pltpu.make_async_copy(head, headv, local.at[0])
     take_head.start()
     take_proxy.start()
-    normed[b, a] = rms_rows(hid[...], gain_in[...]).astype(BF16).reshape(2, 16, 1024)
+    own_hid = pl.ds(pl.multiple_of(me.z * 32, 32), 32)
+    normed[b, a] = rms_rows(hid[own_hid], gain_in[...]).astype(BF16).reshape(2, 16, 1024)
     s2 = Spread(go, me, lambda bb, aa: normed.at[bb, aa])
-    idsg[b, a] = ids[...]
+    both_ids = jnp.concatenate([targets[...], languages[...]] * 4, axis=0)
+    turn = lax.rem(a - me.z + 4, 4)
+    turned = both_ids
+    for n in (1, 2, 3):
+        turned = jnp.where(turn == n, pltpu.roll(both_ids, 32 * n, 1), turned)
+    lane_unit = lax.div(lax.broadcasted_iota(jnp.int32, (8, 128), 1), 32)
+    idsg[b, a] = jnp.where(lane_unit == a, turned, 0)
     s2_ids = Spread(go, me, lambda bb, aa: idsg.at[bb, aa])
     here = pl.ds(pl.multiple_of(f * 128, 128), 128)
 
@@ -231,7 +240,7 @@
     for copy in w_core:
         copy.wait_recv()
     collect = Collect(go, me, rb, ra)
-    for k in (0, 1, 3, 2):
+    for k in (1, 3, 2, 0):
         bb = s2.row(k)
         h = jnp.dot(
             normed[bb].reshape(128, 1024), guw[...].reshape(1024, 256),
@@ -288,10 +297,11 @@
     take_head.wait()
     cross[0].wait_recv()
     ref_rows(0)
-    give[...] = collect.total(x.at[b], units).astype(BF16)
+    collect.turn(x.at[b], units)
+    give[...] = collect.total(units).astype(BF16)
     swap = go.start(give, rp, me.partner())
     swap.wait_recv()
-    middle = hid[...].astype(F32) + (give[...].astype(F32) + rp[...].astype(F32))
+    middle = hid[own_hid].astype(F32) + (give[...].astype(F32) + rp[...].astype(F32))
     mid[...] = middle
     fin[c, b, a] = rms_rows(middle, gain_out[...]).astype(BF16).reshape(2, 16, 1024)
     f2 = Spread(go, me, lambda bb, aa: fin.at[c, bb, aa])
@@ -362,20 +372,20 @@
     slot_yz[yz] = join_all([slot_c[0], slot_c[1]])
     sent = to_plane(go, me, slot_yz.at[yz])
     vf[c, b, a] = fin_x[...]
-    beside = Spread(go, me, lambda bb, aa: vf.at[c, bb, aa])
     for copy in sent.values():
         copy.wait_recv()
     slot_x[0, p] = join_all([slot_yz[j] for j in range(16)])
     spread = [
         go.start(slot_x.at[0, p], slot_x.at[g, p], to) for g, to in zip((0, 1, 1), x_peers)
     ]
-    beside.hand_on()
+    beside = Spread(go, me, lambda bb, aa: vf.at[c, bb, aa])
     for copy in spread:
         copy.wait_recv()
     both[c, 0] = join_all([slot_x[0, 0], slot_x[0, 1]])
     both[c, 1] = join_all([slot_x[1, 0], slot_x[1, 1]])
     share = go.start(both.at[c], both.at[c], me.core())
     share.wait_recv()
+    beside.hand_on()
     excess = [None, None]
     for g in range(2):
         now = [
@@ -395,11 +405,12 @@
         lc[l : l + 1] = jnp.sum(n, axis=0, keepdims=True)
     wide = lambda v: jnp.broadcast_to(jnp.sum(v[...], axis=1, keepdims=True), (LANGS, 128))
     count = jnp.maximum(wide(lc), 1.0)
-    score = jnp.log(dw[...]) + STEP_SIZE * (wide(ls) / count)
+    prior = jnp.broadcast_to(jnp.log(dw[...]), (128, LANGS)).T
+    score = prior + STEP_SIZE * (wide(ls) / count)
     score = jnp.exp(score - jnp.max(score, axis=0, keepdims=True))
     mixture = score / jnp.sum(score, axis=0, keepdims=True)
     new = (1.0 - SMOOTHING) * mixture + SMOOTHING / LANGS
-    logw[...] = jnp.log(new)
+    logw[...] = jnp.log(new).T[0:1]
     per_token = new / count * 2048.0
     weight = jnp.zeros(every.shape, F32)
     for l in range(LANGS):
@@ -448,12 +459,14 @@
         lse_far = line(lambda r: lse[8 + r : 9 + r])
         tw_far = line(lambda r: tw[8 + r : 9 + r])
         d = (tw_far * (jnp.exp(logits - lse_far) - hit)).astype(BF16)
-        grad_head[at] = jnp.dot(d, states, preferred_element_type=F32) + jnp.dot(
-            vd[at], fin[...].reshape(1024, 1024), preferred_element_type=F32
-        )
-
-    pl.loop(0, 4)(head_rows)
-    d_give[...] = collect.total(acc.at[b], d_units).astype(BF16)
+        grad = jnp.dot(d, states, preferred_element_type=F32)
+        grad += jnp.dot(vd[at], fin[...].reshape(1024, 1024), preferred_element_type=F32)
+        grad_head[at] = grad.astype(BF16)
+
+    pl.loop(0, 2)(head_rows)
+    collect.turn(acc.at[b], d_units)
+    pl.loop(2, 4)(head_rows)
+    d_give[...] = collect.total(d_units).astype(BF16)
     swap = go.start(d_give, d_rp, me.partner())
     pl.loop(4, 6)(head_rows)
     swap.wait_recv()
@@ -529,9 +542,9 @@
 
         at = slice(128 * j, 128 * (j + 1))
         got = rg[j].astype(F32)
-        g_gate[:, at] = got[0:128].T
-        g_up[:, at] = got[128:256].T
-        g_down[at] = got[256:384]
+        g_gate[:, at] = got[0:128].T.astype(BF16)
+        g_up[:, at] = got[128:256].T.astype(BF16)
+        g_down[at] = rg[j, 256:384]
     for e, side in ((1, 1), (1, 0), (0, 1)):
         homeward(e, side, me.y).wait_send()
 
@@ -542,7 +555,7 @@
     go.drain()
 
 
-def step(ids, hid, gain_in, gain_out, refh, ref_gain, gate, up, down, domain_weights, head, proxy_head):
+def step(*arrays):
     vmem = pl.BlockSpec(memory_space=pltpu.VMEM)
     hbm = pl.BlockSpec(memory_space=pl.ANY)
     shape = jax.ShapeDtypeStruct
@@ -552,13 +565,13 @@
     return pl.pallas_call(
         step_body,
         out_shape=[
-            shape((LANGS, 128), F32),
-            shape((1024, 1024), F32),
-            shape((128, 512), F32),
-            shape((128, 512), F32),
-            shape((512, 128), F32),
+            shape((1, LANGS), F32),
+            shape((1024, 1024), BF16),
+            shape((128, 512), BF16),
+            shape((128, 512), BF16),
+            shape((512, 128), BF16),
         ],
-        in_specs=[vmem] * 10 + [hbm] * 2,
+        in_specs=[vmem] * 11 + [hbm] * 2,
         out_specs=[vmem] * 5,
         scratch_shapes=[
             half(4, 4, 2, 16, 1024),
@@ -618,10 +631,7 @@
             collective_id=1, has_side_effects=True, vmem_limit_bytes=VMEM_LIMIT * 2**20
         ),
         name="step",
-    )(
-        ids, hid, gain_in, gain_out, refh, ref_gain, gate, up, down,
-        jnp.broadcast_to(domain_weights[:, None], (LANGS, 128)), head, proxy_head,
-    )
+    )(*arrays)
 
 
 def local(
@@ -639,14 +649,10 @@
     proxy_head,
     domain_weights,
 ):
-    me = Place()
-    mine = lambda v: lax.dynamic_slice_in_dim(v, me.z * 32, 32, 0)
-    ids = jnp.tile(jnp.stack([mine(targets), mine(languages)]), (4, 4))
-    lanes = lax.broadcasted_iota(jnp.int32, (8, 128), 1)
-    ids = jnp.where(lax.div(lanes, 32) == me.a, ids, 0)
     log_weights, grad_head, grad_gate, grad_up, grad_down = step(
-        ids,
-        mine(proxy_hidden),
+        targets[None],
+        languages[None],
+        proxy_hidden,
         proxy_gain_in[None],
         proxy_gain_out[None],
         ref_hidden,
@@ -654,11 +660,12 @@
         gate_weight,
         up_weight,
         down_weight,
-        domain_weights,
+        domain_weights[None],
         ref_head,
         proxy_head,
     )
-    return (log_weights[:, 0], grad_gate, grad_up, grad_down, grad_head)
+    grads = [g.astype(F32) for g in (grad_gate, grad_up, grad_down, grad_head)]
+    return (log_weights[0], *grads)
 
 
 def solution(mesh):

time: 155 us -> 148 us (0.955)
  local copies, waits for them, and re-layouts: 14 us -> 0.53 us
  other arithmetic: 0.62 us -> 6.31 us
    unnamed x6 -> x9, local copies, waits for them, and re-layouts: 9.8 us -> 0.53 us
    convert_element_type x0 -> x4, other arithmetic: none -> 6.31 us  [local(): grads = [g.astype(F32) for g in (grad_gate, grad_up, grad_down, grad_head)]]
where the time goes in v7:
time: 148 us; the launch traced here: 146 us
  Pallas kernels  139 us (94%)
  other arithmetic  6.31 us (4%)
    pallas_call x1, Pallas kernels, step(): pl.pallas_call(step_body, out_shape=[shape((1, LANGS), F32), shape((1024,...  139 us
    convert_element_type x4, other arithmetic, local(): grads = [g.astype(F32) for g in (grad_gate, grad_up, grad_down, grad_head)]  6.31 us

profile of v7, /device:TPU:1, one launch (start us, length us, event | category | flops | bytes accessed | tf_op | source)
XLA Modules:
  0.0 146.5 jit_solution(11240152309059932946)
XLA Ops:
  0.6 139.0 %step.1 = (f32[1,64]{1,0:T(1,128)}, bf16[1024,1024]{1,0:T(8,128)(2,1)}, bf16[128,512]{1,0:T(8,128)(2,1)}, bf16[128,512]{1,0:T(8,128)(2,1)}, bf16[512,128]{1,0:T(8,128)(2,1)}) custom-call(s32[1,128]{1,0:T(1,128)} %bitcast.10, s32[1,128]{1,0:T(1,128)} %bitcast.11, bf16[128,1024]{1,0:T(8,128)(2,1)} %hid.1, f32[1,1024]{1,0:T(1,128)} %bitcast.8, ...), custom_call_target="tpu_custom_call" | custom-call | tf_op jit(solution)/shard_map/step/pallas_call | solution.py:565
  139.6 0.0 copy-start.2
  139.6 0.0 copy-start.1
  139.6 0.0 copy-start
  139.6 0.0 copy-start.3
  139.6 4.1 %convert_element_type.15 = f32[1024,1024]{1,0:T(8,128)} convert(bf16[1024,1024]{1,0:T(8,128)(2,1)} %get-tuple-element.14) | non-fusion elementwise | flops 1048576 | bytes 6291456 | tf_op jit(solution)/shard_map/convert_element_type | solution.py:667
  143.8 0.0 copy-done.2
  143.8 0.7 convert_element_type.12
  144.5 0.0 copy-done.1
  144.5 0.7 convert_element_type.13
  145.2 0.0 copy-done
  145.2 0.7 convert_element_type.14
  146.0 0.0 copy-done.3
  146.0 0.5 copy.19
Async XLA Ops:
  139.6 4.2 %copy-start.2 = (bf16[128,512]{1,0:T(8,128)(2,1)S(1)}, bf16[128,512]{1,0:T(8,128)(2,1)}, u32[]{:S(2)}) copy-start(bf16[128,512]{1,0:T(8,128)(2,1)} %get-tuple-element.11) | copy-start | bytes 393220
  139.6 4.9 %copy-start.1 = (bf16[128,512]{1,0:T(8,128)(2,1)S(1)}, bf16[128,512]{1,0:T(8,128)(2,1)}, u32[]{:S(2)}) copy-start(bf16[128,512]{1,0:T(8,128)(2,1)} %get-tuple-element.12) | copy-start | bytes 393220
  139.6 5.6 %copy-start = (bf16[512,128]{1,0:T(8,128)(2,1)S(1)}, bf16[512,128]{1,0:T(8,128)(2,1)}, u32[]{:S(2)}) copy-start(bf16[512,128]{1,0:T(8,128)(2,1)} %get-tuple-element.13) | copy-start | bytes 393220
  139.6 6.3 %copy-start.3 = (f32[1,64]{1,0:T(1,128)S(1)}, f32[1,64]{1,0:T(1,128)}, u32[]{:S(2)}) copy-start(f32[1,64]{1,0:T(1,128)} %get-tuple-element.10) | copy-start | bytes 772

commit v8 on v7

--- a/solution.py
+++ b/solution.py
@@ -273,10 +273,9 @@
     ids_far = go.start(tl.at[0], tl.at[1], me.neighbour())
     vocab = lax.broadcasted_iota(jnp.int32, (1024, 256), 0) + (f * 8 + me.t) * 1024
 
-    def ref_rows(m):
-        b_own, b_far = ring(b, m), ring(a, m)
-        rhs[0:128] = ref_all[c, b_own].reshape(128, 4096)
-        rhs[128:256] = ref_all[1 - c, b_far].reshape(128, 4096)
+    def ref_rows(*pair):
+        for n, at in enumerate(pair):
+            rhs[128 * n : 128 * (n + 1)] = ref_all[at].reshape(128, 4096)
 
         @pl.loop(0, 4)
         def _(n):
@@ -287,16 +286,16 @@
 
         value = logit[...]
         high = jnp.max(value, axis=0, keepdims=True)
-        want = jnp.concatenate([tl[0, 0, 4 * c + b_own], tl[0, 0, 4 * (1 - c) + b_far]], axis=1)
+        want = jnp.concatenate([tl[0, 0, 4 * cc + bb] for cc, bb in pair], axis=1)
         picked = jnp.sum(jnp.where(vocab == want, value, 0.0), axis=0, keepdims=True)
         total = jnp.sum(jnp.exp(value - high), axis=0, keepdims=True)
         for s, got in enumerate((high, total, picked)):
-            ref_st[s, 4 * c + b_own] = got[:, :128]
-            ref_st[s, 4 * (1 - c) + b_far] = got[:, 128:]
+            for n, (cc, bb) in enumerate(pair):
+                ref_st[s, 4 * cc + bb] = got[:, 128 * n : 128 * (n + 1)]
 
     take_head.wait()
     cross[0].wait_recv()
-    ref_rows(0)
+    ref_rows((c, b), (1 - c, a))
     collect.turn(x.at[b], units)
     give[...] = collect.total(units).astype(BF16)
     swap = go.start(give, rp, me.partner())
@@ -306,7 +305,6 @@
     fin[c, b, a] = rms_rows(middle, gain_out[...]).astype(BF16).reshape(2, 16, 1024)
     f2 = Spread(go, me, lambda bb, aa: fin.at[c, bb, aa])
     f_x = go.start(fin.at[c, b, a], fin_x, me.neighbour())
-    f2.hand_on()
     r3[0].wait_recv()
     half = ref_all.at[c, ring(b, 3), pl.ds(0, 2)]
     r4 = [go.start(half, half, right_b)]
@@ -316,14 +314,15 @@
     for m in (3, 1):
         unit = ref_all.at[c, ring(b, m)]
         cross[m] = go.start(unit, unit, me.core())
+    ref_rows((c, ring(b, 3)), (c, ring(b, 1)))
+    f2.hand_on()
     cross[3].wait_recv()
-    ref_rows(3)
+    cross[1].wait_recv()
+    ref_rows((1 - c, ring(a, 3)), (1 - c, ring(a, 1)))
     f3 = []
     for k in (0, 1, 3, 2):
         row = fin.at[c, f2.row(k)]
         f3.append(go.start(row, row, me.core()))
-    for copy in f3 + [f_x, ids_far]:
-        copy.wait_recv()
     take_proxy.wait()
     lanes = (((1,), (1,)), ((), ()))
     rows = (((0,), (0,)), ((), ()))
@@ -333,16 +332,28 @@
     def line(v):
         return jnp.concatenate([v(r) for r in range(8)], axis=1)
 
-    def own_rows(n, high):
-        logits = lax.dot_general(vh[tile(n)], fin[...].reshape(1024, 1024), lanes, preferred_element_type=F32)
-        lg[tile(n)] = logits
-        return jnp.maximum(high, jnp.max(logits, axis=0, keepdims=True))
-
-    high = lax.fori_loop(0, 8, own_rows, jnp.full((1, 1024), -jnp.inf, F32))
+    def half_rows(cc):
+        at = pl.ds(pl.multiple_of(cc * 512, 512), 512)
+
+        def some(n, high):
+            states = fin[cc].reshape(512, 1024)
+            logits = lax.dot_general(vh[tile(n)], states, lanes, preferred_element_type=F32)
+            lg[tile(n), at] = logits
+            return jnp.maximum(high, jnp.max(logits, axis=0, keepdims=True))
+
+        return lax.fori_loop(0, 8, some, jnp.full((1, 512), -jnp.inf, F32))
+
+    high_own = half_rows(c)
     for copy in r4:
         copy.wait_recv()
     unit = ref_all.at[c, ring(b, 2)]
     cross[2] = go.start(unit, unit, me.core())
+    for copy in f3 + [f_x, ids_far]:
+        copy.wait_recv()
+    high_far = half_rows(1 - c)
+    high = jnp.concatenate(
+        [jnp.where(c == 0, high_own, high_far), jnp.where(c == 0, high_far, high_own)], axis=1
+    )
     own_tgt = line(lambda r: tl[0, 0, r])
 
     def own_sums(n, carry):
@@ -355,10 +366,8 @@
 
     zero = jnp.zeros((1, 1024), F32)
     total, picked = lax.fori_loop(0, 8, own_sums, (zero, zero))
-    cross[1].wait_recv()
-    ref_rows(1)
     cross[2].wait_recv()
-    ref_rows(2)
+    ref_rows((c, ring(b, 2)), (1 - c, ring(a, 2)))
     for r in range(8):
         h, q = r // 4, r % 4
         for s in range(3):

time: 148 us -> 150 us (1.014)
  Pallas kernels: 139 us -> 141 us
    pallas_call x1, Pallas kernels: 139 us -> 141 us  [step(): pl.pallas_call(step_body, out_shape=[shape((1, LANGS), F32), shape((1024,...]
where the time goes in v8:
time: 150 us; the launch traced here: 148 us
  Pallas kernels  141 us (94%)
  other arithmetic  6.31 us (4%)
    pallas_call x1, Pallas kernels, step(): pl.pallas_call(step_body, out_shape=[shape((1, LANGS), F32), shape((1024,...  141 us
    convert_element_type x4, other arithmetic, local(): grads = [g.astype(F32) for g in (grad_gate, grad_up, grad_down, grad_head)]  6.31 us

profile of v8, /device:TPU:1, one launch (start us, length us, event | category | flops | bytes accessed | tf_op | source)
XLA Modules:
  0.0 148.2 jit_solution(7763357350765133869)
XLA Ops:
  0.6 140.7 %step.1 = (f32[1,64]{1,0:T(1,128)}, bf16[1024,1024]{1,0:T(8,128)(2,1)}, bf16[128,512]{1,0:T(8,128)(2,1)}, bf16[128,512]{1,0:T(8,128)(2,1)}, bf16[512,128]{1,0:T(8,128)(2,1)}) custom-call(s32[1,128]{1,0:T(1,128)} %bitcast.10, s32[1,128]{1,0:T(1,128)} %bitcast.11, bf16[128,1024]{1,0:T(8,128)(2,1)} %hid.1, f32[1,1024]{1,0:T(1,128)} %bitcast.8, ...), custom_call_target="tpu_custom_call" | custom-call | tf_op jit(solution)/shard_map/step/pallas_call | solution.py:574
  141.3 0.0 copy-start.2
  141.3 0.0 copy-start.1
  141.3 0.0 copy-start
  141.4 0.0 copy-start.3
  141.4 4.1 %convert_element_type.15 = f32[1024,1024]{1,0:T(8,128)} convert(bf16[1024,1024]{1,0:T(8,128)(2,1)} %get-tuple-element.14) | non-fusion elementwise | flops 1048576 | bytes 6291456 | tf_op jit(solution)/shard_map/convert_element_type | solution.py:676
  145.5 0.0 copy-done.2
  145.5 0.7 convert_element_type.12
  146.2 0.0 copy-done.1
  146.2 0.7 convert_element_type.13
  147.0 0.0 copy-done
  147.0 0.7 convert_element_type.14
  147.7 0.0 copy-done.3
  147.7 0.5 copy.19
Async XLA Ops:
  141.3 4.2 %copy-start.2 = (bf16[128,512]{1,0:T(8,128)(2,1)S(1)}, bf16[128,512]{1,0:T(8,128)(2,1)}, u32[]{:S(2)}) copy-start(bf16[128,512]{1,0:T(8,128)(2,1)} %get-tuple-element.11) | copy-start | bytes 393220
  141.3 4.9 %copy-start.1 = (bf16[128,512]{1,0:T(8,128)(2,1)S(1)}, bf16[128,512]{1,0:T(8,128)(2,1)}, u32[]{:S(2)}) copy-start(bf16[128,512]{1,0:T(8,128)(2,1)} %get-tuple-element.12) | copy-start | bytes 393220
  141.3 5.6 %copy-start = (bf16[512,128]{1,0:T(8,128)(2,1)S(1)}, bf16[512,128]{1,0:T(8,128)(2,1)}, u32[]{:S(2)}) copy-start(bf16[512,128]{1,0:T(8,128)(2,1)} %get-tuple-element.13) | copy-start | bytes 393220
  141.4 6.3 %copy-start.3 = (f32[1,64]{1,0:T(1,128)S(1)}, f32[1,64]{1,0:T(1,128)}, u32[]{:S(2)}) copy-start(f32[1,64]{1,0:T(1,128)} %get-tuple-element.10) | copy-start | bytes 772

commit v9 on v8

--- a/solution.py
+++ b/solution.py
@@ -11,7 +11,7 @@
 STEP_SIZE = 1.0
 SMOOTHING = 0.001
 LANGS = 64
-VMEM_LIMIT = 58
+VMEM_LIMIT = 60
 MESH = pl.DeviceIdType.MESH
 F32, BF16 = jnp.float32, jnp.bfloat16
 
@@ -305,6 +305,7 @@
     fin[c, b, a] = rms_rows(middle, gain_out[...]).astype(BF16).reshape(2, 16, 1024)
     f2 = Spread(go, me, lambda bb, aa: fin.at[c, bb, aa])
     f_x = go.start(fin.at[c, b, a], fin_x, me.neighbour())
+    f2.hand_on()
     r3[0].wait_recv()
     half = ref_all.at[c, ring(b, 3), pl.ds(0, 2)]
     r4 = [go.start(half, half, right_b)]
@@ -315,10 +316,6 @@
         unit = ref_all.at[c, ring(b, m)]
         cross[m] = go.start(unit, unit, me.core())
     ref_rows((c, ring(b, 3)), (c, ring(b, 1)))
-    f2.hand_on()
-    cross[3].wait_recv()
-    cross[1].wait_recv()
-    ref_rows((1 - c, ring(a, 3)), (1 - c, ring(a, 1)))
     f3 = []
     for k in (0, 1, 3, 2):
         row = fin.at[c, f2.row(k)]
@@ -366,6 +363,9 @@
 
     zero = jnp.zeros((1, 1024), F32)
     total, picked = lax.fori_loop(0, 8, own_sums, (zero, zero))
+    cross[3].wait_recv()
+    cross[1].wait_recv()
+    ref_rows((1 - c, ring(a, 3)), (1 - c, ring(a, 1)))
     cross[2].wait_recv()
     ref_rows((c, ring(b, 2)), (1 - c, ring(a, 2)))
     for r in range(8):
@@ -643,6 +643,29 @@
     )(*arrays)
 
 
+def results_body(*refs):
+    n = len(refs) // 2
+    for src, dst in zip(refs[:n], refs[n:]):
+        dst[...] = src[...].astype(F32)
+
+
+def results(grads, log_weights):
+    steps = 4
+    block = lambda v: pl.BlockSpec((v.shape[0] // steps, v.shape[1]), lambda i: (i, 0))
+    whole = pl.BlockSpec(log_weights.shape, lambda i: (0, 0))
+    specs = [block(g) for g in grads] + [whole]
+    arrays = [*grads, log_weights]
+    return pl.pallas_call(
+        results_body,
+        grid=(steps,),
+        out_shape=[jax.ShapeDtypeStruct(v.shape, F32) for v in arrays],
+        in_specs=specs,
+        out_specs=specs,
+        compiler_params=pltpu.CompilerParams(vmem_limit_bytes=VMEM_LIMIT * 2**20),
+        name="results",
+    )(*arrays)
+
+
 def local(
     ref_hidden,
     proxy_hidden,
@@ -673,8 +696,10 @@
         ref_head,
         proxy_head,
     )
-    grads = [g.astype(F32) for g in (grad_gate, grad_up, grad_down, grad_head)]
-    return (log_weights[0], *grads)
+    grad_gate, grad_up, grad_down, grad_head, log_weights = results(
+        (grad_gate, grad_up, grad_down, grad_head), log_weights
+    )
+    return (log_weights[0], grad_gate, grad_up, grad_down, grad_head)
 
 
 def solution(mesh):

time: 150 us -> 147 us (0.980)
  other arithmetic: 6.31 us -> 0 us
  Pallas kernels: 141 us -> 145 us
    convert_element_type x4 -> x0, other arithmetic: 6.31 us -> none  [local(): grads = [g.astype(F32) for g in (grad_gate, grad_up, grad_down, grad_head)]]
    pallas_call x0 -> x1, Pallas kernels: none -> 4.5 us  [results(): pl.pallas_call(results_body, grid=(steps,), out_shape=[jax.ShapeDtypeStru...]
where the time goes in v9:
time: 147 us; the launch traced here: 145 us
  Pallas kernels  145 us (99%)
    pallas_call x1, Pallas kernels, step(): pl.pallas_call(step_body, out_shape=[shape((1, LANGS), F32), shape((1024,...  140 us
    pallas_call x1, Pallas kernels, results(): pl.pallas_call(results_body, grid=(steps,), out_shape=[jax.ShapeDtypeStru...  4.5 us

profile of v9, /device:TPU:1, one launch (start us, length us, event | category | flops | bytes accessed | tf_op | source)
XLA Modules:
  0.0 145.2 jit_solution(13636405180667418001)
XLA Ops:
  0.6 140.1 %step.1 = (f32[1,64]{1,0:T(1,128)}, bf16[1024,1024]{1,0:T(8,128)(2,1)}, bf16[128,512]{1,0:T(8,128)(2,1)}, bf16[128,512]{1,0:T(8,128)(2,1)}, bf16[512,128]{1,0:T(8,128)(2,1)}) custom-call(s32[1,128]{1,0:T(1,128)} %bitcast.10, s32[1,128]{1,0:T(1,128)} %bitcast.11, bf16[128,1024]{1,0:T(8,128)(2,1)} %hid.1, f32[1,1024]{1,0:T(1,128)} %bitcast.8, ...), custom_call_target="tpu_custom_call" | custom-call | tf_op jit(solution)/shard_map/step/pallas_call | solution.py:574
  140.7 4.5 %results.1 = (f32[128,512]{1,0:T(8,128)}, f32[128,512]{1,0:T(8,128)}, f32[512,128]{1,0:T(8,128)}, f32[1024,1024]{1,0:T(8,128)}, f32[1,64]{1,0:T(1,128)}) custom-call(bf16[128,512]{1,0:T(8,128)(2,1)} %get-tuple-element.15.refs_0_, bf16[128,512]{1,0:T(8,128)(2,1)} %get-tuple-element.16.refs_1_, bf16[512,128]{1,0:T(8,128)(2,1)} %get-tuple-element.17.refs_2_, ...), custom_call_target="tpu_custom_call" | custom-call | tf_op jit(solution)/shard_map/results/pallas_call | solution.py:658

commit v10 on v7

--- a/solution.py
+++ b/solution.py
@@ -11,7 +11,7 @@
 STEP_SIZE = 1.0
 SMOOTHING = 0.001
 LANGS = 64
-VMEM_LIMIT = 58
+VMEM_LIMIT = 60
 MESH = pl.DeviceIdType.MESH
 F32, BF16 = jnp.float32, jnp.bfloat16
 
@@ -634,6 +634,29 @@
     )(*arrays)
 
 
+def results_body(*refs):
+    n = len(refs) // 2
+    for src, dst in zip(refs[:n], refs[n:]):
+        dst[...] = src[...].astype(F32)
+
+
+def results(grads, log_weights):
+    steps = 4
+    block = lambda v: pl.BlockSpec((v.shape[0] // steps, v.shape[1]), lambda i: (i, 0))
+    whole = pl.BlockSpec(log_weights.shape, lambda i: (0, 0))
+    specs = [block(g) for g in grads] + [whole]
+    arrays = [*grads, log_weights]
+    return pl.pallas_call(
+        results_body,
+        grid=(steps,),
+        out_shape=[jax.ShapeDtypeStruct(v.shape, F32) for v in arrays],
+        in_specs=specs,
+        out_specs=specs,
+        compiler_params=pltpu.CompilerParams(vmem_limit_bytes=VMEM_LIMIT * 2**20),
+        name="results",
+    )(*arrays)
+
+
 def local(
     ref_hidden,
     proxy_hidden,
@@ -664,8 +687,10 @@
         ref_head,
         proxy_head,
     )
-    grads = [g.astype(F32) for g in (grad_gate, grad_up, grad_down, grad_head)]
-    return (log_weights[0], *grads)
+    grad_gate, grad_up, grad_down, grad_head, log_weights = results(
+        (grad_gate, grad_up, grad_down, grad_head), log_weights
+    )
+    return (log_weights[0], grad_gate, grad_up, grad_down, grad_head)
 
 
 def solution(mesh):

time: 148 us -> 146 us (0.986)
  other arithmetic: 6.31 us -> 0 us
  Pallas kernels: 139 us -> 144 us
    convert_element_type x4 -> x0, other arithmetic: 6.31 us -> none  [local(): grads = [g.astype(F32) for g in (grad_gate, grad_up, grad_down, grad_head)]]
    pallas_call x0 -> x1, Pallas kernels: none -> 4.5 us  [results(): pl.pallas_call(results_body, grid=(steps,), out_shape=[jax.ShapeDtypeStru...]
where the time goes in v10:
time: 146 us; the launch traced here: 144 us
  Pallas kernels  144 us (99%)
    pallas_call x1, Pallas kernels, step(): pl.pallas_call(step_body, out_shape=[shape((1, LANGS), F32), shape((1024,...  139 us
    pallas_call x1, Pallas kernels, results(): pl.pallas_call(results_body, grid=(steps,), out_shape=[jax.ShapeDtypeStru...  4.5 us

profile of v10, /device:TPU:1, one launch (start us, length us, event | category | flops | bytes accessed | tf_op | source)
XLA Modules:
  0.0 144.2 jit_solution(14347711311217420144)
XLA Ops:
  0.6 139.0 %step.1 = (f32[1,64]{1,0:T(1,128)}, bf16[1024,1024]{1,0:T(8,128)(2,1)}, bf16[128,512]{1,0:T(8,128)(2,1)}, bf16[128,512]{1,0:T(8,128)(2,1)}, bf16[512,128]{1,0:T(8,128)(2,1)}) custom-call(s32[1,128]{1,0:T(1,128)} %bitcast.10, s32[1,128]{1,0:T(1,128)} %bitcast.11, bf16[128,1024]{1,0:T(8,128)(2,1)} %hid.1, f32[1,1024]{1,0:T(1,128)} %bitcast.8, ...), custom_call_target="tpu_custom_call" | custom-call | tf_op jit(solution)/shard_map/step/pallas_call | solution.py:565
  139.7 4.5 %results.1 = (f32[128,512]{1,0:T(8,128)}, f32[128,512]{1,0:T(8,128)}, f32[512,128]{1,0:T(8,128)}, f32[1024,1024]{1,0:T(8,128)}, f32[1,64]{1,0:T(1,128)}) custom-call(bf16[128,512]{1,0:T(8,128)(2,1)} %get-tuple-element.15.refs_0_, bf16[128,512]{1,0:T(8,128)(2,1)} %get-tuple-element.16.refs_1_, bf16[512,128]{1,0:T(8,128)(2,1)} %get-tuple-element.17.refs_2_, ...), custom_call_target="tpu_custom_call" | custom-call | tf_op jit(solution)/shard_map/results/pallas_call | solution.py:649
